TPU v7x, 32 devices: a whole 2x2x4 slice. The times are simulated.
32 devices in a mesh: sub: 4 (over y, core), row: 2 (over x), col: 4 (over z).
Axes of the slice: x: 2, y: 2, z: 4, core: 2. Of those that a mesh axis runs over, the one named last changes fastest.
Arguments:
- inverse_quarter: bfloat16 [4, 8192, 8192], P('sub', 'row', 'col'), may hold values from -1 to 3
- inverse_half: bfloat16 [4, 8192, 4096], P('sub', 'row', 'col'), may hold values from -1 to 3
- inverse_root: bfloat16 [16384, 16384], P('row', ('sub', 'col')), may hold values from -1 to 3
- quarter_to_half: bfloat16 [4, 2, 4096, 8192], P('sub', None, 'col', 'row'), may hold values from -0.0625 to 0.0625
- quarter_to_root: bfloat16 [4, 2, 4096, 8192], P('sub', None, 'col', 'row'), may hold values from -0.0625 to 0.0625
- half_to_root: bfloat16 [4, 2, 4096, 8192], P('sub', None, 'col', 'row'), may hold values from -0.0625 to 0.0625
- right_quarter: bfloat16 [4, 8192, 256], P('sub', 'col'), may hold values from -6 to 6
- right_half: bfloat16 [4, 4096, 256], P('sub', 'col'), may hold values from -6 to 6
- right_root: bfloat16 [16384, 256], P(('sub', 'col')), may hold values from -6 to 6
- row_blocks: int32 [3, 4, 2, 16], replicated, may hold values 0 or 1
Outputs:
- quarter_solution: float32 [4, 8192, 256], P('sub', 'col', 'row')
- half_solution: bfloat16 [4, 4096, 256], P('sub', 'col')
- root_solution: bfloat16 [16384, 256], P(('sub', 'col'))
All inputs are finite; a program needn't handle non-finite values.
Results may differ from a plain program's by a relative error of at most 0.01.
Values may be sent and summed in bfloat16 or wider, within the bound.
No kernel may reach another device: no remote copies, remote signals or barrier semaphores. Data moves between devices by JAX's collectives and lax.ppermute only.
A program may use at most 256 MiB of HBM per device.

v0:
```python
import jax
import jax.numpy as jnp
from jax import lax
from jax.sharding import PartitionSpec as P

BLK = 256


def from_partner(array, axis, stride):
    return lax.ppermute(array, axis, [(i, i ^ 1 << stride) for i in range(lax.axis_size(axis))])


def sum_rows(values):
    return lax.psum(values, "row")


def sum_columns(values):
    return lax.psum(values, "col")


def partner(values, bit):
    return from_partner(values, "sub", bit)


def partner_solution(values, bit):
    return from_partner(values, "sub", bit)


def project(matrix, vector):
    halves, height, inner = matrix.shape
    flat = jnp.dot(
        matrix.reshape(halves * height, inner), vector, preferred_element_type=jnp.float32
    )
    return flat.reshape(halves, height, vector.shape[1])


def project_back(matrix, pieces):
    inner = matrix.shape[2]
    return lax.dot_general(
        matrix.reshape(-1, inner),
        pieces.reshape(-1, pieces.shape[2]),
        (((0,), (0,)), ((), ())),
        preferred_element_type=jnp.float32,
    )


def transposed(matrix, vector):
    return lax.dot_general(
        matrix, vector, (((0,), (0,)), ((), ())), preferred_element_type=jnp.float32
    )


def pair_reduce(partial_value, bit, own_bit):
    totals = sum_rows(partial_value)
    own_piece = lax.dynamic_index_in_dim(totals, own_bit, 0, keepdims=False)
    other_piece = lax.dynamic_index_in_dim(totals, 1 - own_bit, 0, keepdims=False)
    return own_piece + partner(other_piece, bit)


def order_pair(own_piece, other_piece, own_bit):
    return jnp.where(
        own_bit == 0, jnp.stack([own_piece, other_piece]), jnp.stack([other_piece, own_piece])
    )


def per_device(
    inverse_quarter,
    inverse_half,
    inverse_root,
    quarter_to_half,
    quarter_to_root,
    half_to_root,
    right_quarter,
    right_half,
    right_root,
    row_blocks,
):
    sub_index = lax.axis_index("sub")
    column_index = lax.axis_index("col")
    low_bit = sub_index % 2
    high_bit = sub_index // 2
    piece_rows = quarter_to_half.shape[2]
    block_count = piece_rows // BLK
    row_flags = lax.dynamic_slice(
        row_blocks,
        (jnp.int32(0), sub_index, jnp.int32(0), column_index * block_count),
        (3, 1, 2, block_count),
    )[:, 0]
    masking = jnp.repeat(row_flags, BLK, axis=2).astype(jnp.float32)[:, :, :, None]
    mask_half = masking[0]
    mask_root = masking[1]
    mask_upper = masking[2]
    solved_quarter = sum_columns(
        jnp.dot(inverse_quarter[0], right_quarter[0], preferred_element_type=jnp.float32)
    ).astype(jnp.bfloat16)
    half_part = project(quarter_to_half[0], solved_quarter) * mask_half
    root_part = project(quarter_to_root[0], solved_quarter) * mask_root
    half_terms = pair_reduce(half_part, 0, low_bit)
    root_early = pair_reduce(root_part, 1, high_bit)
    half_right = (right_half[0].astype(jnp.float32) - half_terms).astype(jnp.bfloat16)
    half_sum = sum_columns(jnp.dot(inverse_half[0], half_right, preferred_element_type=jnp.float32))
    solved_half = (half_sum + partner(half_sum, 0)).astype(jnp.bfloat16)
    upper_part = project(half_to_root[0], solved_half) * mask_upper
    root_terms = root_early + pair_reduce(upper_part, 1, high_bit)
    root_right = (right_root.astype(jnp.float32) - root_terms).astype(jnp.bfloat16)
    solved_root = lax.psum(
        jnp.dot(inverse_root, root_right, preferred_element_type=jnp.float32), ("sub", "col")
    ).astype(jnp.bfloat16)
    root_solution = sum_rows(transposed(inverse_root, solved_root)).astype(jnp.bfloat16)
    root_other = partner_solution(root_solution, 1)
    root_pieces = order_pair(root_solution, root_other, high_bit)
    upper_back = project_back(half_to_root[0], root_pieces * mask_upper.astype(jnp.bfloat16))
    quarter_root_back = project_back(
        quarter_to_root[0], root_pieces * mask_root.astype(jnp.bfloat16)
    )
    upper_sum, quarter_root_sum = sum_columns((upper_back, quarter_root_back))
    upper_total = upper_sum + partner(upper_sum, 0)
    half_update = (solved_half.astype(jnp.float32) - upper_total).astype(jnp.bfloat16)
    half_solution = sum_rows(transposed(inverse_half[0], half_update)).astype(jnp.bfloat16)
    half_other = partner_solution(half_solution, 0)
    half_pieces = order_pair(half_solution, half_other, low_bit)
    quarter_half_back = project_back(
        quarter_to_half[0], half_pieces * mask_half.astype(jnp.bfloat16)
    )
    quarter_total = quarter_root_sum + sum_columns(quarter_half_back)
    quarter_update = (solved_quarter.astype(jnp.float32) - quarter_total).astype(jnp.bfloat16)
    quarter_solution = lax.psum_scatter(
        transposed(inverse_quarter[0], quarter_update), "row", scatter_dimension=1, tiled=True
    )
    return (quarter_solution[None], half_solution[None], root_solution)


def solution(mesh):
    placed = (
        P("sub", "row", "col"),
        P("sub", "row", "col"),
        P("row", ("sub", "col")),
        P("sub", None, "col", "row"),
        P("sub", None, "col", "row"),
        P("sub", None, "col", "row"),
        P("sub", "col", None),
        P("sub", "col", None),
        P(("sub", "col"), None),
        P(),
    )
    return jax.shard_map(
        per_device,
        mesh=mesh,
        in_specs=placed,
        out_specs=(P("sub", "col", "row"), P("sub", "col", None), P(("sub", "col"), None)),
        check_vma=False,
    )
```

profile of v0, /device:TPU:0, one launch (start us, length us, event | category | flops | bytes accessed | tf_op | source)
XLA Modules:
  0.0 1504.3 jit_solution(598691174003169941)
XLA Ops:
  8.4 10.1 fusion.2
  18.5 148.8 %all-reduce.20 = bf16[4096,256]{1,0:T(8,128)(2,1)S(1)} all-reduce(f32[4096,256]{1,0:T(8,128)} %fusion.2), channel_id=1, replica_groups=mesh['sub'=4,'row'=2,'col'=4] {'col'}, use_global_device_ids=true, to_apply=%region_0.1 | all-reduce | flops 1048576 | bytes 6291456 | tf_op jit(solution)/shard_map/psum | solution.py:18
  167.3 9.5 convolution_bitcast_fusion.3
  184.7 61.4 %all-reduce.11.cloned.1.call-done = f32[2,1024,256]{1,0,2:T(2,128)} async-done(((f32[2,1024,256]{1,0,2:T(2,128)}), f32[2,1024,256]{1,0,2:T(2,128)}) %all-reduce.11.cloned.1.call-update) | async-done | bytes 2097168 | tf_op jit(solution)/shard_map/psum | solution.py:14
  266.9 154.9 %all-reduce.13.cloned.1.call-done = f32[4096,256]{0,1:T(8,128)} async-done(((f32[4096,256]{0,1:T(8,128)}), f32[4096,256]{0,1:T(8,128)}) %all-reduce.13.cloned.1.call-update) | async-done | bytes 4194320 | tf_op jit(solution)/shard_map/psum | solution.py:18
  421.9 9.6 convolution_bitcast_fusion.4
  442.9 12.3 convolution_bitcast_fusion.2
  463.0 107.1 %all-reduce.19.cloned.1.call-done = (f32[2,1024,256]{1,0,2:T(2,128)}, f32[2,1024,256]{1,0,2:T(2,128)}) async-done(((f32[2,1024,256]{1,0,2:T(2,128)}, f32[2,1024,256]{1,0,2:T(2,128)}), (f32[2,1024,256]{1,0,2:T(2,128)}, f32[2,1024,256]{1,0,2:T(2,128)})) %all-reduce.19.cloned.1.call-update) | async-done | bytes 4194320 | tf_op jit(solution)/shard_map/psum | solution.py:14
  592.4 18.4 %collective-permute-done = f32[1024,256]{1,0:T(8,128)} collective-permute-done((f32[1024,256]{1,0:T(8,128)}, f32[1024,256]{1,0:T(8,128)}, u32[]{:S(2)}, u32[]{:S(2)}) %collective-permute-start) | collective-permute-done | bytes 1048608 | tf_op jit(solution)/shard_map/ppermute | solution.py:10
  610.8 21.3 %collective-permute-done.3 = f32[1024,256]{1,0:T(8,128)} collective-permute-done((f32[1024,256]{1,0:T(8,128)}, f32[1024,256]{1,0:T(8,128)}, u32[]{:S(2)}, u32[]{:S(2)}) %collective-permute-start.3) | collective-permute-done | bytes 1048608 | tf_op jit(solution)/shard_map/ppermute | solution.py:10
  632.1 11.5 convolution_bitcast_fusion
  643.6 350.3 %all-reduce.21 = bf16[8192,256]{0,1:T(8,128)(2,1)} all-reduce(f32[8192,256]{0,1:T(8,128)} %convolution_bitcast_fusion), channel_id=1, replica_groups=mesh['sub'=4,'row'=2,'col'=4] {'sub','col'}, use_global_device_ids=true, to_apply=%region_5.6 | all-reduce | flops 2097152 | bytes 12582912 | tf_op jit(solution)/shard_map/psum | solution.py:106
  993.9 12.5 fusion.17
  1006.4 28.8 %all-reduce.22 = bf16[1024,256]{0,1:T(8,128)(2,1)S(1)} all-reduce(f32[1024,256]{0,1:T(8,128)} %fusion.17), channel_id=1, replica_groups=mesh['sub'=4,'row'=2,'col'=4] {'row'}, use_global_device_ids=true, to_apply=%region_6.7 | all-reduce | flops 262144 | bytes 1572864 | tf_op jit(solution)/shard_map/psum | solution.py:14
  1035.6 11.8 collective-permute-done.4
  1050.5 10.1 convolution_bitcast_fusion.1
  1060.7 157.8 %all-reduce.15.cloned.1.call-done = f32[4096,256]{0,1:T(8,128)} async-done(((f32[4096,256]{0,1:T(8,128)}), f32[4096,256]{0,1:T(8,128)}) %all-reduce.15.cloned.1.call-update) | async-done | bytes 4194320 | tf_op jit(solution)/shard_map/psum | solution.py:18
  1226.0 9.9 fusion.20
  1235.8 30.3 %all-reduce.23 = bf16[1024,256]{0,1:T(8,128)(2,1)S(1)} all-reduce(f32[1024,256]{0,1:T(8,128)} %fusion.20), channel_id=1, replica_groups=mesh['sub'=4,'row'=2,'col'=4] {'row'}, use_global_device_ids=true, to_apply=%region_9.10 | all-reduce | flops 262144 | bytes 1572864 | tf_op jit(solution)/shard_map/psum | solution.py:14
  1266.3 14.8 fusion.35
  1283.7 13.7 fusion.8
  1297.7 153.0 %all-reduce.17.cloned.1.call-done = f32[4096,256]{1,0:T(8,128)} async-done(((f32[4096,256]{1,0:T(8,128)}), f32[4096,256]{1,0:T(8,128)}) %all-reduce.17.cloned.1.call-update) | async-done | bytes 4194320 | tf_op jit(solution)/shard_map/psum | solution.py:18
  1450.7 13.0 fusion.14
  1467.8 26.9 %reduce-scatter.2.cloned.1.call-done = f32[2048,128]{0,1:T(8,128)} async-done(((f32[2048,256]{0,1:T(8,128)}), f32[2048,128]{0,1:T(8,128)}) %reduce-scatter.2.cloned.1.call-update) | async-done | bytes 1048592 | tf_op jit(solution)/shard_map/reduce_scatter | solution.py:127
  (75 shorter events, 92.0 us)
Async XLA Ops:
  7.2 1.2 copy-start
  7.2 238.9 %all-reduce.11.cloned.1.call-start = ((), (), s32[]{:S(2)}) async-start(), calls=%async_computation.1 | async-start | bytes 4194304 | tf_op jit(solution)/shard_map/psum | solution.py:14
  184.1 237.7 %all-reduce.13.cloned.1.call-start = ((), (), s32[]{:S(2)}) async-start(), calls=%async_computation.2 | async-start | bytes 8388608 | tf_op jit(solution)/shard_map/psum | solution.py:18
  255.0 3.0 collective-permute-start.1
  266.6 303.4 %all-reduce.19.cloned.1.call-start = ((), (), s32[]{:S(2)}) async-start(), calls=%async_computation.6 | async-start | bytes 8388608 | tf_op jit(solution)/shard_map/psum | solution.py:14
  421.8 17.1 %collective-permute-start.2 = (f32[4096,256]{0,1:T(8,128)}, f32[4096,256]{0,1:T(8,128)}, u32[]{:S(2)}, u32[]{:S(2)}) collective-permute-start(f32[4096,256]{0,1:T(8,128)} %all-reduce.13.cloned.1.call-done), channel_id=1, source_target_pairs={{0,8},{8,0},{16,24},{24,16},{1,9},{9,1},{17,25},{25,17},{2,10},{10... | collective-permute-start | bytes 12582920 | tf_op jit(solution)/shard_map/ppermute | solution.py:10
  435.4 3.4 copy-start.4
  462.5 756.0 %all-reduce.15.cloned.1.call-start = ((), (), s32[]{:S(2)}) async-start(), calls=%async_computation.3 | async-start | bytes 8388608 | tf_op jit(solution)/shard_map/psum | solution.py:18
  570.1 5.5 copy-start.6
  584.4 26.4 %collective-permute-start = (f32[1024,256]{1,0:T(8,128)}, f32[1024,256]{1,0:T(8,128)}, u32[]{:S(2)}, u32[]{:S(2)}) collective-permute-start(f32[1024,256]{1,0:T(8,128)} %bitcast.6), channel_id=1, source_target_pairs={{0,16},{8,24},{16,0},{24,8},{1,17},{9,25},{17,1},{25,9},{2,18},{10... | collective-permute-start | bytes 3145736 | tf_op jit(solution)/shard_map/ppermute | solution.py:10
  585.9 46.2 %collective-permute-start.3 = (f32[1024,256]{1,0:T(8,128)}, f32[1024,256]{1,0:T(8,128)}, u32[]{:S(2)}, u32[]{:S(2)}) collective-permute-start(f32[1024,256]{1,0:T(8,128)} %bitcast.138), channel_id=1, source_target_pairs={{0,16},{8,24},{16,0},{24,8},{1,17},{9,25},{17,1},{25,9},{2,18},{10... | collective-permute-start | bytes 3145736 | tf_op jit(solution)/shard_map/ppermute | solution.py:10
  1035.2 13.8 copy-start.3
  1035.2 12.1 collective-permute-start.4
  1060.6 157.9 %copy-start.5 = (bf16[2,1024,256]{1,2,0:T(8,128)(2,1)S(1)}, bf16[2,1024,256]{1,2,0:T(8,128)(2,1)}, u32[]{:S(2)}) copy-start(bf16[2,1024,256]{1,2,0:T(8,128)(2,1)} %get-tuple-element.18) | copy-start | bytes 3145732
  1060.7 390.1 %all-reduce.17.cloned.1.call-start = ((), (), s32[]{:S(2)}) async-start(), calls=%async_computation.5 | async-start | bytes 8388608 | tf_op jit(solution)/shard_map/psum | solution.py:18
  1218.5 7.5 collective-permute-start.5
  1266.2 14.9 copy-start.2
  1266.2 14.9 collective-permute-start.6
  1297.5 197.2 %reduce-scatter.2.cloned.1.call-start = ((), (), s32[]{:S(2)}) async-start(), calls=%async_computation.4 | async-start | bytes 3145728 | tf_op jit(solution)/shard_map/reduce_scatter | solution.py:127
  1450.7 46.5 %copy-start.1 = (bf16[1,2048,256]{2,1,0:T(8,128)(2,1)S(1)}, bf16[1,2048,256]{2,1,0:T(8,128)(2,1)}, u32[]{:S(2)}) copy-start(bf16[1,2048,256]{2,1,0:T(8,128)(2,1)} %param.16) | copy-start | bytes 3145732
Sparse Core Ops, SparseCore 0:
  184.2 61.8 all-reduce.10
  266.8 154.9 all-reduce.12
  462.6 107.3 all-reduce.18
  1060.8 157.6 all-reduce.14
  1297.6 153.0 all-reduce.16
  1463.8 30.8 reduce-scatter.1
where the time goes:
time: 1510 us; the launch traced here: 1500 us
  waiting for transfers between devices  720 us (48%)
  blocking collectives  558 us (37%)
  matrix products  135 us (9%)
  local copies, waits for them, and re-layouts  54.8 us (4%)
  other arithmetic  17.5 us (1%)
    psum x3, waiting for transfers between devices, sum_columns(): return lax.psum(values, 'col')  466 us
    psum x1, blocking collectives, per_device(): lax.psum(jnp.dot(inverse_root, root_right, preferred_element_type=jnp.flo...  350 us
    psum x2, waiting for transfers between devices, sum_rows(): return lax.psum(values, 'row')  168 us
    psum x1, blocking collectives, sum_columns(): return lax.psum(values, 'col')  149 us
    psum x2, blocking collectives, sum_rows(): return lax.psum(values, 'row')  59.1 us
    ppermute x7, waiting for transfers between devices, from_partner(): lax.ppermute(array, axis, [(i, i ^ 1 << stride) for i in range(lax.axis_s...  58.6 us
    dot_general x3, matrix products, project_back(): lax.dot_general(matrix.reshape(-1, inner), pieces.reshape(-1, pieces.shap...  38.7 us
    dot_general x3, matrix products, transposed(): lax.dot_general(matrix, vector, (((0,), (0,)), ((), ())), preferred_eleme...  35.3 us
  transfers between devices with their start and end apart: 13, of which 11 were waited for; matrix products, arithmetic and copies ran while one was open for 3% of the time, Pallas kernels for 0%

commit v1 on v0

v1 whole, which is shorter than its diff:
```python
import jax
import jax.numpy as jnp
from jax import lax
from jax.sharding import PartitionSpec as P

BLK = 256
STREAMS = 1
F32 = jnp.float32
BF16 = jnp.bfloat16


def swap(values, axis, distance):
    pairs = [(i, i ^ distance) for i in range(lax.axis_size(axis))]
    return lax.ppermute(values, axis, pairs)


def pick(values, index):
    return lax.dynamic_index_in_dim(values, index, 0, keepdims=False)


def is_power_of_two(count):
    return count & (count - 1) == 0


def scatter_sum(partial, axis):
    count = lax.axis_size(axis)
    own = lax.axis_index(axis)
    pieces = partial.reshape(count, partial.shape[0] // count, partial.shape[1])
    total = pick(pieces, own)
    for distance in range(1, count):
        total = total + swap(pick(pieces, own ^ distance).astype(BF16), axis, distance).astype(F32)
    return total


def gather(piece, axis):
    count = lax.axis_size(axis)
    own = lax.axis_index(axis)
    whole = jnp.zeros((count,) + piece.shape, piece.dtype)
    whole = lax.dynamic_update_index_in_dim(whole, piece, own, 0)
    for distance in range(1, count):
        whole = lax.dynamic_update_index_in_dim(
            whole, swap(piece, axis, distance), own ^ distance, 0
        )
    return whole.reshape((count * piece.shape[0],) + piece.shape[1:])


def pair_scatter(halves, bit_value, axis, distance):
    own_piece = pick(halves, bit_value)
    other_piece = pick(halves, 1 - bit_value)
    return own_piece + swap(other_piece.astype(BF16), axis, distance).astype(F32)


def pair_gather(piece, bit_value, axis, distance):
    other = swap(piece, axis, distance)
    return jnp.where(bit_value == 0, jnp.stack([piece, other]), jnp.stack([other, piece]))


def sum_rows(values):
    if lax.axis_size("row") != 2:
        return lax.psum(values, "row")
    sent = values.astype(BF16)
    return sent.astype(F32) + swap(sent, "row", 1).astype(F32)


def project(matrix, vector):
    halves, height, inner = matrix.shape
    flat = jnp.dot(
        matrix.reshape(halves * height, inner), vector, preferred_element_type=F32
    )
    return flat.reshape(halves, height, vector.shape[1])


def transposed(matrix, vector):
    return lax.dot_general(
        matrix, vector, (((0,), (0,)), ((), ())), preferred_element_type=F32
    )


def project_back(matrix, pieces):
    return transposed(
        matrix.reshape(-1, matrix.shape[2]), pieces.reshape(-1, pieces.shape[2])
    )


def halve(values):
    return values.reshape(2, values.shape[0] // 2, values.shape[1])


def join(values):
    return values.reshape(-1, values.shape[2])


def final_sum(values):
    if lax.axis_size("row") != 2:
        return lax.psum_scatter(values, "row", scatter_dimension=1, tiled=True)
    own = lax.axis_index("row")
    width = values.shape[1] // 2
    mine = lax.dynamic_slice_in_dim(values, own * width, width, 1)
    sent = lax.dynamic_slice_in_dim(values, (1 - own) * width, width, 1)
    return mine + swap(sent.astype(BF16), "row", 1).astype(F32)


def solve(
    inverse_quarter,
    inverse_half,
    inverse_root,
    quarter_to_half,
    quarter_to_root,
    half_to_root,
    right_quarter,
    right_half,
    right_root,
    masking,
):
    sub_index = lax.axis_index("sub")
    low_bit = sub_index % 2
    high_bit = sub_index // 2
    mask_half, mask_root, mask_upper = masking[0], masking[1], masking[2]

    quarter_partial = jnp.dot(inverse_quarter, right_quarter, preferred_element_type=F32)
    quarter_piece = scatter_sum(quarter_partial, "col").astype(BF16)
    solved_quarter = gather(quarter_piece, "col")

    half_part = project(quarter_to_half, solved_quarter) * mask_half
    half_terms = sum_rows(pair_scatter(half_part, low_bit, "sub", 1))
    half_right = (right_half.astype(F32) - half_terms).astype(BF16)
    root_part = project(quarter_to_root, solved_quarter) * mask_root

    half_partial = jnp.dot(inverse_half, half_right, preferred_element_type=F32)
    half_partial = pair_scatter(halve(half_partial), low_bit, "sub", 1)
    half_piece = scatter_sum(half_partial, "col").astype(BF16)
    solved_half = join(pair_gather(gather(half_piece, "col"), low_bit, "sub", 1))

    upper_part = project(half_to_root, solved_half) * mask_upper
    root_terms = sum_rows(pair_scatter(upper_part + root_part, high_bit, "sub", 2))
    root_right = (right_root.astype(F32) - root_terms).astype(BF16)

    root_partial = jnp.dot(inverse_root, root_right, preferred_element_type=F32)
    root_partial = pair_scatter(halve(root_partial), low_bit, "sub", 1)
    root_partial = pair_scatter(halve(root_partial), high_bit, "sub", 2)
    root_piece = scatter_sum(root_partial, "col").astype(BF16)
    solved_root = join(pair_gather(gather(root_piece, "col"), high_bit, "sub", 2))
    solved_root = join(pair_gather(solved_root, low_bit, "sub", 1))

    root_solution = sum_rows(transposed(inverse_root, solved_root)).astype(BF16)
    root_pieces = pair_gather(root_solution, high_bit, "sub", 2)

    upper_back = project_back(half_to_root, root_pieces * mask_upper.astype(BF16))
    upper_back = pair_scatter(halve(upper_back), low_bit, "sub", 1)
    upper_total = scatter_sum(upper_back, "col")
    half_update_piece = (half_piece.astype(F32) - upper_total).astype(BF16)
    half_update = join(pair_gather(gather(half_update_piece, "col"), low_bit, "sub", 1))
    quarter_back = project_back(quarter_to_root, root_pieces * mask_root.astype(BF16))

    half_solution = sum_rows(transposed(inverse_half, half_update)).astype(BF16)
    half_pieces = pair_gather(half_solution, low_bit, "sub", 1)

    quarter_back = quarter_back + project_back(
        quarter_to_half, half_pieces * mask_half.astype(BF16)
    )
    quarter_total = scatter_sum(quarter_back, "col")
    quarter_update_piece = (quarter_piece.astype(F32) - quarter_total).astype(BF16)
    quarter_update = gather(quarter_update_piece, "col")
    return transposed(inverse_quarter, quarter_update), half_solution, root_solution


def per_device(
    inverse_quarter,
    inverse_half,
    inverse_root,
    quarter_to_half,
    quarter_to_root,
    half_to_root,
    right_quarter,
    right_half,
    right_root,
    row_blocks,
):
    sub_index = lax.axis_index("sub")
    column_index = lax.axis_index("col")
    block_count = quarter_to_half.shape[2] // BLK
    row_flags = lax.dynamic_slice(
        row_blocks,
        (jnp.int32(0), sub_index, jnp.int32(0), column_index * block_count),
        (3, 1, 2, block_count),
    )[:, 0]
    masking = jnp.repeat(row_flags, BLK, axis=2).astype(F32)[:, :, :, None]
    width = right_root.shape[1] // STREAMS
    outs = []
    for stream in range(STREAMS):
        columns = slice(stream * width, (stream + 1) * width)
        outs.append(
            solve(
                inverse_quarter[0],
                inverse_half[0],
                inverse_root,
                quarter_to_half[0],
                quarter_to_root[0],
                half_to_root[0],
                right_quarter[0][:, columns],
                right_half[0][:, columns],
                right_root[:, columns],
                masking,
            )
        )
    quarter, half, root = (
        parts[0] if STREAMS == 1 else jnp.concatenate(parts, axis=1) for parts in zip(*outs)
    )
    return (final_sum(quarter)[None], half[None], root)


def solution(mesh):
    placed = (
        P("sub", "row", "col"),
        P("sub", "row", "col"),
        P("row", ("sub", "col")),
        P("sub", None, "col", "row"),
        P("sub", None, "col", "row"),
        P("sub", None, "col", "row"),
        P("sub", "col", None),
        P("sub", "col", None),
        P(("sub", "col"), None),
        P(),
    )
    return jax.shard_map(
        per_device,
        mesh=mesh,
        in_specs=placed,
        out_specs=(P("sub", "col", "row"), P("sub", "col", None), P(("sub", "col"), None)),
        check_vma=False,
    )
```

time: 1510 us -> 786 us (0.52)
  the two profiles are of different devices: /device:TPU:0 before, /device:TPU:12 now
where the time goes in v1:
time: 786 us; the launch traced here: 776 us
  waiting for transfers between devices  445 us (57%)
  local copies, waits for them, and re-layouts  139 us (18%)
  matrix products  119 us (15%)
  starting transfers between devices  46.8 us (6%)
  other arithmetic  24.6 us (3%)
    ppermute x47, waiting for transfers between devices, swap(): return lax.ppermute(values, axis, pairs)  445 us
    dynamic_slice x9, local copies, waits for them, and re-layouts, pick(): return lax.dynamic_index_in_dim(values, index, 0, keepdims=False)  59.6 us
    dot_general x6, matrix products, transposed(): lax.dot_general(matrix, vector, (((0,), (0,)), ((), ())), preferred_eleme...  52.1 us
    ppermute x47, starting transfers between devices, swap(): return lax.ppermute(values, axis, pairs)  46.8 us
    dot_general x3, matrix products, project(): jnp.dot(matrix.reshape(halves * height, inner), vector, preferred_element...  31.3 us
    unnamed x57, local copies, waits for them, and re-layouts  29 us
    reshape x3, local copies, waits for them, and re-layouts, halve(): return values.reshape(2, values.shape[0] // 2, values.shape[1])  25.4 us
    dot_general x1, matrix products, solve(): root_partial = jnp.dot(inverse_root, root_right, preferred_element_type=F32)  19.1 us
  transfers between devices with their start and end apart: 47, of which 41 were waited for; matrix products, arithmetic and copies ran while one was open for 9% of the time, Pallas kernels for 0%

profile of v1, /device:TPU:12, one launch (start us, length us, event | category | flops | bytes accessed | tf_op | source)
XLA Modules:
  0.0 776.0 jit_solution(8693695255014196994)
XLA Ops:
  16.0 18.6 %collective-permute-done = bf16[1024,256]{1,0:T(8,128)(2,1)S(1)} collective-permute-done((bf16[1024,256]{1,0:T(8,128)(2,1)S(1)}, bf16[1024,256]{1,0:T(8,128)(2,1)S(1)}, u32[]{:S(2)}, u32[]{:S(2)}) %collective-permute-start) | collective-permute-done | bytes 524320 | tf_op jit(solution)/shard_map/ppermute | solution.py:14
  34.6 15.8 %collective-permute-done.1 = bf16[1024,256]{1,0:T(8,128)(2,1)S(1)} collective-permute-done((bf16[1024,256]{1,0:T(8,128)(2,1)S(1)}, bf16[1024,256]{1,0:T(8,128)(2,1)S(1)}, u32[]{:S(2)}, u32[]{:S(2)}) %collective-permute-start.1) | collective-permute-done | bytes 524320 | tf_op jit(solution)/shard_map/ppermute | solution.py:14
  68.5 15.5 %collective-permute-done.3 = bf16[1024,256]{1,0:T(8,128)(2,1)S(1)} collective-permute-done((bf16[1024,256]{1,0:T(8,128)(2,1)S(1)}, bf16[1024,256]{1,0:T(8,128)(2,1)S(1)}, u32[]{:S(2)}, u32[]{:S(2)}) %collective-permute-start.3) | collective-permute-done | bytes 524320 | tf_op jit(solution)/shard_map/ppermute | solution.py:14
  84.0 18.8 %collective-permute-done.4 = bf16[1024,256]{1,0:T(8,128)(2,1)} collective-permute-done((bf16[1024,256]{1,0:T(8,128)(2,1)S(1)}, bf16[1024,256]{1,0:T(8,128)(2,1)}, u32[]{:S(2)}, u32[]{:S(2)}) %collective-permute-start.4) | collective-permute-done | bytes 524320 | tf_op jit(solution)/shard_map/ppermute | solution.py:14
  132.9 12.5 %collective-permute-done.7 = bf16[1024,256]{1,0:T(8,128)(2,1)S(1)} collective-permute-done((bf16[1024,256]{1,0:T(8,128)(2,1)S(1)}, bf16[1024,256]{1,0:T(8,128)(2,1)S(1)}, u32[]{:S(2)}, u32[]{:S(2)}) %collective-permute-start.7) | collective-permute-done | bytes 524320 | tf_op jit(solution)/shard_map/ppermute | solution.py:14
  182.5 13.6 %collective-permute-done.10 = bf16[512,256]{1,0:T(8,128)(2,1)S(1)} collective-permute-done((bf16[512,256]{1,0:T(8,128)(2,1)S(1)}, bf16[512,256]{1,0:T(8,128)(2,1)S(1)}, u32[]{:S(2)}, u32[]{:S(2)}) %collective-permute-start.10) | collective-permute-done | bytes 262176 | tf_op jit(solution)/shard_map/ppermute | solution.py:14
  245.3 12.3 %convolution_bitcast_fusion.3 = f32[2048,256]{0,1:T(8,128)} fusion(bf16[4096,256]{1,0:T(8,128)(2,1)} %bitcast.320, bf16[2048,4096]{1,0:T(8,128)(2,1)} %bitcast.282), kind=kOutput, calls=%fused_computation.14 | convolution fusion | flops 4294967296 | bytes 20971520 | tf_op jit(solution)/shard_map/dot_general | solution.py:67
  264.4 13.8 %collective-permute-done.16 = bf16[1024,256]{1,0:T(8,128)(2,1)S(1)} collective-permute-done((bf16[1024,256]{1,0:T(8,128)(2,1)S(1)}, bf16[1024,256]{1,0:T(8,128)(2,1)S(1)}, u32[]{:S(2)}, u32[]{:S(2)}) %collective-permute-start.16) | collective-permute-done | bytes 524320 | tf_op jit(solution)/shard_map/ppermute | solution.py:14
  281.1 12.1 %collective-permute-done.17 = bf16[1024,256]{1,0:T(8,128)(2,1)S(1)} collective-permute-done((bf16[1024,256]{1,0:T(8,128)(2,1)S(1)}, bf16[1024,256]{1,0:T(8,128)(2,1)S(1)}, u32[]{:S(2)}, u32[]{:S(2)}) %collective-permute-start.17) | collective-permute-done | bytes 524320 | tf_op jit(solution)/shard_map/ppermute | solution.py:14
  293.2 19.1 %convolution_bitcast_fusion = f32[8192,256]{0,1:T(8,128)} fusion(bf16[8192,1024]{1,0:T(8,128)(2,1)} %param.12, bf16[1024,256]{1,0:T(8,128)(2,1)S(1)} %collective-permute-done.17, bf16[1024,256]{1,0:T(8,128)(2,1)S(1)} %fusion.25, bf16[1024,256]{1,0:T(8,128)(2,1)S(1)} %copy-done.15), kind=kOutput, calls=%fused_computation.2 | convolution fusion | flops 4296540160 | bytes 26738688 | tf_op jit(solution)/shard_map/dot_general | solution.py:138
  312.2 12.0 %reshape.304 = f32[2,4096,256]{1,0,2:T(2,128)} reshape(f32[8192,256]{0,1:T(8,128)} %convolution_bitcast_fusion) | data formatting | bytes 16777216 | tf_op jit(solution)/shard_map/reshape | solution.py:86
  367.6 25.0 %collective-permute-done.19 = bf16[2048,256]{1,0:T(8,128)(2,1)S(1)} collective-permute-done((bf16[2048,256]{1,0:T(8,128)(2,1)S(1)}, bf16[2048,256]{1,0:T(8,128)(2,1)S(1)}, u32[]{:S(2)}, u32[]{:S(2)}) %collective-permute-start.19) | collective-permute-done | bytes 1048608 | tf_op jit(solution)/shard_map/ppermute | solution.py:14
  428.5 10.6 %collective-permute-done.24 = bf16[512,256]{1,0:T(8,128)(2,1)S(1)} collective-permute-done((bf16[512,256]{1,0:T(8,128)(2,1)S(1)}, bf16[512,256]{1,0:T(8,128)(2,1)S(1)}, u32[]{:S(2)}, u32[]{:S(2)}) %collective-permute-start.24) | collective-permute-done | bytes 262176 | tf_op jit(solution)/shard_map/ppermute | solution.py:14
  444.7 22.4 %collective-permute-done.26 = bf16[2048,256]{1,0:T(8,128)(2,1)S(1)} collective-permute-done((bf16[2048,256]{1,0:T(8,128)(2,1)S(1)}, bf16[2048,256]{1,0:T(8,128)(2,1)S(1)}, u32[]{:S(2)}, u32[]{:S(2)}) %collective-permute-start.26) | collective-permute-done | bytes 1048608 | tf_op jit(solution)/shard_map/ppermute | solution.py:14
  482.3 12.5 %collective-permute-done.28 = bf16[1024,256]{0,1:T(8,128)(2,1)S(1)} collective-permute-done((bf16[1024,256]{0,1:T(8,128)(2,1)S(1)}, bf16[1024,256]{0,1:T(8,128)(2,1)S(1)}, u32[]{:S(2)}, u32[]{:S(2)}) %collective-permute-start.28) | collective-permute-done | bytes 524320 | tf_op jit(solution)/shard_map/ppermute | solution.py:14
  495.6 12.6 %collective-permute-done.29 = bf16[1024,256]{0,1:T(8,128)(2,1)S(1)} collective-permute-done((bf16[1024,256]{0,1:T(8,128)(2,1)S(1)}, bf16[1024,256]{0,1:T(8,128)(2,1)S(1)}, u32[]{:S(2)}, u32[]{:S(2)}) %collective-permute-start.29) | collective-permute-done | bytes 524320 | tf_op jit(solution)/shard_map/ppermute | solution.py:14
  605.7 12.0 %collective-permute-done.38 = bf16[1024,256]{0,1:T(8,128)(2,1)S(1)} collective-permute-done((bf16[1024,256]{0,1:T(8,128)(2,1)S(1)}, bf16[1024,256]{0,1:T(8,128)(2,1)S(1)}, u32[]{:S(2)}, u32[]{:S(2)}) %collective-permute-start.38) | collective-permute-done | bytes 524320 | tf_op jit(solution)/shard_map/ppermute | solution.py:14
  629.0 12.6 %fusion.9 = f32[4096,256]{0,1:T(8,128)} fusion(f32[256,4096]{1,0:T(8,128)} %fusion.68, bf16[2048,256]{1,0:T(8,128)(2,1)S(1)} %bitcast.316, bf16[2048,4096]{1,0:T(8,128)(2,1)} %bitcast.287), kind=kOutput, calls=%fused_computation.10 | convolution fusion | flops 4296015872 | bytes 26214400 | tf_op jit(solution)/shard_map/dot_general | solution.py:74
  652.9 18.1 %collective-permute-done.40 = bf16[1024,256]{1,0:T(8,128)(2,1)S(1)} collective-permute-done((bf16[1024,256]{1,0:T(8,128)(2,1)S(1)}, bf16[1024,256]{1,0:T(8,128)(2,1)S(1)}, u32[]{:S(2)}, u32[]{:S(2)}) %collective-permute-start.40) | collective-permute-done | bytes 524320 | tf_op jit(solution)/shard_map/ppermute | solution.py:14
  671.0 14.6 %collective-permute-done.41 = bf16[1024,256]{1,0:T(8,128)(2,1)S(1)} collective-permute-done((bf16[1024,256]{1,0:T(8,128)(2,1)S(1)}, bf16[1024,256]{1,0:T(8,128)(2,1)S(1)}, u32[]{:S(2)}, u32[]{:S(2)}) %collective-permute-start.41) | collective-permute-done | bytes 524320 | tf_op jit(solution)/shard_map/ppermute | solution.py:14
  685.6 13.0 %collective-permute-done.42 = bf16[1024,256]{1,0:T(8,128)(2,1)S(1)} collective-permute-done((bf16[1024,256]{1,0:T(8,128)(2,1)S(1)}, bf16[1024,256]{1,0:T(8,128)(2,1)S(1)}, u32[]{:S(2)}, u32[]{:S(2)}) %collective-permute-start.42) | collective-permute-done | bytes 524320 | tf_op jit(solution)/shard_map/ppermute | solution.py:14
  703.9 16.8 %collective-permute-done.43 = bf16[1024,256]{1,0:T(8,128)(2,1)} collective-permute-done((bf16[1024,256]{1,0:T(8,128)(2,1)S(1)}, bf16[1024,256]{1,0:T(8,128)(2,1)}, u32[]{:S(2)}, u32[]{:S(2)}) %collective-permute-start.43) | collective-permute-done | bytes 524320 | tf_op jit(solution)/shard_map/ppermute | solution.py:14
  721.7 15.0 %collective-permute-done.44 = bf16[1024,256]{1,0:T(8,128)(2,1)} collective-permute-done((bf16[1024,256]{1,0:T(8,128)(2,1)S(1)}, bf16[1024,256]{1,0:T(8,128)(2,1)}, u32[]{:S(2)}, u32[]{:S(2)}) %collective-permute-start.44) | collective-permute-done | bytes 524320 | tf_op jit(solution)/shard_map/ppermute | solution.py:14
  737.8 10.6 %collective-permute-done.45 = bf16[1024,256]{1,0:T(8,128)(2,1)S(1)} collective-permute-done((bf16[1024,256]{1,0:T(8,128)(2,1)S(1)}, bf16[1024,256]{1,0:T(8,128)(2,1)S(1)}, u32[]{:S(2)}, u32[]{:S(2)}) %collective-permute-start.45) | collective-permute-done | bytes 524320 | tf_op jit(solution)/shard_map/ppermute | solution.py:14
  (215 shorter events, 414.7 us)
Async XLA Ops:
  12.5 22.2 %collective-permute-start = (bf16[1024,256]{1,0:T(8,128)(2,1)S(1)}, bf16[1024,256]{1,0:T(8,128)(2,1)S(1)}, u32[]{:S(2)}, u32[]{:S(2)}) collective-permute-start(bf16[1024,256]{1,0:T(8,128)(2,1)S(1)} %get-tuple-element.22), channel_id=1, source_target_pairs={{0,1},{1,0},{2,3},{3,2},{4,5},{5,4},{6,7},{7,6},{8,9},{9,8},{10,11... | collective-permute-start | bytes 1572872 | tf_op jit(solution)/shard_map/ppermute | solution.py:14
  13.0 37.4 %collective-permute-start.1 = (bf16[1024,256]{1,0:T(8,128)(2,1)S(1)}, bf16[1024,256]{1,0:T(8,128)(2,1)S(1)}, u32[]{:S(2)}, u32[]{:S(2)}) collective-permute-start(bf16[1024,256]{1,0:T(8,128)(2,1)S(1)} %get-tuple-element.24), channel_id=1, source_target_pairs={{0,2},{1,3},{2,0},{3,1},{4,6},{5,7},{6,4},{7,5},{8,10},{9,11},{10,... | collective-permute-start | bytes 1572872 | tf_op jit(solution)/shard_map/ppermute | solution.py:14
  15.6 45.7 %collective-permute-start.2 = (bf16[1024,256]{1,0:T(8,128)(2,1)S(1)}, bf16[1024,256]{1,0:T(8,128)(2,1)}, u32[]{:S(2)}, u32[]{:S(2)}) collective-permute-start(bf16[1024,256]{1,0:T(8,128)(2,1)S(1)} %get-tuple-element.23), channel_id=1, source_target_pairs={{0,3},{1,2},{2,1},{3,0},{4,7},{5,6},{6,5},{7,4},{8,11},{9,10},{10,... | collective-permute-start | bytes 1572872 | tf_op jit(solution)/shard_map/ppermute | solution.py:14
  64.1 19.9 %collective-permute-start.3 = (bf16[1024,256]{1,0:T(8,128)(2,1)S(1)}, bf16[1024,256]{1,0:T(8,128)(2,1)S(1)}, u32[]{:S(2)}, u32[]{:S(2)}) collective-permute-start(bf16[1024,256]{1,0:T(8,128)(2,1)S(1)} %get-tuple-element.18), channel_id=1, source_target_pairs={{0,1},{1,0},{2,3},{3,2},{4,5},{5,4},{6,7},{7,6},{8,9},{9,8},{10,11... | collective-permute-start | bytes 1572872 | tf_op jit(solution)/shard_map/ppermute | solution.py:14
  65.0 37.8 %collective-permute-start.4 = (bf16[1024,256]{1,0:T(8,128)(2,1)S(1)}, bf16[1024,256]{1,0:T(8,128)(2,1)}, u32[]{:S(2)}, u32[]{:S(2)}) collective-permute-start(bf16[1024,256]{1,0:T(8,128)(2,1)S(1)} %get-tuple-element.18), channel_id=1, source_target_pairs={{0,2},{1,3},{2,0},{3,1},{4,6},{5,7},{6,4},{7,5},{8,10},{9,11},{10,... | collective-permute-start | bytes 1572872 | tf_op jit(solution)/shard_map/ppermute | solution.py:14
  67.9 44.5 %collective-permute-start.5 = (bf16[1024,256]{1,0:T(8,128)(2,1)S(1)}, bf16[1024,256]{1,0:T(8,128)(2,1)}, u32[]{:S(2)}, u32[]{:S(2)}) collective-permute-start(bf16[1024,256]{1,0:T(8,128)(2,1)S(1)} %get-tuple-element.18), channel_id=1, source_target_pairs={{0,3},{1,2},{2,1},{3,0},{4,7},{5,6},{6,5},{7,4},{8,11},{9,10},{10,... | collective-permute-start | bytes 1572872 | tf_op jit(solution)/shard_map/ppermute | solution.py:14
  178.1 25.4 %collective-permute-start.11 = (bf16[512,256]{1,0:T(8,128)(2,1)S(1)}, bf16[512,256]{1,0:T(8,128)(2,1)S(1)}, u32[]{:S(2)}, u32[]{:S(2)}) collective-permute-start(bf16[512,256]{1,0:T(8,128)(2,1)S(1)} %get-tuple-element.32), channel_id=1, source_target_pairs={{0,3},{1,2},{2,1},{3,0},{4,7},{5,6},{6,5},{7,4},{8,11},{9,10},{10,... | collective-permute-start | bytes 786440 | tf_op jit(solution)/shard_map/ppermute | solution.py:14
  179.8 23.8 %collective-permute-start.9 = (bf16[512,256]{1,0:T(8,128)(2,1)S(1)}, bf16[512,256]{1,0:T(8,128)(2,1)S(1)}, u32[]{:S(2)}, u32[]{:S(2)}) collective-permute-start(bf16[512,256]{1,0:T(8,128)(2,1)S(1)} %get-tuple-element.31), channel_id=1, source_target_pairs={{0,1},{1,0},{2,3},{3,2},{4,5},{5,4},{6,7},{7,6},{8,9},{9,8},{10,11... | collective-permute-start | bytes 786440 | tf_op jit(solution)/shard_map/ppermute | solution.py:14
  205.9 24.2 %collective-permute-start.14 = (bf16[512,256]{1,0:T(8,128)(2,1)S(1)}, bf16[512,256]{1,0:T(8,128)(2,1)S(1)}, u32[]{:S(2)}, u32[]{:S(2)}) collective-permute-start(bf16[512,256]{1,0:T(8,128)(2,1)S(1)} %get-tuple-element.16), channel_id=1, source_target_pairs={{0,3},{1,2},{2,1},{3,0},{4,7},{5,6},{6,5},{7,4},{8,11},{9,10},{10,... | collective-permute-start | bytes 786440 | tf_op jit(solution)/shard_map/ppermute | solution.py:14
  343.4 20.2 %collective-permute-start.18 = (bf16[4096,256]{1,0:T(8,128)(2,1)S(1)}, bf16[4096,256]{1,0:T(8,128)(2,1)}, u32[]{:S(2)}, u32[]{:S(2)}) collective-permute-start(bf16[4096,256]{1,0:T(8,128)(2,1)S(1)} %bitcast.317), channel_id=1, source_target_pairs={{0,8},{8,0},{16,24},{24,16},{1,9},{9,1},{17,25},{25,17},{2,10},{10... | collective-permute-start | bytes 6291464 | tf_op jit(solution)/shard_map/ppermute | solution.py:14
  367.0 25.6 %collective-permute-start.19 = (bf16[2048,256]{1,0:T(8,128)(2,1)S(1)}, bf16[2048,256]{1,0:T(8,128)(2,1)S(1)}, u32[]{:S(2)}, u32[]{:S(2)}) collective-permute-start(bf16[2048,256]{1,0:T(8,128)(2,1)S(1)} %fusion.17), channel_id=1, source_target_pairs={{0,16},{8,24},{16,0},{24,8},{1,17},{9,25},{17,1},{25,9},{2,18},{10... | collective-permute-start | bytes 3145736 | tf_op jit(solution)/shard_map/ppermute | solution.py:14
  393.0 19.9 %collective-permute-start.21 = (bf16[512,256]{1,0:T(8,128)(2,1)S(1)}, bf16[512,256]{1,0:T(8,128)(2,1)S(1)}, u32[]{:S(2)}, u32[]{:S(2)}) collective-permute-start(bf16[512,256]{1,0:T(8,128)(2,1)S(1)} %get-tuple-element.30), channel_id=1, source_target_pairs={{0,2},{1,3},{2,0},{3,1},{4,6},{5,7},{6,4},{7,5},{8,10},{9,11},{10,... | collective-permute-start | bytes 786440 | tf_op jit(solution)/shard_map/ppermute | solution.py:14
  394.9 24.1 %collective-permute-start.22 = (bf16[512,256]{1,0:T(8,128)(2,1)S(1)}, bf16[512,256]{1,0:T(8,128)(2,1)S(1)}, u32[]{:S(2)}, u32[]{:S(2)}) collective-permute-start(bf16[512,256]{1,0:T(8,128)(2,1)S(1)} %get-tuple-element.29), channel_id=1, source_target_pairs={{0,3},{1,2},{2,1},{3,0},{4,7},{5,6},{6,5},{7,4},{8,11},{9,10},{10,... | collective-permute-start | bytes 786440 | tf_op jit(solution)/shard_map/ppermute | solution.py:14
  419.3 19.9 %collective-permute-start.24 = (bf16[512,256]{1,0:T(8,128)(2,1)S(1)}, bf16[512,256]{1,0:T(8,128)(2,1)S(1)}, u32[]{:S(2)}, u32[]{:S(2)}) collective-permute-start(bf16[512,256]{1,0:T(8,128)(2,1)S(1)} %get-tuple-element.14), channel_id=1, source_target_pairs={{0,2},{1,3},{2,0},{3,1},{4,6},{5,7},{6,4},{7,5},{8,10},{9,11},{10,... | collective-permute-start | bytes 786440 | tf_op jit(solution)/shard_map/ppermute | solution.py:14
  421.2 22.9 %collective-permute-start.25 = (bf16[512,256]{1,0:T(8,128)(2,1)S(1)}, bf16[512,256]{1,0:T(8,128)(2,1)S(1)}, u32[]{:S(2)}, u32[]{:S(2)}) collective-permute-start(bf16[512,256]{1,0:T(8,128)(2,1)S(1)} %get-tuple-element.14), channel_id=1, source_target_pairs={{0,3},{1,2},{2,1},{3,0},{4,7},{5,6},{6,5},{7,4},{8,11},{9,10},{10,... | collective-permute-start | bytes 786440 | tf_op jit(solution)/shard_map/ppermute | solution.py:14
  444.1 23.0 %collective-permute-start.26 = (bf16[2048,256]{1,0:T(8,128)(2,1)S(1)}, bf16[2048,256]{1,0:T(8,128)(2,1)S(1)}, u32[]{:S(2)}, u32[]{:S(2)}) collective-permute-start(bf16[2048,256]{1,0:T(8,128)(2,1)S(1)} %bitcast.314), channel_id=1, source_target_pairs={{0,16},{8,24},{16,0},{24,8},{1,17},{9,25},{17,1},{25,9},{2,18},{10... | collective-permute-start | bytes 3145736 | tf_op jit(solution)/shard_map/ppermute | solution.py:14
  546.9 25.3 %collective-permute-start.33 = (bf16[512,256]{1,0:T(8,128)(2,1)S(1)}, bf16[512,256]{1,0:T(8,128)(2,1)S(1)}, u32[]{:S(2)}, u32[]{:S(2)}) collective-permute-start(bf16[512,256]{1,0:T(8,128)(2,1)S(1)} %get-tuple-element.26), channel_id=1, source_target_pairs={{0,3},{1,2},{2,1},{3,0},{4,7},{5,6},{6,5},{7,4},{8,11},{9,10},{10,... | collective-permute-start | bytes 786440 | tf_op jit(solution)/shard_map/ppermute | solution.py:14
  574.0 24.2 %collective-permute-start.36 = (bf16[512,256]{1,0:T(8,128)(2,1)S(1)}, bf16[512,256]{1,0:T(8,128)(2,1)S(1)}, u32[]{:S(2)}, u32[]{:S(2)}) collective-permute-start(bf16[512,256]{1,0:T(8,128)(2,1)S(1)} %get-tuple-element.12), channel_id=1, source_target_pairs={{0,3},{1,2},{2,1},{3,0},{4,7},{5,6},{6,5},{7,4},{8,11},{9,10},{10,... | collective-permute-start | bytes 786440 | tf_op jit(solution)/shard_map/ppermute | solution.py:14
  649.3 21.6 %collective-permute-start.40 = (bf16[1024,256]{1,0:T(8,128)(2,1)S(1)}, bf16[1024,256]{1,0:T(8,128)(2,1)S(1)}, u32[]{:S(2)}, u32[]{:S(2)}) collective-permute-start(bf16[1024,256]{1,0:T(8,128)(2,1)S(1)} %get-tuple-element.19), channel_id=1, source_target_pairs={{0,1},{1,0},{2,3},{3,2},{4,5},{5,4},{6,7},{7,6},{8,9},{9,8},{10,11... | collective-permute-start | bytes 1572872 | tf_op jit(solution)/shard_map/ppermute | solution.py:14
  649.4 36.1 %collective-permute-start.41 = (bf16[1024,256]{1,0:T(8,128)(2,1)S(1)}, bf16[1024,256]{1,0:T(8,128)(2,1)S(1)}, u32[]{:S(2)}, u32[]{:S(2)}) collective-permute-start(bf16[1024,256]{1,0:T(8,128)(2,1)S(1)} %get-tuple-element.21), channel_id=1, source_target_pairs={{0,2},{1,3},{2,0},{3,1},{4,6},{5,7},{6,4},{7,5},{8,10},{9,11},{10,... | collective-permute-start | bytes 1572872 | tf_op jit(solution)/shard_map/ppermute | solution.py:14
  650.9 47.7 %collective-permute-start.42 = (bf16[1024,256]{1,0:T(8,128)(2,1)S(1)}, bf16[1024,256]{1,0:T(8,128)(2,1)S(1)}, u32[]{:S(2)}, u32[]{:S(2)}) collective-permute-start(bf16[1024,256]{1,0:T(8,128)(2,1)S(1)} %get-tuple-element.20), channel_id=1, source_target_pairs={{0,3},{1,2},{2,1},{3,0},{4,7},{5,6},{6,5},{7,4},{8,11},{9,10},{10,... | collective-permute-start | bytes 1572872 | tf_op jit(solution)/shard_map/ppermute | solution.py:14
  700.3 20.3 %collective-permute-start.43 = (bf16[1024,256]{1,0:T(8,128)(2,1)S(1)}, bf16[1024,256]{1,0:T(8,128)(2,1)}, u32[]{:S(2)}, u32[]{:S(2)}) collective-permute-start(bf16[1024,256]{1,0:T(8,128)(2,1)S(1)} %get-tuple-element.10), channel_id=1, source_target_pairs={{0,1},{1,0},{2,3},{3,2},{4,5},{5,4},{6,7},{7,6},{8,9},{9,8},{10,11... | collective-permute-start | bytes 1572872 | tf_op jit(solution)/shard_map/ppermute | solution.py:14
  700.4 36.3 %collective-permute-start.44 = (bf16[1024,256]{1,0:T(8,128)(2,1)S(1)}, bf16[1024,256]{1,0:T(8,128)(2,1)}, u32[]{:S(2)}, u32[]{:S(2)}) collective-permute-start(bf16[1024,256]{1,0:T(8,128)(2,1)S(1)} %get-tuple-element.10), channel_id=1, source_target_pairs={{0,2},{1,3},{2,0},{3,1},{4,6},{5,7},{6,4},{7,5},{8,10},{9,11},{10,... | collective-permute-start | bytes 1572872 | tf_op jit(solution)/shard_map/ppermute | solution.py:14
  701.8 46.5 %collective-permute-start.45 = (bf16[1024,256]{1,0:T(8,128)(2,1)S(1)}, bf16[1024,256]{1,0:T(8,128)(2,1)S(1)}, u32[]{:S(2)}, u32[]{:S(2)}) collective-permute-start(bf16[1024,256]{1,0:T(8,128)(2,1)S(1)} %get-tuple-element.10), channel_id=1, source_target_pairs={{0,3},{1,2},{2,1},{3,0},{4,7},{5,6},{6,5},{7,4},{8,11},{9,10},{10,... | collective-permute-start | bytes 1572872 | tf_op jit(solution)/shard_map/ppermute | solution.py:14
  (46 other events, 664.3 us)

commit v2 on v1

--- a/solution.py
+++ b/solution.py
@@ -1,10 +1,12 @@
 import jax
 import jax.numpy as jnp
 from jax import lax
+from jax.experimental import pallas as pl
+from jax.experimental.pallas import tpu as pltpu
 from jax.sharding import PartitionSpec as P
 
 BLK = 256
-STREAMS = 1
+BLOCK_BYTES = 1 << 21
 F32 = jnp.float32
 BF16 = jnp.bfloat16
 
@@ -12,6 +14,372 @@
 def swap(values, axis, distance):
     pairs = [(i, i ^ distance) for i in range(lax.axis_size(axis))]
     return lax.ppermute(values, axis, pairs)
+
+
+def swap_core(values):
+    return swap(values, "sub", 1)
+
+
+def swap_y(values):
+    return swap(values, "sub", 2)
+
+
+def swap_z(values, distance):
+    return swap(values, "col", distance)
+
+
+def swap_x(values):
+    return swap(values, "row", 1)
+
+
+def multiply(matrix, vectors, in_blocks, order, outs, flags=None, addend=None):
+    rows, inner = matrix.shape
+    width = vectors[0].shape[1]
+    tile = rows // order.shape[0]
+    steps = order.shape[0]
+    in_size = inner // in_blocks.shape[0]
+    starts = [0]
+    for out_rows, _ in outs:
+        starts.append(starts[-1] + out_rows // tile)
+    count = len(vectors)
+    gathered = count > 1
+
+    def body(places, visit, shown, *refs):
+        vector_refs = refs[:count]
+        matrix_ref = refs[count]
+        addend_ref = refs[count + 1] if addend is not None else None
+        out_refs = refs[count + 1 + (addend is not None) :][: len(outs)]
+        step = pl.program_id(0)
+        if gathered:
+            x_ref = refs[-1]
+
+            @pl.when(step == 0)
+            def _():
+                at = 0
+                for ref in vector_refs:
+                    for part in range(ref.shape[0] // in_size):
+                        place = pl.multiple_of(places[at] * in_size, in_size)
+                        x_ref[pl.ds(place, in_size), :] = ref[part * in_size : (part + 1) * in_size, :]
+                        at += 1
+
+        else:
+            x_ref = vector_refs[0]
+        total = jnp.dot(matrix_ref[...], x_ref[...], preferred_element_type=F32)
+        if flags is not None:
+            total = total * shown[visit[step]].astype(F32)
+        if addend is not None:
+            total = total + addend_ref[...]
+        for index, ref in enumerate(out_refs):
+
+            @pl.when((step >= starts[index]) & (step < starts[index + 1]))
+            def _():
+                ref[...] = total.astype(ref.dtype)
+
+    def out_map(first, last):
+        return lambda i, *_: (jnp.clip(i - first, 0, last - first - 1), 0)
+
+    in_specs = [pl.BlockSpec(v.shape, lambda i, *_: (0, 0)) for v in vectors]
+    in_specs.append(pl.BlockSpec((tile, inner), lambda i, places, visit, shown: (visit[i], 0)))
+    operands = list(vectors) + [matrix]
+    if addend is not None:
+        in_specs.append(pl.BlockSpec((tile, width), lambda i, *_: (i, 0)))
+        operands.append(addend)
+    if flags is None:
+        flags_operand = jnp.zeros((1,), jnp.int32)
+    else:
+        flags_operand = flags
+    return pl.pallas_call(
+        body,
+        grid_spec=pltpu.PrefetchScalarGridSpec(
+            num_scalar_prefetch=3,
+            grid=(steps,),
+            in_specs=in_specs,
+            out_specs=[
+                pl.BlockSpec((tile, width), out_map(starts[i], starts[i + 1]))
+                for i in range(len(outs))
+            ],
+            scratch_shapes=[pltpu.VMEM((inner, width), BF16)] if gathered else [],
+        ),
+        out_shape=[jax.ShapeDtypeStruct((r, width), t) for r, t in outs],
+        compiler_params=pltpu.CompilerParams(vmem_limit_bytes=40 << 20),
+        cost_estimate=pl.CostEstimate(
+            flops=2 * rows * inner * width,
+            transcendentals=0,
+            bytes_accessed=2 * rows * inner + 4 * (rows + inner) * width,
+        ),
+    )(in_blocks, order, flags_operand, *operands)
+
+
+def multiply_back(matrix, vectors, in_blocks, order, outs, flags=None, addend=None, side=None):
+    inner, columns = matrix.shape
+    width = vectors[0].shape[0]
+    steps = order.shape[0]
+    tile = columns // steps
+    in_size = inner // in_blocks.shape[0]
+    mask_size = min(BLK, in_size)
+    starts = [0]
+    for out_columns, _ in outs:
+        starts.append(starts[-1] + out_columns // tile)
+    count = len(vectors)
+
+    def body(places, visit, shown, *refs):
+        vector_refs = refs[:count]
+        matrix_ref = refs[count]
+        addend_ref = refs[count + 1] if addend is not None else None
+        y_ref = refs[-1]
+        out_refs = refs[count + 1 + (addend is not None) : -1]
+        step = pl.program_id(0)
+
+        @pl.when(step == 0)
+        def _():
+            at = 0
+            for ref in vector_refs:
+                for part in range(ref.shape[1] // in_size):
+                    if flags is None:
+                        place = pl.multiple_of(places[at] * in_size, in_size)
+                        y_ref[:, pl.ds(place, in_size)] = ref[:, part * in_size : (part + 1) * in_size]
+                    else:
+                        for inside in range(in_size // mask_size):
+                            block = places[at] * (in_size // mask_size) + inside
+                            place = pl.multiple_of(block * mask_size, mask_size)
+                            start = part * in_size + inside * mask_size
+                            held = ref[:, start : start + mask_size]
+                            y_ref[:, pl.ds(place, mask_size)] = jnp.where(
+                                shown[block] != 0, held, jnp.zeros_like(held)
+                            )
+                    at += 1
+
+        total = jnp.dot(y_ref[...], matrix_ref[...], preferred_element_type=F32)
+        if addend is not None:
+            total = total + addend_ref[...]
+        if side is not None:
+            half = width // 2
+            first = shown[0] == 0
+            low, high = total[:half], total[half:]
+            out_refs[0][...] = jnp.where(first, low, high).T
+            out_refs[1][...] = jnp.where(first, high, low).T.astype(BF16)
+            return
+        for index, ref in enumerate(out_refs):
+
+            @pl.when((step >= starts[index]) & (step < starts[index + 1]))
+            def _():
+                ref[...] = total.astype(ref.dtype)
+
+    def out_map(first, last):
+        return lambda i, *_: (0, jnp.clip(i - first, 0, last - first - 1))
+
+    in_specs = [pl.BlockSpec(v.shape, lambda i, *_: (0, 0)) for v in vectors]
+    in_specs.append(pl.BlockSpec((inner, tile), lambda i, places, visit, shown: (0, visit[i])))
+    operands = list(vectors) + [matrix]
+    if addend is not None:
+        in_specs.append(pl.BlockSpec((width, tile), lambda i, *_: (0, i)))
+        operands.append(addend)
+    if side is not None:
+        scalars = side[None]
+        out_specs = [pl.BlockSpec((tile, width // 2), lambda i, *_: (i, 0))] * 2
+        out_shape = [jax.ShapeDtypeStruct((columns, width // 2), t) for t in (F32, BF16)]
+    else:
+        scalars = jnp.zeros((1,), jnp.int32) if flags is None else flags
+        out_specs = [
+            pl.BlockSpec((width, tile), out_map(starts[i], starts[i + 1])) for i in range(len(outs))
+        ]
+        out_shape = [jax.ShapeDtypeStruct((width, c), t) for c, t in outs]
+    return pl.pallas_call(
+        body,
+        grid_spec=pltpu.PrefetchScalarGridSpec(
+            num_scalar_prefetch=3,
+            grid=(steps,),
+            in_specs=in_specs,
+            out_specs=out_specs,
+            scratch_shapes=[pltpu.VMEM((width, inner), BF16)],
+        ),
+        out_shape=out_shape,
+        compiler_params=pltpu.CompilerParams(vmem_limit_bytes=40 << 20),
+        cost_estimate=pl.CostEstimate(
+            flops=2 * columns * inner * width,
+            transcendentals=0,
+            bytes_accessed=2 * columns * inner + 4 * (columns + inner) * width,
+        ),
+    )(in_blocks, order, scalars, *operands)
+
+
+def listed(*values):
+    return jnp.stack([jnp.asarray(v, jnp.int32) for v in values])
+
+
+def spread(blocks, size, tile):
+    parts = size // tile
+    return (blocks[:, None] * parts + jnp.arange(parts, dtype=jnp.int32)[None]).reshape(-1)
+
+
+def tile_of(piece, inner):
+    return min(piece, max(128, BLOCK_BYTES // (2 * inner)))
+
+
+def add_all(own, *others):
+    total = own
+    for other in others:
+        total = total + other.astype(F32)
+    return total
+
+
+def both_rows(values):
+    return values.astype(F32) + swap_x(values).astype(F32)
+
+
+def solve(
+    inverse_quarter,
+    inverse_half,
+    inverse_root,
+    quarter_to_half,
+    quarter_to_root,
+    half_to_root,
+    right_quarter,
+    right_half,
+    right_root,
+    row_flags,
+):
+    sub_index = lax.axis_index("sub")
+    column = lax.axis_index("col")
+    low = sub_index % 2
+    high = sub_index // 2
+    zs = range(4)
+    mask_half, mask_root, mask_upper = row_flags[0], row_flags[1], row_flags[2]
+    near = [1, 2, 3, 0]
+    panel_rows, panel_columns = quarter_to_half.shape
+    piece_rows = panel_rows // 2
+
+    col_blocks = listed(*[column ^ d for d in zs])
+    col_visit = listed(*[column ^ d for d in near])
+    low_visit = listed(low ^ 1, low)
+    high_visit = listed(high ^ 1, high)
+    low_blocks = listed(low, low ^ 1)
+    high_blocks = listed(high, high ^ 1)
+    half_blocks = listed(*[(low ^ a) * 4 + (column ^ d) for a in (0, 1) for d in zs])
+    half_visit = listed(*[(low ^ a) * 4 + (column ^ d) for a in (1, 0) for d in zs])
+    root_visit = listed(
+        *[((low ^ a) * 2 + (high ^ b)) * 4 + (column ^ d) for a in (1, 0) for b in (0, 1) for d in zs]
+    )
+    root_blocks = listed(
+        *[((low ^ a) * 2 + (high ^ b)) * 4 + (column ^ d) for a in (0, 1) for b in (0, 1) for d in zs]
+    )
+    one = jnp.zeros((1,), jnp.int32)
+
+    rows, inner = inverse_quarter.shape
+    piece = rows // 4
+    tile = tile_of(piece, inner)
+    *sends, own = multiply(
+        inverse_quarter, [right_quarter], one, spread(col_visit, piece, tile),
+        [(piece, BF16)] * 3 + [(piece, F32)],
+    )
+    quarter_piece = add_all(own, *[swap_z(s, d) for s, d in zip(sends, (1, 2, 3))]).astype(BF16)
+    quarter_parts = [quarter_piece] + [swap_z(quarter_piece, d) for d in (1, 2, 3)]
+
+    send, own = multiply(
+        quarter_to_half, quarter_parts, col_blocks, spread(low_visit, piece_rows, BLK),
+        [(piece_rows, BF16), (piece_rows, F32)], flags=mask_half,
+    )
+    half_terms = both_rows(add_all(own, swap_core(send)).astype(BF16))
+    half_right = (right_half.astype(F32) - half_terms).astype(BF16)
+    (root_part,) = multiply(
+        quarter_to_root, quarter_parts, col_blocks, spread(high_visit, piece_rows, BLK),
+        [(panel_rows, F32)], flags=mask_root,
+    )
+
+    rows, inner = inverse_half.shape
+    piece = rows // 8
+    tile = tile_of(piece, inner)
+    send, own = multiply(
+        inverse_half, [half_right], one, spread(half_visit, piece, tile),
+        [(rows // 2, BF16), (rows // 2, F32)],
+    )
+    total = add_all(own, swap_core(send))
+    sends = [total[d * piece : (d + 1) * piece].astype(BF16) for d in zs]
+    half_piece = add_all(total[:piece], *[swap_z(sends[d], d) for d in (1, 2, 3)]).astype(BF16)
+    half_parts = [half_piece] + [swap_z(half_piece, d) for d in (1, 2, 3)]
+    half_parts = half_parts + [swap_core(p) for p in half_parts]
+
+    send, own = multiply(
+        half_to_root, half_parts, half_blocks, spread(high_visit, piece_rows, BLK),
+        [(piece_rows, BF16), (piece_rows, F32)], flags=mask_upper, addend=root_part,
+    )
+    root_terms = both_rows(add_all(own, swap_y(send)).astype(BF16))
+    root_right = (right_root.astype(F32) - root_terms).astype(BF16)
+
+    rows, inner = inverse_root.shape
+    piece = rows // 16
+    tile = tile_of(piece, inner)
+    send, own = multiply(
+        inverse_root, [root_right], one, spread(root_visit, piece, tile),
+        [(rows // 2, BF16), (rows // 2, F32)],
+    )
+    total = add_all(own, swap_core(send))
+    quarter_rows = rows // 4
+    totals = []
+    for d in zs:
+        kept = total[d * piece : (d + 1) * piece]
+        sent = total[quarter_rows + d * piece : quarter_rows + (d + 1) * piece]
+        totals.append(add_all(kept, swap_y(sent.astype(BF16))))
+    root_piece = add_all(
+        totals[0], *[swap_z(totals[d].astype(BF16), d) for d in (1, 2, 3)]
+    ).astype(BF16)
+
+    root_piece = root_piece.T
+    root_parts = [root_piece] + [swap_z(root_piece, d) for d in (1, 2, 3)]
+    root_parts = root_parts + [swap_y(p) for p in root_parts]
+    root_parts = root_parts + [swap_core(p) for p in root_parts]
+    inner, columns = inverse_root.shape
+    tile = tile_of(columns, inner)
+    (partial,) = multiply_back(
+        inverse_root, root_parts, root_blocks, jnp.arange(columns // tile, dtype=jnp.int32),
+        [(columns, BF16)],
+    )
+    root_solution = both_rows(partial).astype(BF16)
+    root_pieces = [root_solution, swap_y(root_solution)]
+
+    piece = panel_columns // 8
+    tile = tile_of(piece, panel_rows)
+    send, own = multiply_back(
+        half_to_root, root_pieces, high_blocks, spread(half_visit, piece, tile),
+        [(panel_columns // 2, BF16), (panel_columns // 2, F32)], flags=mask_upper,
+    )
+    total = add_all(own, swap_core(send))
+    sends = [total[:, d * piece : (d + 1) * piece].astype(BF16) for d in zs]
+    upper_total = add_all(total[:, :piece], *[swap_z(sends[d], d) for d in (1, 2, 3)])
+    update = (half_piece.T.astype(F32) - upper_total).astype(BF16)
+    update_parts = [update] + [swap_z(update, d) for d in (1, 2, 3)]
+    update_parts = update_parts + [swap_core(p) for p in update_parts]
+    piece = panel_columns // 4
+    tile = tile_of(piece, panel_rows)
+    (quarter_back,) = multiply_back(
+        quarter_to_root, root_pieces, high_blocks, spread(col_visit, piece, tile),
+        [(panel_columns, F32)], flags=mask_root,
+    )
+
+    inner, columns = inverse_half.shape
+    tile = tile_of(columns, inner)
+    (partial,) = multiply_back(
+        inverse_half, update_parts, half_blocks, jnp.arange(columns // tile, dtype=jnp.int32),
+        [(columns, BF16)],
+    )
+    half_solution = both_rows(partial).astype(BF16)
+    half_pieces = [half_solution, swap_core(half_solution)]
+
+    tile = tile_of(piece, panel_rows)
+    *sends, own = multiply_back(
+        quarter_to_half, half_pieces, low_blocks, spread(col_visit, piece, tile),
+        [(piece, BF16)] * 3 + [(piece, F32)], flags=mask_half, addend=quarter_back,
+    )
+    quarter_total = add_all(own, *[swap_z(s, d) for s, d in zip(sends, (1, 2, 3))])
+    update = (quarter_piece.T.astype(F32) - quarter_total).astype(BF16)
+    update_parts = [update] + [swap_z(update, d) for d in (1, 2, 3)]
+    inner, columns = inverse_quarter.shape
+    tile = tile_of(columns, inner)
+    own, send = multiply_back(
+        inverse_quarter, update_parts, col_blocks, jnp.arange(columns // tile, dtype=jnp.int32),
+        [], side=lax.axis_index("row"),
+    )
+    return own + swap_x(send).astype(F32), half_solution.T, root_solution.T
 
 
 def pick(values, index):
@@ -100,7 +468,7 @@
     return mine + swap(sent.astype(BF16), "row", 1).astype(F32)
 
 
-def solve(
+def solve_plain(
     inverse_quarter,
     inverse_half,
     inverse_root,
@@ -184,29 +552,33 @@
         (jnp.int32(0), sub_index, jnp.int32(0), column_index * block_count),
         (3, 1, 2, block_count),
     )[:, 0]
-    masking = jnp.repeat(row_flags, BLK, axis=2).astype(F32)[:, :, :, None]
-    width = right_root.shape[1] // STREAMS
-    outs = []
-    for stream in range(STREAMS):
-        columns = slice(stream * width, (stream + 1) * width)
-        outs.append(
-            solve(
-                inverse_quarter[0],
-                inverse_half[0],
-                inverse_root,
-                quarter_to_half[0],
-                quarter_to_root[0],
-                half_to_root[0],
-                right_quarter[0][:, columns],
-                right_half[0][:, columns],
-                right_root[:, columns],
-                masking,
-            )
+    smallest = min(inverse_quarter.shape[1] // 4, inverse_half.shape[1] // 8, inverse_root.shape[0] // 16)
+    if (lax.axis_size("row"), lax.axis_size("col")) != (2, 4) or smallest % 128:
+        quarter, half, root = solve_plain(
+            inverse_quarter[0],
+            inverse_half[0],
+            inverse_root,
+            quarter_to_half[0],
+            quarter_to_root[0],
+            half_to_root[0],
+            right_quarter[0],
+            right_half[0],
+            right_root,
+            jnp.repeat(row_flags, BLK, axis=2).astype(F32)[:, :, :, None],
         )
-    quarter, half, root = (
-        parts[0] if STREAMS == 1 else jnp.concatenate(parts, axis=1) for parts in zip(*outs)
-    )
-    return (final_sum(quarter)[None], half[None], root)
+        return (final_sum(quarter)[None], half[None], root)
+    panels = [p[0].reshape(-1, p.shape[3]) for p in (quarter_to_half, quarter_to_root, half_to_root)]
+    quarter, half, root = solve(
+        inverse_quarter[0],
+        inverse_half[0],
+        inverse_root,
+        *panels,
+        right_quarter[0],
+        right_half[0],
+        right_root,
+        row_flags.reshape(3, -1),
+    )
+    return (quarter[None], half[None], root)
 
 
 def solution(mesh):

time: 786 us -> 668 us (0.85)
  the two profiles are of different devices: /device:TPU:12 before, /device:TPU:0 now
where the time goes in v2:
time: 668 us; the launch traced here: 666 us
  waiting for transfers between devices  380 us (57%)
  Pallas kernels  131 us (20%)
  starting transfers between devices  96.8 us (14%)
  local copies, waits for them, and re-layouts  45.9 us (7%)
  other arithmetic  11.1 us (2%)
    ppermute x66, waiting for transfers between devices, swap(): return lax.ppermute(values, axis, pairs)  380 us
    ppermute x66, starting transfers between devices, swap(): return lax.ppermute(values, axis, pairs)  96.8 us
    pallas_call x6, Pallas kernels, multiply_back(): pl.pallas_call(body, grid_spec=pltpu.PrefetchScalarGridSpec(num_scalar_pr...  66 us
    pallas_call x6, Pallas kernels, multiply(): pl.pallas_call(body, grid_spec=pltpu.PrefetchScalarGridSpec(num_scalar_pr...  64.5 us
    unnamed x48, local copies, waits for them, and re-layouts  18.2 us
    pallas_call x8, local copies, waits for them, and re-layouts, multiply(): pl.pallas_call(body, grid_spec=pltpu.PrefetchScalarGridSpec(num_scalar_pr...  15.2 us
  transfers between devices with their start and end apart: 66, of which 39 were waited for; matrix products, arithmetic and copies ran while one was open for 3% of the time, Pallas kernels for 3%

profile of v2, /device:TPU:0, one launch (start us, length us, event | category | flops | bytes accessed | tf_op | source)
XLA Modules:
  0.0 665.8 jit_solution(8225808961036576588)
XLA Ops:
  2.1 11.2 %shard_map.121 = (bf16[1024,256]{1,0:T(8,128)(2,1)S(1)}, bf16[1024,256]{1,0:T(8,128)(2,1)S(1)}, bf16[1024,256]{1,0:T(8,128)(2,1)S(1)}, f32[1024,256]{1,0:T(8,128)S(1)}) custom-call(s32[1]{0:T(128)} %constant.43.clone.1.places.shown, s32[8]{0:T(128)S(1)} %add.309.visit, s32[1]{0:T(128)} %constant.43.clone.1.places.shown, bf16[2048,256]{1,0:T(8,128)(2,1)S(1)} %bitcast.62, ...), custom_call_target="tpu_custom_call" | custom-call | flops 4294967296 | bytes 23068672 | tf_op jit(solution)/shard_map/pallas_call | solution.py:91
  32.6 31.9 %collective-permute-done.1 = bf16[1024,256]{0,1:T(8,128)(2,1)} collective-permute-done((bf16[1024,256]{0,1:T(8,128)(2,1)}, bf16[1024,256]{0,1:T(8,128)(2,1)}, u32[]{:S(2)}, u32[]{:S(2)}) %collective-permute-start.1) | collective-permute-done | bytes 524320 | tf_op jit(solution)/shard_map/ppermute | solution.py:16
  83.1 28.6 %collective-permute-done.4 = bf16[1024,256]{0,1:T(8,128)(2,1)S(1)} collective-permute-done((bf16[1024,256]{0,1:T(8,128)(2,1)S(1)}, bf16[1024,256]{0,1:T(8,128)(2,1)S(1)}, u32[]{:S(2)}, u32[]{:S(2)}) %collective-permute-start.4) | collective-permute-done | bytes 524320 | tf_op jit(solution)/shard_map/ppermute | solution.py:16
  112.2 11.2 %shard_map.122 = (bf16[1024,256]{1,0:T(8,128)(2,1)S(1)}, f32[1024,256]{1,0:T(8,128)S(1)}) custom-call(s32[4]{0:T(128)S(1)} %pad_add_fusion.places, s32[8]{0:T(128)S(1)} %add.327.visit, s32[8]{0:T(128)S(1)} %squeeze.21.shown, bf16[1024,256]{1,0:T(8,128)(2,1)S(1)} %copy.43.refs_0_, bf16[1024,256]{1,0:T(8,128)(2,1)S(1)} %copy.44.refs_1_, ...), custom_call_target="tpu_custom_call" | custom-call | flops 4294967296 | bytes 23068672 | tf_op jit(solution)/shard_map/pallas_call | solution.py:91
  127.2 12.4 %collective-permute-done.7 = bf16[1024,256]{1,0:T(8,128)(2,1)S(1)} collective-permute-done((bf16[1024,256]{1,0:T(8,128)(2,1)S(1)}, bf16[1024,256]{1,0:T(8,128)(2,1)S(1)}, u32[]{:S(2)}, u32[]{:S(2)}) %collective-permute-start.7) | collective-permute-done | bytes 524320 | tf_op jit(solution)/shard_map/ppermute | solution.py:16
  170.5 12.0 %collective-permute-done.10 = bf16[512,256]{0,1:T(8,128)(2,1)S(1)} collective-permute-done((bf16[512,256]{0,1:T(8,128)(2,1)S(1)}, bf16[512,256]{0,1:T(8,128)(2,1)S(1)}, u32[]{:S(2)}, u32[]{:S(2)}) %collective-permute-start.10) | collective-permute-done | bytes 262176 | tf_op jit(solution)/shard_map/ppermute | solution.py:16
  231.6 11.3 %shard_map.125 = (bf16[1024,256]{1,0:T(8,128)(2,1)S(1)}, f32[1024,256]{1,0:T(8,128)S(1)}) custom-call(s32[8]{0:T(128)S(1)} %stack.175.places, s32[8]{0:T(128)S(1)} %add.357.visit, s32[8]{0:T(128)S(1)} %squeeze.23.shown, bf16[512,256]{1,0:T(8,128)(2,1)S(1)} %copy.53.refs_0_, bf16[512,256]{1,0:T(8,128)(2,1)S(1)} %copy.54.refs_1_, ...), custom_call_target="tpu_custom_call" | custom-call | flops 4294967296 | bytes 23068672 | tf_op jit(solution)/shard_map/pallas_call | solution.py:91
  244.5 12.3 %collective-permute-done.19 = bf16[1024,256]{1,0:T(8,128)(2,1)S(1)} collective-permute-done((bf16[1024,256]{1,0:T(8,128)(2,1)S(1)}, bf16[1024,256]{1,0:T(8,128)(2,1)S(1)}, u32[]{:S(2)}, u32[]{:S(2)}) %collective-permute-start.19) | collective-permute-done | bytes 524320 | tf_op jit(solution)/shard_map/ppermute | solution.py:16
  258.6 11.4 %collective-permute-done.20 = bf16[1024,256]{1,0:T(8,128)(2,1)S(1)} collective-permute-done((bf16[1024,256]{1,0:T(8,128)(2,1)S(1)}, bf16[1024,256]{1,0:T(8,128)(2,1)S(1)}, u32[]{:S(2)}, u32[]{:S(2)}) %collective-permute-start.20) | collective-permute-done | bytes 524320 | tf_op jit(solution)/shard_map/ppermute | solution.py:16
  270.2 15.3 %shard_map.126 = (bf16[4096,256]{1,0:T(8,128)(2,1)S(1)}, f32[4096,256]{1,0:T(8,128)S(1)}) custom-call(s32[1]{0:T(128)} %constant.43.clone.1.places.shown, s32[16]{0:T(128)S(1)} %stack.198.visit, s32[1]{0:T(128)} %constant.43.clone.1.places.shown, bf16[1024,256]{1,0:T(8,128)(2,1)S(1)} %subtract_convert_fusion.refs_0_, bf16[8192,1024]{1,0:T(8,128)(2,1)} %refs_16_.1), custom_call_target="tpu_custom_call" | custom-call | flops 4294967296 | bytes 26214400 | tf_op jit(solution)/shard_map/pallas_call | solution.py:91
  355.8 14.8 %collective-permute-done.30.refs_2_ = bf16[256,512]{1,0:T(8,128)(2,1)S(1)} collective-permute-done((bf16[256,512]{1,0:T(8,128)(2,1)S(1)}, bf16[256,512]{1,0:T(8,128)(2,1)S(1)}, u32[]{:S(2)}, u32[]{:S(2)}) %collective-permute-start.30) | collective-permute-done | bytes 262176 | tf_op jit(solution)/shard_map/ppermute | solution.py:16
  382.9 14.0 %shard_map.127 = bf16[256,1024]{1,0:T(8,128)(2,1)S(1)} custom-call(s32[16]{0:T(128)S(1)} %stack.197.places, s32[8]{0:T(128)S(1)} %iota.24.visit, s32[1]{0:T(128)} %constant.43.clone.1.places.shown, bf16[256,512]{1,0:T(8,128)(2,1)S(1)} %fusion.16.refs_0_, bf16[256,512]{1,0:T(8,128)(2,1)S(1)} %collective-permute-done.29.refs_1_, ...), custom_call_target="tpu_custom_call" | custom-call | flops 4294967296 | bytes 26214400 | tf_op jit(solution)/shard_map/pallas_call | solution.py:187
  398.5 12.5 %collective-permute-done.44 = bf16[256,1024]{1,0:T(8,128)(2,1)S(1)} collective-permute-done((bf16[256,1024]{1,0:T(8,128)(2,1)S(1)}, bf16[256,1024]{1,0:T(8,128)(2,1)S(1)}, u32[]{:S(2)}, u32[]{:S(2)}) %collective-permute-start.44) | collective-permute-done | bytes 524320 | tf_op jit(solution)/shard_map/ppermute | solution.py:16
  411.6 12.8 %collective-permute-done.45.refs_1_ = bf16[256,1024]{1,0:T(8,128)(2,1)S(1)} collective-permute-done((bf16[256,1024]{1,0:T(8,128)(2,1)S(1)}, bf16[256,1024]{1,0:T(8,128)(2,1)S(1)}, u32[]{:S(2)}, u32[]{:S(2)}) %collective-permute-start.45) | collective-permute-done | bytes 524320 | tf_op jit(solution)/shard_map/ppermute | solution.py:16
  424.4 11.5 %shard_map.128 = (bf16[256,2048]{1,0:T(8,128)(2,1)S(1)}, f32[256,2048]{1,0:T(8,128)S(1)}) custom-call(s32[2]{0:T(128)S(1)} %pad_add_fusion.2.places, s32[8]{0:T(128)S(1)} %stack.176.visit, s32[8]{0:T(128)S(1)} %squeeze.23.shown, bf16[256,1024]{1,0:T(8,128)(2,1)S(1)} %add_convert_fusion.1.refs_0_, bf16[256,1024]{1,0:T(8,128)(2,1)S(1)} %collective-permute-done.45.refs_1_, ...), custom_call_target="tpu_custom_call" | custom-call | flops 4294967296 | bytes 23068672 | tf_op jit(solution)/shard_map/pallas_call | solution.py:187
  482.4 12.1 %collective-permute-done.51.refs_2_ = bf16[256,512]{1,0:T(8,128)(2,1)S(1)} collective-permute-done((bf16[256,512]{1,0:T(8,128)(2,1)S(1)}, bf16[256,512]{1,0:T(8,128)(2,1)S(1)}, u32[]{:S(2)}, u32[]{:S(2)}) %collective-permute-start.51) | collective-permute-done | bytes 262176 | tf_op jit(solution)/shard_map/ppermute | solution.py:16
  502.8 12.5 %collective-permute-done.57 = bf16[256,1024]{1,0:T(8,128)(2,1)S(1)} collective-permute-done((bf16[256,1024]{1,0:T(8,128)(2,1)S(1)}, bf16[256,1024]{1,0:T(8,128)(2,1)S(1)}, u32[]{:S(2)}, u32[]{:S(2)}) %collective-permute-start.57) | collective-permute-done | bytes 524320 | tf_op jit(solution)/shard_map/ppermute | solution.py:16
  515.7 11.5 %shard_map.130.refs_3_ = f32[256,4096]{1,0:T(8,128)S(1)} custom-call(s32[2]{0:T(128)S(1)} %pad_add_fusion.2.places, s32[8]{0:T(128)S(1)} %add.309.visit, s32[8]{0:T(128)S(1)} %squeeze.24.shown, bf16[256,1024]{1,0:T(8,128)(2,1)S(1)} %add_convert_fusion.1.refs_0_, bf16[256,1024]{1,0:T(8,128)(2,1)S(1)} %collective-permute-done.45.refs_1_, ...), custom_call_target="tpu_custom_call" | custom-call | flops 4294967296 | bytes 23068672 | tf_op jit(solution)/shard_map/pallas_call | solution.py:187
  527.2 11.8 %shard_map.131 = (bf16[256,1024]{1,0:T(8,128)(2,1)S(1)}, bf16[256,1024]{1,0:T(8,128)(2,1)S(1)}, bf16[256,1024]{1,0:T(8,128)(2,1)S(1)}, f32[256,1024]{1,0:T(8,128)S(1)}) custom-call(s32[2]{0:T(128)S(1)} %pad_add_fusion.1.places, s32[8]{0:T(128)S(1)} %add.309.visit, s32[8]{0:T(128)S(1)} %squeeze.21.shown, bf16[256,1024]{1,0:T(8,128)(2,1)S(1)} %add_convert_fusion.refs_0_, ...), custom_call_target="tpu_custom_call" | custom-call | flops 4294967296 | bytes 23068672 | tf_op jit(solution)/shard_map/pallas_call | solution.py:187
  543.4 20.1 %collective-permute-done.59 = bf16[256,1024]{1,0:T(8,128)(2,1)S(1)} collective-permute-done((bf16[256,1024]{1,0:T(8,128)(2,1)S(1)}, bf16[256,1024]{1,0:T(8,128)(2,1)S(1)}, u32[]{:S(2)}, u32[]{:S(2)}) %collective-permute-start.59) | collective-permute-done | bytes 524320 | tf_op jit(solution)/shard_map/ppermute | solution.py:16
  563.5 13.8 %collective-permute-done.60 = bf16[256,1024]{1,0:T(8,128)(2,1)S(1)} collective-permute-done((bf16[256,1024]{1,0:T(8,128)(2,1)S(1)}, bf16[256,1024]{1,0:T(8,128)(2,1)S(1)}, u32[]{:S(2)}, u32[]{:S(2)}) %collective-permute-start.60) | collective-permute-done | bytes 524320 | tf_op jit(solution)/shard_map/ppermute | solution.py:16
  579.3 22.5 %collective-permute-start.63 = (bf16[256,1024]{1,0:T(8,128)(2,1)S(1)}, bf16[256,1024]{1,0:T(8,128)(2,1)S(1)}, u32[]{:S(2)}, u32[]{:S(2)}) collective-permute-start(bf16[256,1024]{1,0:T(8,128)(2,1)S(1)} %fusion.1.refs_0_), channel_id=1, source_target_pairs={{0,2},{1,3},{2,0},{3,1},{4,6},{5,7},{6,4},{7,5},{8,10},{9,11},{10,... | collective-permute-start | bytes 1572872 | tf_op jit(solution)/shard_map/ppermute | solution.py:16
  601.8 34.0 %collective-permute-done.63.refs_2_ = bf16[256,1024]{1,0:T(8,128)(2,1)S(1)} collective-permute-done((bf16[256,1024]{1,0:T(8,128)(2,1)S(1)}, bf16[256,1024]{1,0:T(8,128)(2,1)S(1)}, u32[]{:S(2)}, u32[]{:S(2)}) %collective-permute-start.63) | collective-permute-done | bytes 524320 | tf_op jit(solution)/shard_map/ppermute | solution.py:16
  639.5 12.4 %shard_map.132 = (f32[2048,128]{1,0:T(8,128)S(1)}, bf16[2048,128]{1,0:T(8,128)(2,1)}) custom-call(s32[4]{0:T(128)S(1)} %pad_add_fusion.places, s32[8]{0:T(128)S(1)} %iota.22.visit, s32[1]{0:T(128)} %bitcast.4.shown, bf16[256,1024]{1,0:T(8,128)(2,1)S(1)} %fusion.1.refs_0_, bf16[256,1024]{1,0:T(8,128)(2,1)S(1)} %copy-done.14, ...), custom_call_target="tpu_custom_call" | custom-call | flops 4294967296 | bytes 23068672 | tf_op jit(solution)/shard_map/pallas_call | solution.py:187
  (230 shorter events, 290.8 us)
Async XLA Ops:
  20.4 44.1 %collective-permute-start.1 = (bf16[1024,256]{0,1:T(8,128)(2,1)}, bf16[1024,256]{0,1:T(8,128)(2,1)}, u32[]{:S(2)}, u32[]{:S(2)}) collective-permute-start(bf16[1024,256]{0,1:T(8,128)(2,1)} %copy.41), channel_id=1, source_target_pairs={{0,2},{1,3},{2,0},{3,1},{4,6},{5,7},{6,4},{7,5},{8,10},{9,11},{10,... | collective-permute-start | bytes 1572872 | tf_op jit(solution)/shard_map/ppermute | solution.py:16
  20.6 43.9 %collective-permute-start = (bf16[1024,256]{0,1:T(8,128)(2,1)S(1)}, bf16[1024,256]{0,1:T(8,128)(2,1)S(1)}, u32[]{:S(2)}, u32[]{:S(2)}) collective-permute-start(bf16[1024,256]{0,1:T(8,128)(2,1)S(1)} %copy.39), channel_id=1, source_target_pairs={{0,1},{1,0},{2,3},{3,2},{4,5},{5,4},{6,7},{7,6},{8,9},{9,8},{10,11... | collective-permute-start | bytes 1572872 | tf_op jit(solution)/shard_map/ppermute | solution.py:16
  68.6 43.1 %collective-permute-start.4 = (bf16[1024,256]{0,1:T(8,128)(2,1)S(1)}, bf16[1024,256]{0,1:T(8,128)(2,1)S(1)}, u32[]{:S(2)}, u32[]{:S(2)}) collective-permute-start(bf16[1024,256]{0,1:T(8,128)(2,1)S(1)} %add_convert_fusion.4), channel_id=1, source_target_pairs={{0,2},{1,3},{2,0},{3,1},{4,6},{5,7},{6,4},{7,5},{8,10},{9,11},{10,... | collective-permute-start | bytes 1572872 | tf_op jit(solution)/shard_map/ppermute | solution.py:16
  68.6 43.3 %collective-permute-start.3 = (bf16[1024,256]{0,1:T(8,128)(2,1)S(1)}, bf16[1024,256]{0,1:T(8,128)(2,1)S(1)}, u32[]{:S(2)}, u32[]{:S(2)}) collective-permute-start(bf16[1024,256]{0,1:T(8,128)(2,1)S(1)} %add_convert_fusion.4), channel_id=1, source_target_pairs={{0,1},{1,0},{2,3},{3,2},{4,5},{5,4},{6,7},{7,6},{8,9},{9,8},{10,11... | collective-permute-start | bytes 1572872 | tf_op jit(solution)/shard_map/ppermute | solution.py:16
  157.7 24.8 %collective-permute-start.10 = (bf16[512,256]{0,1:T(8,128)(2,1)S(1)}, bf16[512,256]{0,1:T(8,128)(2,1)S(1)}, u32[]{:S(2)}, u32[]{:S(2)}) collective-permute-start(bf16[512,256]{0,1:T(8,128)(2,1)S(1)} %get-tuple-element.67), channel_id=1, source_target_pairs={{0,2},{1,3},{2,0},{3,1},{4,6},{5,7},{6,4},{7,5},{8,10},{9,11},{10,... | collective-permute-start | bytes 786440 | tf_op jit(solution)/shard_map/ppermute | solution.py:16
  184.3 20.8 %collective-permute-start.13 = (bf16[512,256]{0,1:T(8,128)(2,1)S(1)}, bf16[512,256]{0,1:T(8,128)(2,1)}, u32[]{:S(2)}, u32[]{:S(2)}) collective-permute-start(bf16[512,256]{0,1:T(8,128)(2,1)S(1)} %fusion.15), channel_id=1, source_target_pairs={{0,2},{1,3},{2,0},{3,1},{4,6},{5,7},{6,4},{7,5},{8,10},{9,11},{10,... | collective-permute-start | bytes 786440 | tf_op jit(solution)/shard_map/ppermute | solution.py:16
  184.3 20.8 %collective-permute-start.12 = (bf16[512,256]{0,1:T(8,128)(2,1)S(1)}, bf16[512,256]{0,1:T(8,128)(2,1)}, u32[]{:S(2)}, u32[]{:S(2)}) collective-permute-start(bf16[512,256]{0,1:T(8,128)(2,1)S(1)} %fusion.15), channel_id=1, source_target_pairs={{0,1},{1,0},{2,3},{3,2},{4,5},{5,4},{6,7},{7,6},{8,9},{9,8},{10,11... | collective-permute-start | bytes 786440 | tf_op jit(solution)/shard_map/ppermute | solution.py:16
  187.5 34.8 %collective-permute-start.15 = (bf16[512,256]{0,1:T(8,128)(2,1)S(1)}, bf16[512,256]{0,1:T(8,128)(2,1)}, u32[]{:S(2)}, u32[]{:S(2)}) collective-permute-start(bf16[512,256]{0,1:T(8,128)(2,1)S(1)} %fusion.15), channel_id=1, source_target_pairs={{0,8},{8,0},{16,24},{24,16},{1,9},{9,1},{17,25},{25,17},{2,10},{10... | collective-permute-start | bytes 786440 | tf_op jit(solution)/shard_map/ppermute | solution.py:16
  194.0 29.4 %collective-permute-start.18 = (bf16[512,256]{0,1:T(8,128)(2,1)}, bf16[512,256]{0,1:T(8,128)(2,1)}, u32[]{:S(2)}, u32[]{:S(2)}) collective-permute-start(bf16[512,256]{0,1:T(8,128)(2,1)} %collective-permute-done.14), channel_id=1, source_target_pairs={{0,8},{8,0},{16,24},{24,16},{1,9},{9,1},{17,25},{25,17},{2,10},{10... | collective-permute-start | bytes 786440 | tf_op jit(solution)/shard_map/ppermute | solution.py:16
  205.1 20.1 %collective-permute-start.17 = (bf16[512,256]{0,1:T(8,128)(2,1)}, bf16[512,256]{0,1:T(8,128)(2,1)}, u32[]{:S(2)}, u32[]{:S(2)}) collective-permute-start(bf16[512,256]{0,1:T(8,128)(2,1)} %collective-permute-done.13), channel_id=1, source_target_pairs={{0,8},{8,0},{16,24},{24,16},{1,9},{9,1},{17,25},{25,17},{2,10},{10... | collective-permute-start | bytes 786440 | tf_op jit(solution)/shard_map/ppermute | solution.py:16
  205.1 21.9 %collective-permute-start.16 = (bf16[512,256]{0,1:T(8,128)(2,1)}, bf16[512,256]{0,1:T(8,128)(2,1)}, u32[]{:S(2)}, u32[]{:S(2)}) collective-permute-start(bf16[512,256]{0,1:T(8,128)(2,1)} %collective-permute-done.12), channel_id=1, source_target_pairs={{0,8},{8,0},{16,24},{24,16},{1,9},{9,1},{17,25},{25,17},{2,10},{10... | collective-permute-start | bytes 786440 | tf_op jit(solution)/shard_map/ppermute | solution.py:16
  302.7 22.0 %collective-permute-start.22 = (bf16[512,256]{0,1:T(8,128)(2,1)S(1)}, bf16[512,256]{0,1:T(8,128)(2,1)S(1)}, u32[]{:S(2)}, u32[]{:S(2)}) collective-permute-start(bf16[512,256]{0,1:T(8,128)(2,1)S(1)} %get-tuple-element.58), channel_id=1, source_target_pairs={{0,16},{8,24},{16,0},{24,8},{1,17},{9,25},{17,1},{25,9},{2,18},{10... | collective-permute-start | bytes 786440 | tf_op jit(solution)/shard_map/ppermute | solution.py:16
  319.8 21.4 %collective-permute-start.26 = (bf16[512,256]{0,1:T(8,128)(2,1)S(1)}, bf16[512,256]{0,1:T(8,128)(2,1)S(1)}, u32[]{:S(2)}, u32[]{:S(2)}) collective-permute-start(bf16[512,256]{0,1:T(8,128)(2,1)S(1)} %get-tuple-element.56), channel_id=1, source_target_pairs={{0,2},{1,3},{2,0},{3,1},{4,6},{5,7},{6,4},{7,5},{8,10},{9,11},{10,... | collective-permute-start | bytes 786440 | tf_op jit(solution)/shard_map/ppermute | solution.py:16
  345.3 25.2 %collective-permute-start.30 = (bf16[256,512]{1,0:T(8,128)(2,1)S(1)}, bf16[256,512]{1,0:T(8,128)(2,1)S(1)}, u32[]{:S(2)}, u32[]{:S(2)}) collective-permute-start(bf16[256,512]{1,0:T(8,128)(2,1)S(1)} %fusion.16.refs_0_), channel_id=1, source_target_pairs={{0,2},{1,3},{2,0},{3,1},{4,6},{5,7},{6,4},{7,5},{8,10},{9,11},{10,... | collective-permute-start | bytes 786440 | tf_op jit(solution)/shard_map/ppermute | solution.py:16
  448.6 22.5 %collective-permute-start.48 = (bf16[256,512]{1,0:T(8,128)(2,1)S(1)}, bf16[256,512]{1,0:T(8,128)(2,1)S(1)}, u32[]{:S(2)}, u32[]{:S(2)}) collective-permute-start(bf16[256,512]{1,0:T(8,128)(2,1)S(1)} %get-tuple-element.64), channel_id=1, source_target_pairs={{0,2},{1,3},{2,0},{3,1},{4,6},{5,7},{6,4},{7,5},{8,10},{9,11},{10,... | collective-permute-start | bytes 786440 | tf_op jit(solution)/shard_map/ppermute | solution.py:16
  473.5 21.0 %collective-permute-start.51 = (bf16[256,512]{1,0:T(8,128)(2,1)S(1)}, bf16[256,512]{1,0:T(8,128)(2,1)S(1)}, u32[]{:S(2)}, u32[]{:S(2)}) collective-permute-start(bf16[256,512]{1,0:T(8,128)(2,1)S(1)} %fusion.5.refs_0_), channel_id=1, source_target_pairs={{0,2},{1,3},{2,0},{3,1},{4,6},{5,7},{6,4},{7,5},{8,10},{9,11},{10,... | collective-permute-start | bytes 786440 | tf_op jit(solution)/shard_map/ppermute | solution.py:16
  473.5 21.0 %collective-permute-start.50 = (bf16[256,512]{1,0:T(8,128)(2,1)S(1)}, bf16[256,512]{1,0:T(8,128)(2,1)S(1)}, u32[]{:S(2)}, u32[]{:S(2)}) collective-permute-start(bf16[256,512]{1,0:T(8,128)(2,1)S(1)} %fusion.5.refs_0_), channel_id=1, source_target_pairs={{0,1},{1,0},{2,3},{3,2},{4,5},{5,4},{6,7},{7,6},{8,9},{9,8},{10,11... | collective-permute-start | bytes 786440 | tf_op jit(solution)/shard_map/ppermute | solution.py:16
  475.7 19.4 %collective-permute-start.53 = (bf16[256,512]{1,0:T(8,128)(2,1)S(1)}, bf16[256,512]{1,0:T(8,128)(2,1)S(1)}, u32[]{:S(2)}, u32[]{:S(2)}) collective-permute-start(bf16[256,512]{1,0:T(8,128)(2,1)S(1)} %fusion.5.refs_0_), channel_id=1, source_target_pairs={{0,8},{8,0},{16,24},{24,16},{1,9},{9,1},{17,25},{25,17},{2,10},{10... | collective-permute-start | bytes 786440 | tf_op jit(solution)/shard_map/ppermute | solution.py:16
  538.9 24.5 %collective-permute-start.59 = (bf16[256,1024]{1,0:T(8,128)(2,1)S(1)}, bf16[256,1024]{1,0:T(8,128)(2,1)S(1)}, u32[]{:S(2)}, u32[]{:S(2)}) collective-permute-start(bf16[256,1024]{1,0:T(8,128)(2,1)S(1)} %get-tuple-element.38), channel_id=1, source_target_pairs={{0,1},{1,0},{2,3},{3,2},{4,5},{5,4},{6,7},{7,6},{8,9},{9,8},{10,11... | collective-permute-start | bytes 1572872 | tf_op jit(solution)/shard_map/ppermute | solution.py:16
  539.0 38.2 %collective-permute-start.60 = (bf16[256,1024]{1,0:T(8,128)(2,1)S(1)}, bf16[256,1024]{1,0:T(8,128)(2,1)S(1)}, u32[]{:S(2)}, u32[]{:S(2)}) collective-permute-start(bf16[256,1024]{1,0:T(8,128)(2,1)S(1)} %get-tuple-element.39), channel_id=1, source_target_pairs={{0,2},{1,3},{2,0},{3,1},{4,6},{5,7},{6,4},{7,5},{8,10},{9,11},{10,... | collective-permute-start | bytes 1572872 | tf_op jit(solution)/shard_map/ppermute | solution.py:16
  541.1 36.1 %collective-permute-start.61 = (bf16[256,1024]{1,0:T(8,128)(2,1)S(1)}, bf16[256,1024]{1,0:T(8,128)(2,1)S(1)}, u32[]{:S(2)}, u32[]{:S(2)}) collective-permute-start(bf16[256,1024]{1,0:T(8,128)(2,1)S(1)} %get-tuple-element.40), channel_id=1, source_target_pairs={{0,3},{1,2},{2,1},{3,0},{4,7},{5,6},{6,5},{7,4},{8,11},{9,10},{10,... | collective-permute-start | bytes 1572872 | tf_op jit(solution)/shard_map/ppermute | solution.py:16
  577.7 24.2 %collective-permute-start.64 = (bf16[256,1024]{1,0:T(8,128)(2,1)S(1)}, bf16[256,1024]{1,0:T(8,128)(2,1)S(1)}, u32[]{:S(2)}, u32[]{:S(2)}) collective-permute-start(bf16[256,1024]{1,0:T(8,128)(2,1)S(1)} %fusion.1.refs_0_), channel_id=1, source_target_pairs={{0,3},{1,2},{2,1},{3,0},{4,7},{5,6},{6,5},{7,4},{8,11},{9,10},{10,... | collective-permute-start | bytes 1572872 | tf_op jit(solution)/shard_map/ppermute | solution.py:16
  579.3 56.5 %collective-permute-start.63 = (bf16[256,1024]{1,0:T(8,128)(2,1)S(1)}, bf16[256,1024]{1,0:T(8,128)(2,1)S(1)}, u32[]{:S(2)}, u32[]{:S(2)}) collective-permute-start(bf16[256,1024]{1,0:T(8,128)(2,1)S(1)} %fusion.1.refs_0_), channel_id=1, source_target_pairs={{0,2},{1,3},{2,0},{3,1},{4,6},{5,7},{6,4},{7,5},{8,10},{9,11},{10,... | collective-permute-start | bytes 1572872 | tf_op jit(solution)/shard_map/ppermute | solution.py:16
  601.8 34.8 %collective-permute-start.62 = (bf16[256,1024]{1,0:T(8,128)(2,1)S(1)}, bf16[256,1024]{1,0:T(8,128)(2,1)S(1)}, u32[]{:S(2)}, u32[]{:S(2)}) collective-permute-start(bf16[256,1024]{1,0:T(8,128)(2,1)S(1)} %fusion.1.refs_0_), channel_id=1, source_target_pairs={{0,1},{1,0},{2,3},{3,2},{4,5},{5,4},{6,7},{7,6},{8,9},{9,8},{10,11... | collective-permute-start | bytes 1572872 | tf_op jit(solution)/shard_map/ppermute | solution.py:16
  (65 other events, 891.2 us)

commit v3 on v2

--- a/solution.py
+++ b/solution.py
@@ -6,7 +6,8 @@
 from jax.sharding import PartitionSpec as P
 
 BLK = 256
-BLOCK_BYTES = 1 << 21
+STREAMS = 2
+KERNEL_VMEM = 20 << 20
 F32 = jnp.float32
 BF16 = jnp.bfloat16
 
@@ -32,11 +33,33 @@
     return swap(values, "row", 1)
 
 
+def fetch(matrix, after=None):
+    def body(*refs):
+        copy = pltpu.make_async_copy(refs[0], refs[-2], refs[-1])
+        copy.start()
+        copy.wait()
+
+    matrix = pltpu.with_memory_space_constraint(matrix, pltpu.HBM)
+    operands = [matrix] if after is None else [matrix, after]
+    return pl.pallas_call(
+        body,
+        in_specs=[pl.BlockSpec(memory_space=pltpu.HBM)] * len(operands),
+        out_specs=pl.BlockSpec(memory_space=pltpu.VMEM),
+        out_shape=jax.ShapeDtypeStruct(matrix.shape, matrix.dtype),
+        scratch_shapes=[pltpu.SemaphoreType.DMA],
+        compiler_params=pltpu.CompilerParams(vmem_limit_bytes=1 << 20),
+        cost_estimate=pl.CostEstimate(
+            flops=0, transcendentals=0, bytes_accessed=4 * matrix.size
+        ),
+        name="fetch",
+    )(*operands)
+
+
 def multiply(matrix, vectors, in_blocks, order, outs, flags=None, addend=None):
     rows, inner = matrix.shape
     width = vectors[0].shape[1]
-    tile = rows // order.shape[0]
     steps = order.shape[0]
+    tile = rows // steps
     in_size = inner // in_blocks.shape[0]
     starts = [0]
     for out_rows, _ in outs:
@@ -64,9 +87,18 @@
 
         else:
             x_ref = vector_refs[0]
-        total = jnp.dot(matrix_ref[...], x_ref[...], preferred_element_type=F32)
+        first_row = pl.multiple_of(visit[step] * tile, tile)
+        total = jnp.dot(
+            matrix_ref[pl.ds(first_row, tile), :], x_ref[...], preferred_element_type=F32
+        )
         if flags is not None:
-            total = total * shown[visit[step]].astype(F32)
+            block = visit[step] * (tile // BLK)
+            total = jnp.concatenate(
+                [
+                    total[i * BLK : (i + 1) * BLK] * shown[block + i].astype(F32)
+                    for i in range(tile // BLK)
+                ]
+            )
         if addend is not None:
             total = total + addend_ref[...]
         for index, ref in enumerate(out_refs):
@@ -78,16 +110,11 @@
     def out_map(first, last):
         return lambda i, *_: (jnp.clip(i - first, 0, last - first - 1), 0)
 
-    in_specs = [pl.BlockSpec(v.shape, lambda i, *_: (0, 0)) for v in vectors]
-    in_specs.append(pl.BlockSpec((tile, inner), lambda i, places, visit, shown: (visit[i], 0)))
+    in_specs = [pl.BlockSpec(memory_space=pltpu.VMEM)] * (count + 1)
     operands = list(vectors) + [matrix]
     if addend is not None:
         in_specs.append(pl.BlockSpec((tile, width), lambda i, *_: (i, 0)))
         operands.append(addend)
-    if flags is None:
-        flags_operand = jnp.zeros((1,), jnp.int32)
-    else:
-        flags_operand = flags
     return pl.pallas_call(
         body,
         grid_spec=pltpu.PrefetchScalarGridSpec(
@@ -101,16 +128,17 @@
             scratch_shapes=[pltpu.VMEM((inner, width), BF16)] if gathered else [],
         ),
         out_shape=[jax.ShapeDtypeStruct((r, width), t) for r, t in outs],
-        compiler_params=pltpu.CompilerParams(vmem_limit_bytes=40 << 20),
+        compiler_params=pltpu.CompilerParams(vmem_limit_bytes=KERNEL_VMEM),
         cost_estimate=pl.CostEstimate(
             flops=2 * rows * inner * width,
             transcendentals=0,
-            bytes_accessed=2 * rows * inner + 4 * (rows + inner) * width,
+            bytes_accessed=4 * (rows + inner) * width,
         ),
-    )(in_blocks, order, flags_operand, *operands)
-
-
-def multiply_back(matrix, vectors, in_blocks, order, outs, flags=None, addend=None, side=None):
+        name="multiply",
+    )(in_blocks, order, jnp.zeros((1,), jnp.int32) if flags is None else flags, *operands)
+
+
+def multiply_back(matrix, vectors, in_blocks, order, outs, flags=None, addend=None):
     inner, columns = matrix.shape
     width = vectors[0].shape[0]
     steps = order.shape[0]
@@ -149,16 +177,12 @@
                             )
                     at += 1
 
-        total = jnp.dot(y_ref[...], matrix_ref[...], preferred_element_type=F32)
+        first_column = pl.multiple_of(visit[step] * tile, tile)
+        total = jnp.dot(
+            y_ref[...], matrix_ref[:, pl.ds(first_column, tile)], preferred_element_type=F32
+        )
         if addend is not None:
             total = total + addend_ref[...]
-        if side is not None:
-            half = width // 2
-            first = shown[0] == 0
-            low, high = total[:half], total[half:]
-            out_refs[0][...] = jnp.where(first, low, high).T
-            out_refs[1][...] = jnp.where(first, high, low).T.astype(BF16)
-            return
         for index, ref in enumerate(out_refs):
 
             @pl.when((step >= starts[index]) & (step < starts[index + 1]))
@@ -168,39 +192,48 @@
     def out_map(first, last):
         return lambda i, *_: (0, jnp.clip(i - first, 0, last - first - 1))
 
-    in_specs = [pl.BlockSpec(v.shape, lambda i, *_: (0, 0)) for v in vectors]
-    in_specs.append(pl.BlockSpec((inner, tile), lambda i, places, visit, shown: (0, visit[i])))
+    in_specs = [pl.BlockSpec(memory_space=pltpu.VMEM)] * (count + 1)
     operands = list(vectors) + [matrix]
     if addend is not None:
         in_specs.append(pl.BlockSpec((width, tile), lambda i, *_: (0, i)))
         operands.append(addend)
-    if side is not None:
-        scalars = side[None]
-        out_specs = [pl.BlockSpec((tile, width // 2), lambda i, *_: (i, 0))] * 2
-        out_shape = [jax.ShapeDtypeStruct((columns, width // 2), t) for t in (F32, BF16)]
-    else:
-        scalars = jnp.zeros((1,), jnp.int32) if flags is None else flags
-        out_specs = [
-            pl.BlockSpec((width, tile), out_map(starts[i], starts[i + 1])) for i in range(len(outs))
-        ]
-        out_shape = [jax.ShapeDtypeStruct((width, c), t) for c, t in outs]
     return pl.pallas_call(
         body,
         grid_spec=pltpu.PrefetchScalarGridSpec(
             num_scalar_prefetch=3,
             grid=(steps,),
             in_specs=in_specs,
-            out_specs=out_specs,
+            out_specs=[
+                pl.BlockSpec((width, tile), out_map(starts[i], starts[i + 1]))
+                for i in range(len(outs))
+            ],
             scratch_shapes=[pltpu.VMEM((width, inner), BF16)],
         ),
-        out_shape=out_shape,
-        compiler_params=pltpu.CompilerParams(vmem_limit_bytes=40 << 20),
+        out_shape=[jax.ShapeDtypeStruct((width, c), t) for c, t in outs],
+        compiler_params=pltpu.CompilerParams(vmem_limit_bytes=KERNEL_VMEM),
         cost_estimate=pl.CostEstimate(
             flops=2 * columns * inner * width,
             transcendentals=0,
-            bytes_accessed=2 * columns * inner + 4 * (columns + inner) * width,
+            bytes_accessed=4 * (columns + inner) * width,
         ),
-    )(in_blocks, order, scalars, *operands)
+        name="multiply_back",
+    )(in_blocks, order, jnp.zeros((1,), jnp.int32) if flags is None else flags, *operands)
+
+
+def flip(values):
+    def body(in_ref, out_ref):
+        out_ref[...] = in_ref[...].T
+
+    rows, columns = values.shape
+    tile = min(rows, 256)
+    return pl.pallas_call(
+        body,
+        grid=(rows // tile,),
+        in_specs=[pl.BlockSpec((tile, columns), lambda i: (i, 0))],
+        out_specs=pl.BlockSpec((columns, tile), lambda i: (0, i)),
+        out_shape=jax.ShapeDtypeStruct((columns, rows), values.dtype),
+        name="flip",
+    )(values)
 
 
 def listed(*values):
@@ -210,10 +243,6 @@
 def spread(blocks, size, tile):
     parts = size // tile
     return (blocks[:, None] * parts + jnp.arange(parts, dtype=jnp.int32)[None]).reshape(-1)
-
-
-def tile_of(piece, inner):
-    return min(piece, max(128, BLOCK_BYTES // (2 * inner)))
 
 
 def add_all(own, *others):
@@ -225,6 +254,53 @@
 
 def both_rows(values):
     return values.astype(F32) + swap_x(values).astype(F32)
+
+
+def reduce_z(far_send, near_send, far_own, own):
+    passed = add_all(far_own, swap_z(far_send, 1)).astype(BF16)
+    return add_all(own, swap_z(near_send, 1), swap_z(passed, 3))
+
+
+def gather_z(piece):
+    across = swap_z(piece, 3)
+    beside = swap_z(piece, 1)
+    return [piece, beside, swap_z(across, 1), across]
+
+
+def cut(values, count, axis):
+    size = values.shape[axis] // count
+    return [lax.slice_in_dim(values, i * size, (i + 1) * size, axis=axis) for i in range(count)]
+
+
+def paired(parts, axis):
+    return [jnp.concatenate(parts[:2], axis=axis), jnp.concatenate(parts[2:], axis=axis)]
+
+
+def reduce_core_z(send, own, axis):
+    total = add_all(own, swap_core(send))
+    far_send, near_send, far_own, own = cut(total, 4, axis)
+    return reduce_z(far_send.astype(BF16), near_send.astype(BF16), far_own, own)
+
+
+def reduce_core_y_z(send, own, axis):
+    kept, sent = cut(add_all(own, swap_core(send)), 2, axis)
+    passed, final = [
+        add_all(k, swap_y(s.astype(BF16))) for k, s in zip(cut(kept, 2, axis), cut(sent, 2, axis))
+    ]
+    far_send, near_send = cut(passed, 2, axis)
+    far_own, own = cut(final, 2, axis)
+    return reduce_z(far_send.astype(BF16), near_send.astype(BF16), far_own, own)
+
+
+def gather_z_core(piece, axis):
+    parts = paired(gather_z(piece), axis)
+    return parts + [swap_core(p) for p in parts]
+
+
+def gather_z_y_core(piece, axis):
+    parts = paired(gather_z(piece), axis)
+    parts = parts + [swap_y(p) for p in parts]
+    return parts + [swap_core(p) for p in parts]
 
 
 def solve(
@@ -244,142 +320,141 @@
     low = sub_index % 2
     high = sub_index // 2
     zs = range(4)
+    visit_z = (2, 1, 3, 0)
     mask_half, mask_root, mask_upper = row_flags[0], row_flags[1], row_flags[2]
-    near = [1, 2, 3, 0]
     panel_rows, panel_columns = quarter_to_half.shape
     piece_rows = panel_rows // 2
+    panel_tile = min(piece_rows, 1024)
 
     col_blocks = listed(*[column ^ d for d in zs])
-    col_visit = listed(*[column ^ d for d in near])
-    low_visit = listed(low ^ 1, low)
-    high_visit = listed(high ^ 1, high)
+    col_visit = listed(*[column ^ d for d in visit_z])
     low_blocks = listed(low, low ^ 1)
     high_blocks = listed(high, high ^ 1)
+    low_visit = spread(listed(low ^ 1, low), piece_rows, panel_tile)
+    high_visit = spread(listed(high ^ 1, high), piece_rows, panel_tile)
     half_blocks = listed(*[(low ^ a) * 4 + (column ^ d) for a in (0, 1) for d in zs])
-    half_visit = listed(*[(low ^ a) * 4 + (column ^ d) for a in (1, 0) for d in zs])
-    root_visit = listed(
-        *[((low ^ a) * 2 + (high ^ b)) * 4 + (column ^ d) for a in (1, 0) for b in (0, 1) for d in zs]
-    )
-    root_blocks = listed(
-        *[((low ^ a) * 2 + (high ^ b)) * 4 + (column ^ d) for a in (0, 1) for b in (0, 1) for d in zs]
-    )
+    half_visit = listed(*[(low ^ a) * 4 + (column ^ d) for a in (1, 0) for d in visit_z])
+    root_place = lambda a, b, d: ((low ^ a) * 2 + (high ^ b)) * 4 + (column ^ d)
+    root_visit = listed(*[root_place(a, b, d) for a in (1, 0) for b in (0, 1) for d in visit_z])
+    root_blocks = listed(*[root_place(a, b, d) for a in (0, 1) for b in (0, 1) for d in zs])
     one = jnp.zeros((1,), jnp.int32)
-
-    rows, inner = inverse_quarter.shape
-    piece = rows // 4
-    tile = tile_of(piece, inner)
-    *sends, own = multiply(
-        inverse_quarter, [right_quarter], one, spread(col_visit, piece, tile),
-        [(piece, BF16)] * 3 + [(piece, F32)],
-    )
-    quarter_piece = add_all(own, *[swap_z(s, d) for s, d in zip(sends, (1, 2, 3))]).astype(BF16)
-    quarter_parts = [quarter_piece] + [swap_z(quarter_piece, d) for d in (1, 2, 3)]
-
-    send, own = multiply(
-        quarter_to_half, quarter_parts, col_blocks, spread(low_visit, piece_rows, BLK),
-        [(piece_rows, BF16), (piece_rows, F32)], flags=mask_half,
-    )
-    half_terms = both_rows(add_all(own, swap_core(send)).astype(BF16))
-    half_right = (right_half.astype(F32) - half_terms).astype(BF16)
-    (root_part,) = multiply(
-        quarter_to_root, quarter_parts, col_blocks, spread(high_visit, piece_rows, BLK),
-        [(panel_rows, F32)], flags=mask_root,
-    )
-
-    rows, inner = inverse_half.shape
-    piece = rows // 8
-    tile = tile_of(piece, inner)
-    send, own = multiply(
-        inverse_half, [half_right], one, spread(half_visit, piece, tile),
-        [(rows // 2, BF16), (rows // 2, F32)],
-    )
-    total = add_all(own, swap_core(send))
-    sends = [total[d * piece : (d + 1) * piece].astype(BF16) for d in zs]
-    half_piece = add_all(total[:piece], *[swap_z(sends[d], d) for d in (1, 2, 3)]).astype(BF16)
-    half_parts = [half_piece] + [swap_z(half_piece, d) for d in (1, 2, 3)]
-    half_parts = half_parts + [swap_core(p) for p in half_parts]
-
-    send, own = multiply(
-        half_to_root, half_parts, half_blocks, spread(high_visit, piece_rows, BLK),
-        [(piece_rows, BF16), (piece_rows, F32)], flags=mask_upper, addend=root_part,
-    )
-    root_terms = both_rows(add_all(own, swap_y(send)).astype(BF16))
-    root_right = (right_root.astype(F32) - root_terms).astype(BF16)
-
-    rows, inner = inverse_root.shape
-    piece = rows // 16
-    tile = tile_of(piece, inner)
-    send, own = multiply(
-        inverse_root, [root_right], one, spread(root_visit, piece, tile),
-        [(rows // 2, BF16), (rows // 2, F32)],
-    )
-    total = add_all(own, swap_core(send))
-    quarter_rows = rows // 4
-    totals = []
-    for d in zs:
-        kept = total[d * piece : (d + 1) * piece]
-        sent = total[quarter_rows + d * piece : quarter_rows + (d + 1) * piece]
-        totals.append(add_all(kept, swap_y(sent.astype(BF16))))
-    root_piece = add_all(
-        totals[0], *[swap_z(totals[d].astype(BF16), d) for d in (1, 2, 3)]
-    ).astype(BF16)
-
-    root_piece = root_piece.T
-    root_parts = [root_piece] + [swap_z(root_piece, d) for d in (1, 2, 3)]
-    root_parts = root_parts + [swap_y(p) for p in root_parts]
-    root_parts = root_parts + [swap_core(p) for p in root_parts]
-    inner, columns = inverse_root.shape
-    tile = tile_of(columns, inner)
-    (partial,) = multiply_back(
-        inverse_root, root_parts, root_blocks, jnp.arange(columns // tile, dtype=jnp.int32),
-        [(columns, BF16)],
-    )
-    root_solution = both_rows(partial).astype(BF16)
-    root_pieces = [root_solution, swap_y(root_solution)]
-
-    piece = panel_columns // 8
-    tile = tile_of(piece, panel_rows)
-    send, own = multiply_back(
-        half_to_root, root_pieces, high_blocks, spread(half_visit, piece, tile),
-        [(panel_columns // 2, BF16), (panel_columns // 2, F32)], flags=mask_upper,
-    )
-    total = add_all(own, swap_core(send))
-    sends = [total[:, d * piece : (d + 1) * piece].astype(BF16) for d in zs]
-    upper_total = add_all(total[:, :piece], *[swap_z(sends[d], d) for d in (1, 2, 3)])
-    update = (half_piece.T.astype(F32) - upper_total).astype(BF16)
-    update_parts = [update] + [swap_z(update, d) for d in (1, 2, 3)]
-    update_parts = update_parts + [swap_core(p) for p in update_parts]
+    in_turn = lambda columns: jnp.arange(columns // min(columns, 512), dtype=jnp.int32)
+
+    rows = inverse_quarter.shape[0]
+    held = fetch(inverse_quarter)
+    parts = [
+        multiply(
+            held, [x], one, col_visit, [(rows // 4, BF16)] * 2 + [(rows // 4, F32)] * 2
+        )
+        for x in right_quarter
+    ]
+    quarter_piece = [reduce_z(*p).astype(BF16) for p in parts]
+    held = fetch(quarter_to_half, quarter_piece[0])
+    quarter_parts = [gather_z(p) for p in quarter_piece]
+
+    parts = [
+        multiply(
+            held, x, col_blocks, low_visit, [(piece_rows, BF16), (piece_rows, F32)], flags=mask_half
+        )
+        for x in quarter_parts
+    ]
+    held_root = fetch(quarter_to_root, parts[0][0])
+    half_right = [
+        (r.astype(F32) - both_rows(add_all(own, swap_core(send)).astype(BF16))).astype(BF16)
+        for r, (send, own) in zip(right_half, parts)
+    ]
+    root_part = [
+        multiply(held_root, x, col_blocks, high_visit, [(panel_rows, F32)], flags=mask_root)[0]
+        for x in quarter_parts
+    ]
+
+    held = fetch(inverse_half, root_part[0])
+    rows = inverse_half.shape[0]
+    parts = [
+        multiply(held, [x], one, half_visit, [(rows // 2, BF16), (rows // 2, F32)])
+        for x in half_right
+    ]
+    half_piece = [reduce_core_z(send, own, 0).astype(BF16) for send, own in parts]
+    held = fetch(half_to_root, half_piece[0])
+    half_parts = [gather_z_core(p, 0) for p in half_piece]
+
+    parts = [
+        multiply(
+            held, x, half_blocks, high_visit, [(piece_rows, BF16), (piece_rows, F32)],
+            flags=mask_upper, addend=early,
+        )
+        for x, early in zip(half_parts, root_part)
+    ]
+    held_root = fetch(inverse_root, parts[0][0])
+    root_right = [
+        (r.astype(F32) - both_rows(add_all(own, swap_y(send)).astype(BF16))).astype(BF16)
+        for r, (send, own) in zip(right_root, parts)
+    ]
+
+    rows = inverse_root.shape[0]
+    parts = [
+        multiply(held_root, [x], one, root_visit, [(rows // 2, BF16), (rows // 2, F32)])
+        for x in root_right
+    ]
+
+    root_piece = [flip(reduce_core_y_z(send, own, 0).astype(BF16)) for send, own in parts]
+    held_root = fetch(inverse_root, root_piece[0])
+    root_parts = [gather_z_y_core(p, 1) for p in root_piece]
+    columns = inverse_root.shape[1]
+    parts = [
+        multiply_back(held_root, y, root_blocks, in_turn(columns), [(columns, BF16)])[0]
+        for y in root_parts
+    ]
+    held = fetch(half_to_root, parts[0])
+    root_solution = [both_rows(p).astype(BF16) for p in parts]
+    root_pieces = [[p, swap_y(p)] for p in root_solution]
+
+    parts = [
+        multiply_back(
+            held, y, high_blocks, half_visit,
+            [(panel_columns // 2, BF16), (panel_columns // 2, F32)], flags=mask_upper,
+        )
+        for y in root_pieces
+    ]
+    held_root = fetch(quarter_to_root, parts[0][0])
+    update = [
+        (flip(p).astype(F32) - reduce_core_z(send, own, 1)).astype(BF16)
+        for p, (send, own) in zip(half_piece, parts)
+    ]
+    update_parts = [gather_z_core(p, 1) for p in update]
+    quarter_back = [
+        multiply_back(held_root, y, high_blocks, col_visit, [(panel_columns, F32)], flags=mask_root)[0]
+        for y in root_pieces
+    ]
+
+    columns = inverse_half.shape[1]
+    held = fetch(inverse_half, quarter_back[0])
+    parts = [
+        multiply_back(held, y, half_blocks, in_turn(columns), [(columns, BF16)])[0]
+        for y in update_parts
+    ]
+    held_root = fetch(quarter_to_half, parts[0])
+    half_solution = [both_rows(p).astype(BF16) for p in parts]
+    half_pieces = [[p, swap_core(p)] for p in half_solution]
+
     piece = panel_columns // 4
-    tile = tile_of(piece, panel_rows)
-    (quarter_back,) = multiply_back(
-        quarter_to_root, root_pieces, high_blocks, spread(col_visit, piece, tile),
-        [(panel_columns, F32)], flags=mask_root,
-    )
-
-    inner, columns = inverse_half.shape
-    tile = tile_of(columns, inner)
-    (partial,) = multiply_back(
-        inverse_half, update_parts, half_blocks, jnp.arange(columns // tile, dtype=jnp.int32),
-        [(columns, BF16)],
-    )
-    half_solution = both_rows(partial).astype(BF16)
-    half_pieces = [half_solution, swap_core(half_solution)]
-
-    tile = tile_of(piece, panel_rows)
-    *sends, own = multiply_back(
-        quarter_to_half, half_pieces, low_blocks, spread(col_visit, piece, tile),
-        [(piece, BF16)] * 3 + [(piece, F32)], flags=mask_half, addend=quarter_back,
-    )
-    quarter_total = add_all(own, *[swap_z(s, d) for s, d in zip(sends, (1, 2, 3))])
-    update = (quarter_piece.T.astype(F32) - quarter_total).astype(BF16)
-    update_parts = [update] + [swap_z(update, d) for d in (1, 2, 3)]
-    inner, columns = inverse_quarter.shape
-    tile = tile_of(columns, inner)
-    own, send = multiply_back(
-        inverse_quarter, update_parts, col_blocks, jnp.arange(columns // tile, dtype=jnp.int32),
-        [], side=lax.axis_index("row"),
-    )
-    return own + swap_x(send).astype(F32), half_solution.T, root_solution.T
+    parts = [
+        multiply_back(
+            held_root, y, low_blocks, col_visit, [(piece, BF16)] * 2 + [(piece, F32)] * 2,
+            flags=mask_half, addend=early,
+        )
+        for y, early in zip(half_pieces, quarter_back)
+    ]
+    update = [
+        (flip(q).astype(F32) - reduce_z(*p)).astype(BF16) for q, p in zip(quarter_piece, parts)
+    ]
+    held = fetch(inverse_quarter, update[0])
+    columns = inverse_quarter.shape[1]
+    quarter = [
+        multiply_back(held, gather_z(y), col_blocks, in_turn(columns), [(columns, F32)])[0]
+        for y in update
+    ]
+    return quarter, [flip(p) for p in half_solution], [flip(p) for p in root_solution]
 
 
 def pick(values, index):
@@ -573,12 +648,17 @@
         inverse_half[0],
         inverse_root,
         *panels,
-        right_quarter[0],
-        right_half[0],
-        right_root,
+        jnp.split(right_quarter[0], STREAMS, axis=1),
+        jnp.split(right_half[0], STREAMS, axis=1),
+        jnp.split(right_root, STREAMS, axis=1),
         row_flags.reshape(3, -1),
     )
-    return (quarter[None], half[None], root)
+    low_side, high_side = jnp.split(quarter[0], 2) if STREAMS == 1 else quarter
+    first = lax.axis_index("row") == 0
+    own = jnp.where(first, low_side, high_side)
+    send = jnp.where(first, high_side, low_side).astype(BF16)
+    quarter = (own + swap_x(send).astype(F32)).T
+    return (quarter[None], jnp.concatenate(half, axis=1)[None], jnp.concatenate(root, axis=1))
 
 
 def solution(mesh):

time: 668 us -> 539 us (0.81); the launches traced: 666 us -> 529 us
  waiting for transfers between devices: 380 us -> 175 us
  Pallas kernels: 131 us -> 197 us
  local copies, waits for them, and re-layouts: 45.9 us -> 18.1 us
  starting transfers between devices: 96.8 us -> 120 us
    ppermute x66 -> x107, waiting for transfers between devices: 380 us -> 175 us  [swap(): return lax.ppermute(values, axis, pairs)]
    pallas_call x0 -> x22, Pallas kernels: none -> 84.5 us  [the longest x12 64.7 us: fetch(): pl.pallas_call(body, in_specs=[pl.BlockSpec(memory_space=pltpu.HBM)] * le...]
    ppermute x66 -> x107, starting transfers between devices: 96.8 us -> 120 us  [swap(): return lax.ppermute(values, axis, pairs)]
    pallas_call x6 -> x12, Pallas kernels: 66 us -> 44.3 us  [multiply_back(): pl.pallas_call(body, grid_spec=pltpu.PrefetchScalarGridSpec(num_scalar_pr...]
    pallas_call x8 -> x0, local copies, waits for them, and re-layouts: 15.2 us -> none  [multiply(): pl.pallas_call(body, grid_spec=pltpu.PrefetchScalarGridSpec(num_scalar_pr...]
    ppermute x10 -> x0, local copies, waits for them, and re-layouts: 10.3 us -> none  [swap(): return lax.ppermute(values, axis, pairs)]
    pallas_call x6 -> x12, Pallas kernels: 64.5 us -> 68 us  [multiply(): pl.pallas_call(body, grid_spec=pltpu.PrefetchScalarGridSpec(num_scalar_pr...]
    unnamed x48 -> x51, local copies, waits for them, and re-layouts: 18.2 us -> 15.1 us
  transfers between devices with their start and end apart: 66 -> 107, of which waited for: 39 -> 49; matrix products, arithmetic and copies ran while one was open for 3% -> 3% of each run, Pallas kernels for 3% -> 32%
where the time goes in v3:
time: 539 us; the launch traced here: 529 us
  Pallas kernels  197 us (37%)
  waiting for transfers between devices  175 us (32%)
  starting transfers between devices  120 us (22%)
  local copies, waits for them, and re-layouts  18.1 us (3%)
  other arithmetic  16.8 us (3%)
    ppermute x107, waiting for transfers between devices, swap(): return lax.ppermute(values, axis, pairs)  175 us
    ppermute x107, starting transfers between devices, swap(): return lax.ppermute(values, axis, pairs)  120 us
    pallas_call x12, Pallas kernels, multiply(): pl.pallas_call(body, grid_spec=pltpu.PrefetchScalarGridSpec(num_scalar_pr...  68 us
    pallas_call x12, Pallas kernels, fetch(): pl.pallas_call(body, in_specs=[pl.BlockSpec(memory_space=pltpu.HBM)] * le...  64.7 us
    pallas_call x12, Pallas kernels, multiply_back(): pl.pallas_call(body, grid_spec=pltpu.PrefetchScalarGridSpec(num_scalar_pr...  44.3 us
    pallas_call x10, Pallas kernels, flip(): pl.pallas_call(body, grid=(rows // tile,), in_specs=[pl.BlockSpec((tile,...  19.8 us
    unnamed x51, local copies, waits for them, and re-layouts  15.1 us
  transfers between devices with their start and end apart: 107, of which 49 were waited for; matrix products, arithmetic and copies ran while one was open for 3% of the time, Pallas kernels for 32%

profile of v3, /device:TPU:0, one launch (start us, length us, event | category | flops | bytes accessed | tf_op | source)
XLA Modules:
  0.0 529.0 jit_solution(11440163797733204316)
XLA Ops:
  1.9 5.8 %fetch.12.refs_1_ = bf16[4096,2048]{1,0:T(8,128)(2,1)S(1)} custom-call(bf16[4096,2048]{1,0:T(8,128)(2,1)} %bitcast.51), custom_call_target="tpu_custom_call" | custom-call | bytes 33554432 | tf_op jit(solution)/shard_map/fetch/pallas_call | solution.py:44
  7.8 5.7 %multiply.18 = (bf16[1024,128]{1,0:T(8,128)(2,1)S(1)}, bf16[1024,128]{1,0:T(8,128)(2,1)S(1)}, f32[1024,128]{1,0:T(8,128)S(1)}, f32[1024,128]{1,0:T(8,128)S(1)}) custom-call(s32[1]{0:T(128)} %constant.42.clone.1.places.shown, s32[4]{0:T(128)S(1)} %pad_add_fusion.1.visit, s32[1]{0:T(128)} %constant.42.clone.1.places.shown, ...), custom_call_target="tpu_custom_call" | custom-call | flops 2147483648 | bytes 3145728 | tf_op jit(solution)/shard_map/multiply/pallas_call | solution.py:118
  16.6 5.7 %multiply.12 = (bf16[1024,128]{1,0:T(8,128)(2,1)S(1)}, bf16[1024,128]{1,0:T(8,128)(2,1)S(1)}, f32[1024,128]{1,0:T(8,128)S(1)}, f32[1024,128]{1,0:T(8,128)S(1)}) custom-call(s32[1]{0:T(128)} %constant.42.clone.1.places.shown, s32[4]{0:T(128)S(1)} %pad_add_fusion.1.visit, s32[1]{0:T(128)} %constant.42.clone.1.places.shown, ...), custom_call_target="tpu_custom_call" | custom-call | flops 2147483648 | bytes 3145728 | tf_op jit(solution)/shard_map/multiply/pallas_call | solution.py:118
  38.1 6.8 %collective-permute-done.55 = bf16[1024,128]{1,0:T(8,128)(2,1)S(1)} collective-permute-done((bf16[1024,128]{1,0:T(8,128)(2,1)S(1)}, bf16[1024,128]{1,0:T(8,128)(2,1)S(1)}, u32[]{:S(2)}, u32[]{:S(2)}) %collective-permute-start.55) | collective-permute-done | bytes 262176 | tf_op jit(solution)/shard_map/ppermute | solution.py:17
  47.0 9.3 %collective-permute-done.2 = bf16[1024,128]{1,0:T(8,128)(2,1)S(1)} collective-permute-done((bf16[1024,128]{1,0:T(8,128)(2,1)S(1)}, bf16[1024,128]{1,0:T(8,128)(2,1)S(1)}, u32[]{:S(2)}, u32[]{:S(2)}) %collective-permute-start.2) | collective-permute-done | bytes 262176 | tf_op jit(solution)/shard_map/ppermute | solution.py:17
  56.3 7.4 %collective-permute-start.4 = (bf16[1024,128]{1,0:T(8,128)(2,1)S(1)}, bf16[1024,128]{1,0:T(8,128)(2,1)S(1)}, u32[]{:S(2)}, u32[]{:S(2)}) collective-permute-start(bf16[1024,128]{1,0:T(8,128)(2,1)S(1)} %add_convert_fusion.12.in_ref.refs_1_.refs_0_), channel_id=1, source_target_pairs={{0,3},{1,2},{2,1},{3,0},{4,7},{5,6},{6,5},{7,4},{8,11},{9,10},{10,... | collective-permute-start | bytes 786440 | tf_op jit(solution)/shard_map/ppermute | solution.py:17
  73.1 5.8 %fetch.13.refs_4_ = bf16[2048,4096]{1,0:T(8,128)(2,1)S(1)} custom-call(bf16[2048,4096]{1,0:T(8,128)(2,1)} %bitcast.49, bf16[1024,128]{1,0:T(8,128)(2,1)S(1)} %add_convert_fusion.12.in_ref.refs_1_.refs_0_), custom_call_target="tpu_custom_call" | custom-call | bytes 33554432 | tf_op jit(solution)/shard_map/fetch/pallas_call | solution.py:44
  97.9 5.8 %fetch.14.refs_4_ = bf16[2048,4096]{1,0:T(8,128)(2,1)S(1)} custom-call(bf16[2048,4096]{1,0:T(8,128)(2,1)} %bitcast.47, bf16[1024,128]{1,0:T(8,128)(2,1)S(1)} %get-tuple-element.44.refs_1_), custom_call_target="tpu_custom_call" | custom-call | bytes 33554432 | tf_op jit(solution)/shard_map/fetch/pallas_call | solution.py:44
  163.5 5.8 %copy-done.1 = bf16[2048,4096]{1,0:T(8,128)(2,1)S(1)} copy-done((bf16[2048,4096]{1,0:T(8,128)(2,1)S(1)}, bf16[2048,4096]{1,0:T(8,128)(2,1)}, u32[]{:S(2)}) %copy-start.1) | copy-done | bytes 16777240
  174.9 5.8 %fetch.16.refs_4_ = bf16[2048,4096]{1,0:T(8,128)(2,1)S(1)} custom-call(bf16[2048,4096]{1,0:T(8,128)(2,1)} %bitcast.45, bf16[512,128]{1,0:T(8,128)(2,1)S(1)} %fusion.21.in_ref.refs_1_), custom_call_target="tpu_custom_call" | custom-call | bytes 33554432 | tf_op jit(solution)/shard_map/fetch/pallas_call | solution.py:44
  195.6 5.9 %collective-permute-done.17 = bf16[1024,128]{1,0:T(8,128)(2,1)S(1)} collective-permute-done((bf16[1024,128]{1,0:T(8,128)(2,1)S(1)}, bf16[1024,128]{1,0:T(8,128)(2,1)S(1)}, u32[]{:S(2)}, u32[]{:S(2)}) %collective-permute-start.17) | collective-permute-done | bytes 262176 | tf_op jit(solution)/shard_map/ppermute | solution.py:17
  202.4 5.8 %fetch.17.refs_1_ = bf16[8192,1024]{1,0:T(8,128)(2,1)S(1)} custom-call(bf16[8192,1024]{1,0:T(8,128)(2,1)} %refs_0_.3, bf16[1024,128]{1,0:T(8,128)(2,1)S(1)} %get-tuple-element.48.refs_1_), custom_call_target="tpu_custom_call" | custom-call | bytes 33554432 | tf_op jit(solution)/shard_map/fetch/pallas_call | solution.py:44
  209.5 7.9 %multiply.23 = (bf16[4096,128]{1,0:T(8,128)(2,1)S(1)}, f32[4096,128]{1,0:T(8,128)S(1)}) custom-call(s32[1]{0:T(128)} %constant.42.clone.1.places.shown, s32[16]{0:T(128)S(1)} %stack.199.visit, s32[1]{0:T(128)} %constant.42.clone.1.places.shown, bf16[1024,128]{1,0:T(8,128)(2,1)S(1)} %get-tuple-element.105.refs_0_, bf16[8192,1024]{1,0:T(8,128)(2,1)S(1)} %fetch.17.refs_1_), custom_call_target="tpu_custom_call" | custom-call | flops 2147483648 | bytes 4718592 | tf_op jit(solution)/shard_map/multiply/pallas_call | solution.py:118
  217.4 7.8 %multiply.17 = (bf16[4096,128]{1,0:T(8,128)(2,1)S(1)}, f32[4096,128]{1,0:T(8,128)S(1)}) custom-call(s32[1]{0:T(128)} %constant.42.clone.1.places.shown, s32[16]{0:T(128)S(1)} %stack.199.visit, s32[1]{0:T(128)} %constant.42.clone.1.places.shown, bf16[1024,128]{1,0:T(8,128)(2,1)S(1)} %get-tuple-element.104.refs_0_, bf16[8192,1024]{1,0:T(8,128)(2,1)S(1)} %fetch.17.refs_1_), custom_call_target="tpu_custom_call" | custom-call | flops 2147483648 | bytes 4718592 | tf_op jit(solution)/shard_map/multiply/pallas_call | solution.py:118
  284.9 6.3 %collective-permute-done.26 = bf16[128,512]{1,0:T(8,128)(2,1)S(1)} collective-permute-done((bf16[128,512]{1,0:T(8,128)(2,1)}, bf16[128,512]{1,0:T(8,128)(2,1)S(1)}, u32[]{:S(2)}, u32[]{:S(2)}) %collective-permute-start.26) | collective-permute-done | bytes 131104 | tf_op jit(solution)/shard_map/ppermute | solution.py:17
  292.2 5.8 %fetch.18.refs_8_ = bf16[8192,1024]{1,0:T(8,128)(2,1)S(1)} custom-call(bf16[8192,1024]{1,0:T(8,128)(2,1)} %refs_0_.3, bf16[128,512]{1,0:T(8,128)(2,1)S(1)} %copy-done.11), custom_call_target="tpu_custom_call" | custom-call | bytes 33554432 | tf_op jit(solution)/shard_map/fetch/pallas_call | solution.py:44
  319.0 5.8 %fetch.19.refs_2_ = bf16[2048,4096]{1,0:T(8,128)(2,1)S(1)} custom-call(bf16[2048,4096]{1,0:T(8,128)(2,1)} %bitcast.46, bf16[128,1024]{1,0:T(8,128)(2,1)S(1)} %multiply_back.12.refs_1_), custom_call_target="tpu_custom_call" | custom-call | bytes 33554432 | tf_op jit(solution)/shard_map/fetch/pallas_call | solution.py:44
  339.5 5.8 %copy-done.3 = bf16[2048,4096]{1,0:T(8,128)(2,1)S(1)} copy-done((bf16[2048,4096]{1,0:T(8,128)(2,1)S(1)}, bf16[2048,4096]{1,0:T(8,128)(2,1)}, u32[]{:S(2)}) %copy-start.3) | copy-done | bytes 16777240
  373.7 6.2 %collective-permute-start.40 = (bf16[128,512]{1,0:T(8,128)(2,1)S(1)}, bf16[128,512]{1,0:T(8,128)(2,1)S(1)}, u32[]{:S(2)}, u32[]{:S(2)}) collective-permute-start(bf16[128,512]{1,0:T(8,128)(2,1)S(1)} %fusion.15), channel_id=1, source_target_pairs={{0,1},{1,0},{2,3},{3,2},{4,5},{5,4},{6,7},{7,6},{8,9},{9,8},{10,11... | collective-permute-start | bytes 393224 | tf_op jit(solution)/shard_map/ppermute | solution.py:17
  379.9 5.8 %fetch.20.refs_2_ = bf16[2048,4096]{1,0:T(8,128)(2,1)S(1)} custom-call(bf16[2048,4096]{1,0:T(8,128)(2,1)} %bitcast.48, bf16[128,2048]{1,0:T(8,128)(2,1)S(1)} %get-tuple-element.52.refs_1_), custom_call_target="tpu_custom_call" | custom-call | bytes 33554432 | tf_op jit(solution)/shard_map/fetch/pallas_call | solution.py:44
  426.9 5.8 %fetch.22.refs_2_ = bf16[2048,4096]{1,0:T(8,128)(2,1)S(1)} custom-call(bf16[2048,4096]{1,0:T(8,128)(2,1)} %bitcast.50, bf16[128,1024]{1,0:T(8,128)(2,1)S(1)} %multiply_back.15.refs_1_), custom_call_target="tpu_custom_call" | custom-call | bytes 33554432 | tf_op jit(solution)/shard_map/fetch/pallas_call | solution.py:44
  468.1 6.2 %collective-permute-done.49 = bf16[128,1024]{1,0:T(8,128)(2,1)S(1)} collective-permute-done((bf16[128,1024]{1,0:T(8,128)(2,1)S(1)}, bf16[128,1024]{1,0:T(8,128)(2,1)S(1)}, u32[]{:S(2)}, u32[]{:S(2)}) %collective-permute-start.49) | collective-permute-done | bytes 262176 | tf_op jit(solution)/shard_map/ppermute | solution.py:17
  480.0 11.2 %collective-permute-start.105 = (bf16[128,1024]{1,0:T(8,128)(2,1)S(1)}, bf16[128,1024]{1,0:T(8,128)(2,1)S(1)}, u32[]{:S(2)}, u32[]{:S(2)}) collective-permute-start(bf16[128,1024]{1,0:T(8,128)(2,1)S(1)} %collective-permute-done.104.refs_3_), channel_id=1, source_target_pairs={{0,1},{1,0},{2,3},{3,2},{4,5},{5,4},{6,7},{7,6},{8,9},{9,8},{10,11... | collective-permute-start | bytes 786440 | tf_op jit(solution)/shard_map/ppermute | solution.py:17
  496.7 5.8 %fetch.23.refs_4_ = bf16[4096,2048]{1,0:T(8,128)(2,1)S(1)} custom-call(bf16[4096,2048]{1,0:T(8,128)(2,1)} %bitcast.52, bf16[128,1024]{1,0:T(8,128)(2,1)S(1)} %subtract_convert_fusion.3.refs_1_.refs_0_), custom_call_target="tpu_custom_call" | custom-call | bytes 33554432 | tf_op jit(solution)/shard_map/fetch/pallas_call | solution.py:44
  (369 shorter events, 370.7 us)
Async XLA Ops:
  24.4 20.5 %collective-permute-start.55 = (bf16[1024,128]{1,0:T(8,128)(2,1)S(1)}, bf16[1024,128]{1,0:T(8,128)(2,1)S(1)}, u32[]{:S(2)}, u32[]{:S(2)}) collective-permute-start(bf16[1024,128]{1,0:T(8,128)(2,1)S(1)} %add_convert_fusion.6), channel_id=1, source_target_pairs={{0,3},{1,2},{2,1},{3,0},{4,7},{5,6},{6,5},{7,4},{8,11},{9,10},{10,... | collective-permute-start | bytes 786440 | tf_op jit(solution)/shard_map/ppermute | solution.py:17
  27.0 20.0 %collective-permute-start = (bf16[1024,128]{1,0:T(8,128)(2,1)S(1)}, bf16[1024,128]{1,0:T(8,128)(2,1)S(1)}, u32[]{:S(2)}, u32[]{:S(2)}) collective-permute-start(bf16[1024,128]{1,0:T(8,128)(2,1)S(1)} %get-tuple-element.40), channel_id=1, source_target_pairs={{0,1},{1,0},{2,3},{3,2},{4,5},{5,4},{6,7},{7,6},{8,9},{9,8},{10,11... | collective-permute-start | bytes 786440 | tf_op jit(solution)/shard_map/ppermute | solution.py:17
  31.7 24.6 %collective-permute-start.2 = (bf16[1024,128]{1,0:T(8,128)(2,1)S(1)}, bf16[1024,128]{1,0:T(8,128)(2,1)S(1)}, u32[]{:S(2)}, u32[]{:S(2)}) collective-permute-start(bf16[1024,128]{1,0:T(8,128)(2,1)S(1)} %add_convert_fusion.13), channel_id=1, source_target_pairs={{0,3},{1,2},{2,1},{3,0},{4,7},{5,6},{6,5},{7,4},{8,11},{9,10},{10,... | collective-permute-start | bytes 786440 | tf_op jit(solution)/shard_map/ppermute | solution.py:17
  45.0 18.8 %collective-permute-start.57 = (bf16[1024,128]{1,0:T(8,128)(2,1)S(1)}, bf16[1024,128]{1,0:T(8,128)(2,1)S(1)}, u32[]{:S(2)}, u32[]{:S(2)}) collective-permute-start(bf16[1024,128]{1,0:T(8,128)(2,1)S(1)} %add_convert_fusion.5.in_ref.refs_0_), channel_id=1, source_target_pairs={{0,3},{1,2},{2,1},{3,0},{4,7},{5,6},{6,5},{7,4},{8,11},{9,10},{10,... | collective-permute-start | bytes 786440 | tf_op jit(solution)/shard_map/ppermute | solution.py:17
  66.8 19.1 %collective-permute-start.3 = (bf16[1024,128]{1,0:T(8,128)(2,1)S(1)}, bf16[1024,128]{1,0:T(8,128)(2,1)S(1)}, u32[]{:S(2)}, u32[]{:S(2)}) collective-permute-start(bf16[1024,128]{1,0:T(8,128)(2,1)S(1)} %add_convert_fusion.12.in_ref.refs_1_.refs_0_), channel_id=1, source_target_pairs={{0,1},{1,0},{2,3},{3,2},{4,5},{5,4},{6,7},{7,6},{8,9},{9,8},{10,11... | collective-permute-start | bytes 786440 | tf_op jit(solution)/shard_map/ppermute | solution.py:17
  71.0 17.5 %collective-permute-start.5 = (bf16[1024,128]{1,0:T(8,128)(2,1)S(1)}, bf16[1024,128]{1,0:T(8,128)(2,1)S(1)}, u32[]{:S(2)}, u32[]{:S(2)}) collective-permute-start(bf16[1024,128]{1,0:T(8,128)(2,1)S(1)} %collective-permute-done.4.refs_3_), channel_id=1, source_target_pairs={{0,1},{1,0},{2,3},{3,2},{4,5},{5,4},{6,7},{7,6},{8,9},{9,8},{10,11... | collective-permute-start | bytes 786440 | tf_op jit(solution)/shard_map/ppermute | solution.py:17
  94.0 18.9 %collective-permute-start.60 = (bf16[1024,128]{1,0:T(8,128)(2,1)S(1)}, bf16[1024,128]{1,0:T(8,128)(2,1)}, u32[]{:S(2)}, u32[]{:S(2)}) collective-permute-start(bf16[1024,128]{1,0:T(8,128)(2,1)S(1)} %add_convert_fusion.4), channel_id=1, source_target_pairs={{0,4},{4,0},{1,5},{5,1},{2,6},{6,2},{3,7},{7,3},{8,12},{12,8},{9,1... | collective-permute-start | bytes 786440 | tf_op jit(solution)/shard_map/ppermute | solution.py:17
  153.1 27.5 %collective-permute-start.68 = (bf16[1024,128]{1,0:T(8,128)(2,1)S(1)}, bf16[1024,128]{1,0:T(8,128)(2,1)S(1)}, u32[]{:S(2)}, u32[]{:S(2)}) collective-permute-start(bf16[1024,128]{1,0:T(8,128)(2,1)S(1)} %pad_maximum_fusion.4.refs_0_), channel_id=1, source_target_pairs={{0,8},{8,0},{16,24},{24,16},{1,9},{9,1},{17,25},{25,17},{2,10},{10... | collective-permute-start | bytes 786440 | tf_op jit(solution)/shard_map/ppermute | solution.py:17
  156.5 31.1 %collective-permute-start.15 = (bf16[1024,128]{1,0:T(8,128)(2,1)S(1)}, bf16[1024,128]{1,0:T(8,128)(2,1)S(1)}, u32[]{:S(2)}, u32[]{:S(2)}) collective-permute-start(bf16[1024,128]{1,0:T(8,128)(2,1)S(1)} %pad_maximum_fusion.1.refs_0_), channel_id=1, source_target_pairs={{0,8},{8,0},{16,24},{24,16},{1,9},{9,1},{17,25},{25,17},{2,10},{10... | collective-permute-start | bytes 786440 | tf_op jit(solution)/shard_map/ppermute | solution.py:17
  159.4 21.2 %collective-permute-start.69 = (bf16[1024,128]{1,0:T(8,128)(2,1)S(1)}, bf16[1024,128]{1,0:T(8,128)(2,1)S(1)}, u32[]{:S(2)}, u32[]{:S(2)}) collective-permute-start(bf16[1024,128]{1,0:T(8,128)(2,1)S(1)} %constant_dynamic-update-slice_fusion.6.refs_1_), channel_id=1, source_target_pairs={{0,8},{8,0},{16,24},{24,16},{1,9},{9,1},{17,25},{25,17},{2,10},{10... | collective-permute-start | bytes 786440 | tf_op jit(solution)/shard_map/ppermute | solution.py:17
  163.4 24.3 %collective-permute-start.16 = (bf16[1024,128]{1,0:T(8,128)(2,1)S(1)}, bf16[1024,128]{1,0:T(8,128)(2,1)S(1)}, u32[]{:S(2)}, u32[]{:S(2)}) collective-permute-start(bf16[1024,128]{1,0:T(8,128)(2,1)S(1)} %constant_dynamic-update-slice_fusion.refs_1_), channel_id=1, source_target_pairs={{0,8},{8,0},{16,24},{24,16},{1,9},{9,1},{17,25},{25,17},{2,10},{10... | collective-permute-start | bytes 786440 | tf_op jit(solution)/shard_map/ppermute | solution.py:17
  228.6 18.1 %collective-permute-start.21 = (bf16[1024,128]{1,0:T(8,128)(2,1)S(1)}, bf16[1024,128]{1,0:T(8,128)(2,1)S(1)}, u32[]{:S(2)}, u32[]{:S(2)}) collective-permute-start(bf16[1024,128]{1,0:T(8,128)(2,1)S(1)} %get-tuple-element.94), channel_id=1, source_target_pairs={{0,16},{8,24},{16,0},{24,8},{1,17},{9,25},{17,1},{25,9},{2,18},{10... | collective-permute-start | bytes 786440 | tf_op jit(solution)/shard_map/ppermute | solution.py:17
  229.4 21.9 %collective-permute-start.20 = (bf16[1024,128]{1,0:T(8,128)(2,1)S(1)}, bf16[1024,128]{1,0:T(8,128)(2,1)S(1)}, u32[]{:S(2)}, u32[]{:S(2)}) collective-permute-start(bf16[1024,128]{1,0:T(8,128)(2,1)S(1)} %get-tuple-element.95), channel_id=1, source_target_pairs={{0,16},{8,24},{16,0},{24,8},{1,17},{9,25},{17,1},{25,9},{2,18},{10... | collective-permute-start | bytes 786440 | tf_op jit(solution)/shard_map/ppermute | solution.py:17
  263.1 17.5 %collective-permute-start.22 = (bf16[512,128]{1,0:T(8,128)(2,1)S(1)}, bf16[512,128]{1,0:T(8,128)(2,1)S(1)}, u32[]{:S(2)}, u32[]{:S(2)}) collective-permute-start(bf16[512,128]{1,0:T(8,128)(2,1)S(1)} %get-tuple-element.112), channel_id=1, source_target_pairs={{0,1},{1,0},{2,3},{3,2},{4,5},{5,4},{6,7},{7,6},{8,9},{9,8},{10,11... | collective-permute-start | bytes 393224 | tf_op jit(solution)/shard_map/ppermute | solution.py:17
  278.3 20.2 %collective-permute-start.81 = (bf16[128,1024]{1,0:T(8,128)(2,1)S(1)}, bf16[128,1024]{1,0:T(8,128)(2,1)S(1)}, u32[]{:S(2)}, u32[]{:S(2)}) collective-permute-start(bf16[128,1024]{1,0:T(8,128)(2,1)S(1)} %pad_maximum_fusion.5.refs_0_), channel_id=1, source_target_pairs={{0,16},{8,24},{16,0},{24,8},{1,17},{9,25},{17,1},{25,9},{2,18},{10... | collective-permute-start | bytes 786440 | tf_op jit(solution)/shard_map/ppermute | solution.py:17
  279.2 19.5 %collective-permute-start.82 = (bf16[128,1024]{1,0:T(8,128)(2,1)S(1)}, bf16[128,1024]{1,0:T(8,128)(2,1)S(1)}, u32[]{:S(2)}, u32[]{:S(2)}) collective-permute-start(bf16[128,1024]{1,0:T(8,128)(2,1)S(1)} %constant_dynamic-update-slice_fusion.8.refs_1_), channel_id=1, source_target_pairs={{0,16},{8,24},{16,0},{24,8},{1,17},{9,25},{17,1},{25,9},{2,18},{10... | collective-permute-start | bytes 786440 | tf_op jit(solution)/shard_map/ppermute | solution.py:17
  330.6 19.6 %collective-permute-start.89 = (bf16[128,2048]{1,0:T(8,128)(2,1)S(1)}, bf16[128,2048]{1,0:T(8,128)(2,1)}, u32[]{:S(2)}, u32[]{:S(2)}) collective-permute-start(bf16[128,2048]{1,0:T(8,128)(2,1)S(1)} %get-tuple-element.70), channel_id=1, source_target_pairs={{0,8},{8,0},{16,24},{24,16},{1,9},{9,1},{17,25},{25,17},{2,10},{10... | collective-permute-start | bytes 1572872 | tf_op jit(solution)/shard_map/ppermute | solution.py:17
  353.9 18.8 %collective-permute-start.37 = (bf16[128,512]{1,0:T(8,128)(2,1)S(1)}, bf16[128,512]{1,0:T(8,128)(2,1)S(1)}, u32[]{:S(2)}, u32[]{:S(2)}) collective-permute-start(bf16[128,512]{1,0:T(8,128)(2,1)S(1)} %get-tuple-element.100), channel_id=1, source_target_pairs={{0,1},{1,0},{2,3},{3,2},{4,5},{5,4},{6,7},{7,6},{8,9},{9,8},{10,11... | collective-permute-start | bytes 393224 | tf_op jit(solution)/shard_map/ppermute | solution.py:17
  387.6 18.6 %collective-permute-start.96 = (bf16[128,1024]{1,0:T(8,128)(2,1)S(1)}, bf16[128,1024]{1,0:T(8,128)(2,1)S(1)}, u32[]{:S(2)}, u32[]{:S(2)}) collective-permute-start(bf16[128,1024]{1,0:T(8,128)(2,1)S(1)} %pad_maximum_fusion.6.refs_0_), channel_id=1, source_target_pairs={{0,8},{8,0},{16,24},{24,16},{1,9},{9,1},{17,25},{25,17},{2,10},{10... | collective-permute-start | bytes 786440 | tf_op jit(solution)/shard_map/ppermute | solution.py:17
  387.7 22.2 %collective-permute-start.43 = (bf16[128,1024]{1,0:T(8,128)(2,1)S(1)}, bf16[128,1024]{1,0:T(8,128)(2,1)S(1)}, u32[]{:S(2)}, u32[]{:S(2)}) collective-permute-start(bf16[128,1024]{1,0:T(8,128)(2,1)S(1)} %pad_maximum_fusion.3.refs_0_), channel_id=1, source_target_pairs={{0,8},{8,0},{16,24},{24,16},{1,9},{9,1},{17,25},{25,17},{2,10},{10... | collective-permute-start | bytes 786440 | tf_op jit(solution)/shard_map/ppermute | solution.py:17
  454.7 19.6 %collective-permute-start.49 = (bf16[128,1024]{1,0:T(8,128)(2,1)S(1)}, bf16[128,1024]{1,0:T(8,128)(2,1)S(1)}, u32[]{:S(2)}, u32[]{:S(2)}) collective-permute-start(bf16[128,1024]{1,0:T(8,128)(2,1)S(1)} %add_convert_fusion.7), channel_id=1, source_target_pairs={{0,3},{1,2},{2,1},{3,0},{4,7},{5,6},{6,5},{7,4},{8,11},{9,10},{10,... | collective-permute-start | bytes 786440 | tf_op jit(solution)/shard_map/ppermute | solution.py:17
  477.4 25.1 %collective-permute-start.103 = (bf16[128,1024]{1,0:T(8,128)(2,1)S(1)}, bf16[128,1024]{1,0:T(8,128)(2,1)S(1)}, u32[]{:S(2)}, u32[]{:S(2)}) collective-permute-start(bf16[128,1024]{1,0:T(8,128)(2,1)S(1)} %subtract_convert_fusion.refs_0_), channel_id=1, source_target_pairs={{0,1},{1,0},{2,3},{3,2},{4,5},{5,4},{6,7},{7,6},{8,9},{9,8},{10,11... | collective-permute-start | bytes 786440 | tf_op jit(solution)/shard_map/ppermute | solution.py:17
  480.0 22.5 %collective-permute-start.105 = (bf16[128,1024]{1,0:T(8,128)(2,1)S(1)}, bf16[128,1024]{1,0:T(8,128)(2,1)S(1)}, u32[]{:S(2)}, u32[]{:S(2)}) collective-permute-start(bf16[128,1024]{1,0:T(8,128)(2,1)S(1)} %collective-permute-done.104.refs_3_), channel_id=1, source_target_pairs={{0,1},{1,0},{2,3},{3,2},{4,5},{5,4},{6,7},{7,6},{8,9},{9,8},{10,11... | collective-permute-start | bytes 786440 | tf_op jit(solution)/shard_map/ppermute | solution.py:17
  491.2 17.6 %collective-permute-start.52 = (bf16[128,1024]{1,0:T(8,128)(2,1)S(1)}, bf16[128,1024]{1,0:T(8,128)(2,1)S(1)}, u32[]{:S(2)}, u32[]{:S(2)}) collective-permute-start(bf16[128,1024]{1,0:T(8,128)(2,1)S(1)} %collective-permute-done.51.refs_3_), channel_id=1, source_target_pairs={{0,1},{1,0},{2,3},{3,2},{4,5},{5,4},{6,7},{7,6},{8,9},{9,8},{10,11... | collective-permute-start | bytes 786440 | tf_op jit(solution)/shard_map/ppermute | solution.py:17
  (105 other events, 1413.2 us)

commit v4 on v3

--- a/solution.py
+++ b/solution.py
@@ -33,26 +33,45 @@
     return swap(values, "row", 1)
 
 
-def fetch(matrix, after=None):
+def fetch(matrix, *after, pieces=None, size=None):
+    count = 1 if pieces is None else pieces.shape[0]
+    rows = matrix.shape[0] if pieces is None else count * size
+
     def body(*refs):
-        copy = pltpu.make_async_copy(refs[0], refs[-2], refs[-1])
-        copy.start()
-        copy.wait()
-
-    matrix = pltpu.with_memory_space_constraint(matrix, pltpu.HBM)
-    operands = [matrix] if after is None else [matrix, after]
+        source, target, sems = refs[1], refs[-2], refs[-1]
+        if pieces is None:
+            copies = [pltpu.make_async_copy(source, target, sems.at[0])]
+        else:
+            copies = [
+                pltpu.make_async_copy(
+                    source.at[pl.ds(pl.multiple_of(refs[0][i] * size, size), size), :],
+                    target.at[pl.ds(i * size, size), :],
+                    sems.at[i],
+                )
+                for i in range(count)
+            ]
+        for copy in copies:
+            copy.start()
+        for copy in copies:
+            copy.wait()
+
+    operands = [pltpu.with_memory_space_constraint(matrix, pltpu.HBM), *after]
     return pl.pallas_call(
         body,
-        in_specs=[pl.BlockSpec(memory_space=pltpu.HBM)] * len(operands),
-        out_specs=pl.BlockSpec(memory_space=pltpu.VMEM),
-        out_shape=jax.ShapeDtypeStruct(matrix.shape, matrix.dtype),
-        scratch_shapes=[pltpu.SemaphoreType.DMA],
+        grid_spec=pltpu.PrefetchScalarGridSpec(
+            num_scalar_prefetch=1,
+            grid=(1,),
+            in_specs=[pl.BlockSpec(memory_space=pltpu.HBM)] * len(operands),
+            out_specs=pl.BlockSpec(memory_space=pltpu.VMEM),
+            scratch_shapes=[pltpu.SemaphoreType.DMA((count,))],
+        ),
+        out_shape=jax.ShapeDtypeStruct((rows, matrix.shape[1]), matrix.dtype),
         compiler_params=pltpu.CompilerParams(vmem_limit_bytes=1 << 20),
         cost_estimate=pl.CostEstimate(
-            flops=0, transcendentals=0, bytes_accessed=4 * matrix.size
+            flops=0, transcendentals=0, bytes_accessed=4 * rows * matrix.shape[1]
         ),
         name="fetch",
-    )(*operands)
+    )(jnp.zeros((1,), jnp.int32) if pieces is None else pieces, *operands)
 
 
 def multiply(matrix, vectors, in_blocks, order, outs, flags=None, addend=None):
@@ -220,20 +239,30 @@
     )(in_blocks, order, jnp.zeros((1,), jnp.int32) if flags is None else flags, *operands)
 
 
-def flip(values):
-    def body(in_ref, out_ref):
-        out_ref[...] = in_ref[...].T
-
-    rows, columns = values.shape
-    tile = min(rows, 256)
+def flip(*values):
+    count = len(values)
+    columns = values[0].shape[1]
+    tile = min(columns, 256)
+
+    def body(*refs):
+        at = 0
+        for ref in refs[:count]:
+            refs[-1][:, at : at + ref.shape[0]] = ref[...].T
+            at += ref.shape[0]
+
+    rows = sum(v.shape[0] for v in values)
     return pl.pallas_call(
         body,
-        grid=(rows // tile,),
-        in_specs=[pl.BlockSpec((tile, columns), lambda i: (i, 0))],
-        out_specs=pl.BlockSpec((columns, tile), lambda i: (0, i)),
-        out_shape=jax.ShapeDtypeStruct((columns, rows), values.dtype),
+        grid=(columns // tile,),
+        in_specs=[pl.BlockSpec((v.shape[0], tile), lambda i: (0, i)) for v in values],
+        out_specs=pl.BlockSpec((tile, rows), lambda i: (i, 0)),
+        out_shape=jax.ShapeDtypeStruct((columns, rows), values[0].dtype),
+        compiler_params=pltpu.CompilerParams(vmem_limit_bytes=4 << 20),
+        cost_estimate=pl.CostEstimate(
+            flops=0, transcendentals=0, bytes_accessed=4 * rows * columns
+        ),
         name="flip",
-    )(values)
+    )(*values)
 
 
 def listed(*values):
@@ -324,7 +353,7 @@
     mask_half, mask_root, mask_upper = row_flags[0], row_flags[1], row_flags[2]
     panel_rows, panel_columns = quarter_to_half.shape
     piece_rows = panel_rows // 2
-    panel_tile = min(piece_rows, 1024)
+    panel_tile = min(piece_rows, 512)
 
     col_blocks = listed(*[column ^ d for d in zs])
     col_visit = listed(*[column ^ d for d in visit_z])
@@ -341,12 +370,14 @@
     in_turn = lambda columns: jnp.arange(columns // min(columns, 512), dtype=jnp.int32)
 
     rows = inverse_quarter.shape[0]
-    held = fetch(inverse_quarter)
-    parts = [
-        multiply(
-            held, [x], one, col_visit, [(rows // 4, BF16)] * 2 + [(rows // 4, F32)] * 2
-        )
-        for x in right_quarter
+    piece = rows // 4
+    held = fetch(inverse_quarter, pieces=col_visit[:2], size=piece)
+    pair = jnp.arange(4, dtype=jnp.int32)
+    sends = [multiply(held, [x], one, pair, [(piece, BF16)] * 2) for x in right_quarter]
+    held = fetch(inverse_quarter, sends[-1][0], pieces=col_visit[2:], size=piece)
+    parts = [
+        send + multiply(held, [x], one, pair, [(piece, F32)] * 2)
+        for x, send in zip(right_quarter, sends)
     ]
     quarter_piece = [reduce_z(*p).astype(BF16) for p in parts]
     held = fetch(quarter_to_half, quarter_piece[0])
@@ -358,24 +389,23 @@
         )
         for x in quarter_parts
     ]
-    held_root = fetch(quarter_to_root, parts[0][0])
+    held = fetch(inverse_half, parts[0][0])
     half_right = [
         (r.astype(F32) - both_rows(add_all(own, swap_core(send)).astype(BF16))).astype(BF16)
         for r, (send, own) in zip(right_half, parts)
     ]
+    rows = inverse_half.shape[0]
+    parts = [
+        multiply(held, [x], one, half_visit, [(rows // 2, BF16), (rows // 2, F32)])
+        for x in half_right
+    ]
+    held_root = fetch(quarter_to_root, parts[-1][0])
     root_part = [
         multiply(held_root, x, col_blocks, high_visit, [(panel_rows, F32)], flags=mask_root)[0]
         for x in quarter_parts
     ]
-
-    held = fetch(inverse_half, root_part[0])
-    rows = inverse_half.shape[0]
-    parts = [
-        multiply(held, [x], one, half_visit, [(rows // 2, BF16), (rows // 2, F32)])
-        for x in half_right
-    ]
     half_piece = [reduce_core_z(send, own, 0).astype(BF16) for send, own in parts]
-    held = fetch(half_to_root, half_piece[0])
+    held = fetch(half_to_root, half_piece[0], root_part[-1])
     half_parts = [gather_z_core(p, 0) for p in half_piece]
 
     parts = [
@@ -417,9 +447,12 @@
         for y in root_pieces
     ]
     held_root = fetch(quarter_to_root, parts[0][0])
+    root_out, *flipped = lax.optimization_barrier(
+        (flip(*root_solution), *[flip(p) for p in half_piece])
+    )
     update = [
-        (flip(p).astype(F32) - reduce_core_z(send, own, 1)).astype(BF16)
-        for p, (send, own) in zip(half_piece, parts)
+        (p.astype(F32) - reduce_core_z(send, own, 1)).astype(BF16)
+        for p, (send, own) in zip(flipped, parts)
     ]
     update_parts = [gather_z_core(p, 1) for p in update]
     quarter_back = [
@@ -445,8 +478,11 @@
         )
         for y, early in zip(half_pieces, quarter_back)
     ]
+    half_out, *flipped = lax.optimization_barrier(
+        (flip(*half_solution), *[flip(q) for q in quarter_piece])
+    )
     update = [
-        (flip(q).astype(F32) - reduce_z(*p)).astype(BF16) for q, p in zip(quarter_piece, parts)
+        (q.astype(F32) - reduce_z(*p)).astype(BF16) for q, p in zip(flipped, parts)
     ]
     held = fetch(inverse_quarter, update[0])
     columns = inverse_quarter.shape[1]
@@ -454,7 +490,7 @@
         multiply_back(held, gather_z(y), col_blocks, in_turn(columns), [(columns, F32)])[0]
         for y in update
     ]
-    return quarter, [flip(p) for p in half_solution], [flip(p) for p in root_solution]
+    return quarter, half_out, root_out
 
 
 def pick(values, index):
@@ -658,7 +694,7 @@
     own = jnp.where(first, low_side, high_side)
     send = jnp.where(first, high_side, low_side).astype(BF16)
     quarter = (own + swap_x(send).astype(F32)).T
-    return (quarter[None], jnp.concatenate(half, axis=1)[None], jnp.concatenate(root, axis=1))
+    return (quarter[None], half[None], root)
 
 
 def solution(mesh):

time: 539 us -> 528 us (0.980); the launches traced: 529 us -> 527 us
  starting transfers between devices: 120 us -> 139 us
  other arithmetic: 16.8 us -> 7.62 us
  Pallas kernels: 197 us -> 189 us
  local copies, waits for them, and re-layouts: 18.1 us -> 12.4 us
    ppermute x107, starting transfers between devices: 120 us -> 139 us  [swap(): return lax.ppermute(values, axis, pairs)]
    pallas_call x22 -> x21, Pallas kernels: 84.5 us -> 70.9 us  [the longest x13 67 us: fetch(): pl.pallas_call(body, grid_spec=pltpu.PrefetchScalarGridSpec(num_scalar_pr...]
    unnamed x51 -> x23, local copies, waits for them, and re-layouts: 15.1 us -> 8.19 us
    pallas_call x12 -> x14, Pallas kernels: 68 us -> 73.8 us  [multiply(): pl.pallas_call(body, grid_spec=pltpu.PrefetchScalarGridSpec(num_scalar_pr...]
  transfers between devices with their start and end apart: 107 -> 107, of which waited for: 49 -> 47; matrix products, arithmetic and copies ran while one was open for 3% -> 2% of each run, Pallas kernels for 32% -> 31%
where the time goes in v4:
time: 528 us; the launch traced here: 527 us
  Pallas kernels  189 us (36%)
  waiting for transfers between devices  177 us (34%)
  starting transfers between devices  139 us (26%)
  local copies, waits for them, and re-layouts  12.4 us (2%)
  other arithmetic  7.62 us (1%)
    ppermute x107, waiting for transfers between devices, swap(): return lax.ppermute(values, axis, pairs)  177 us
    ppermute x107, starting transfers between devices, swap(): return lax.ppermute(values, axis, pairs)  139 us
    pallas_call x14, Pallas kernels, multiply(): pl.pallas_call(body, grid_spec=pltpu.PrefetchScalarGridSpec(num_scalar_pr...  73.8 us
    pallas_call x13, Pallas kernels, fetch(): pl.pallas_call(body, grid_spec=pltpu.PrefetchScalarGridSpec(num_scalar_pr...  67 us
    pallas_call x12, Pallas kernels, multiply_back(): pl.pallas_call(body, grid_spec=pltpu.PrefetchScalarGridSpec(num_scalar_pr...  44.6 us
  transfers between devices with their start and end apart: 107, of which 47 were waited for; matrix products, arithmetic and copies ran while one was open for 2% of the time, Pallas kernels for 31%

profile of v4, /device:TPU:0, one launch (start us, length us, event | category | flops | bytes accessed | tf_op | source)
XLA Modules:
  0.0 527.3 jit_solution(10345001527603155426)
XLA Ops:
  36.1 8.3 %collective-permute-done.19 = bf16[1024,128]{1,0:T(8,128)(2,1)S(1)} collective-permute-done((bf16[1024,128]{1,0:T(8,128)(2,1)}, bf16[1024,128]{1,0:T(8,128)(2,1)S(1)}, u32[]{:S(2)}, u32[]{:S(2)}) %collective-permute-start.19) | collective-permute-done | bytes 262176 | tf_op jit(solution)/shard_map/ppermute | solution.py:17
  44.5 9.2 %collective-permute-start.21 = (bf16[1024,128]{1,0:T(8,128)(2,1)S(1)}, bf16[1024,128]{1,0:T(8,128)(2,1)S(1)}, u32[]{:S(2)}, u32[]{:S(2)}) collective-permute-start(bf16[1024,128]{1,0:T(8,128)(2,1)S(1)} %add_convert_fusion.9.refs_0_), channel_id=1, source_target_pairs={{0,3},{1,2},{2,1},{3,0},{4,7},{5,6},{6,5},{7,4},{8,11},{9,10},{10,... | collective-permute-start | bytes 786440 | tf_op jit(solution)/shard_map/ppermute | solution.py:17
  54.0 6.7 %collective-permute-done.21.refs_3_ = bf16[1024,128]{1,0:T(8,128)(2,1)S(1)} collective-permute-done((bf16[1024,128]{1,0:T(8,128)(2,1)S(1)}, bf16[1024,128]{1,0:T(8,128)(2,1)S(1)}, u32[]{:S(2)}, u32[]{:S(2)}) %collective-permute-start.21) | collective-permute-done | bytes 262176 | tf_op jit(solution)/shard_map/ppermute | solution.py:17
  60.7 10.3 %collective-permute-start.22 = (bf16[1024,128]{1,0:T(8,128)(2,1)S(1)}, bf16[1024,128]{1,0:T(8,128)(2,1)S(1)}, u32[]{:S(2)}, u32[]{:S(2)}) collective-permute-start(bf16[1024,128]{1,0:T(8,128)(2,1)S(1)} %collective-permute-done.21.refs_3_), channel_id=1, source_target_pairs={{0,1},{1,0},{2,3},{3,2},{4,5},{5,4},{6,7},{7,6},{8,9},{9,8},{10,11... | collective-permute-start | bytes 786440 | tf_op jit(solution)/shard_map/ppermute | solution.py:17
  75.1 5.8 %fetch.15.refs_4_ = bf16[2048,4096]{1,0:T(8,128)(2,1)S(1)} custom-call(s32[1]{0:T(128)} %constant.43.clone.1.places.shown.refs_0_, bf16[2048,4096]{1,0:T(8,128)(2,1)} %bitcast.51, bf16[1024,128]{1,0:T(8,128)(2,1)S(1)} %add_convert_fusion.12.refs_2_.refs_0_), custom_call_target="tpu_custom_call" | custom-call | bytes 33554432 | tf_op jit(solution)/shard_map/fetch/pallas_call | solution.py:59
  80.9 5.8 %multiply.20 = (bf16[1024,128]{1,0:T(8,128)(2,1)S(1)}, f32[1024,128]{1,0:T(8,128)S(1)}) custom-call(s32[4]{0:T(128)S(1)} %pad_add_fusion.places, s32[4]{0:T(128)S(1)} %add.378.visit, s32[8]{0:T(128)S(1)} %squeeze.23.shown, bf16[1024,128]{1,0:T(8,128)(2,1)S(1)} %add_convert_fusion.9.refs_0_, bf16[1024,128]{1,0:T(8,128)(2,1)S(1)} %collective-permute-done.20.refs_1_, ...), custom_call_target="tpu_custom_call" | custom-call | flops 2147483648 | bytes 3145728 | tf_op jit(solution)/shard_map/multiply/pallas_call | solution.py:137
  86.8 5.8 %multiply.17 = (bf16[1024,128]{1,0:T(8,128)(2,1)S(1)}, f32[1024,128]{1,0:T(8,128)S(1)}) custom-call(s32[4]{0:T(128)S(1)} %pad_add_fusion.places, s32[4]{0:T(128)S(1)} %add.378.visit, s32[8]{0:T(128)S(1)} %squeeze.23.shown, bf16[1024,128]{1,0:T(8,128)(2,1)S(1)} %add_convert_fusion.12.refs_2_.refs_0_, bf16[1024,128]{1,0:T(8,128)(2,1)S(1)} %collective-permute-done.3.refs_1_, ...), custom_call_target="tpu_custom_call" | custom-call | flops 2147483648 | bytes 3145728 | tf_op jit(solution)/shard_map/multiply/pallas_call | solution.py:137
  171.8 5.8 %fetch.18.refs_4_ = bf16[2048,4096]{1,0:T(8,128)(2,1)S(1)} custom-call(s32[1]{0:T(128)} %constant.43.clone.1.places.shown.refs_0_, bf16[2048,4096]{1,0:T(8,128)(2,1)} %bitcast.47, bf16[512,128]{1,0:T(8,128)(2,1)S(1)} %fusion.21.refs_2_.refs_0_, f32[2048,128]{1,0:T(8,128)S(1)} %multiply.22.refs_3_.refs_5_), custom_call_target="tpu_custom_call" | custom-call | bytes 33554432 | tf_op jit(solution)/shard_map/fetch/pallas_call | solution.py:59
  184.0 5.8 %multiply.26 = (bf16[1024,128]{1,0:T(8,128)(2,1)S(1)}, f32[1024,128]{1,0:T(8,128)S(1)}) custom-call(s32[8]{0:T(128)S(1)} %stack.175.places, s32[4]{0:T(128)S(1)} %copy-done.5, s32[8]{0:T(128)S(1)} %copy-done.4, bf16[1024,128]{1,0:T(8,128)(2,1)S(1)} %pad_maximum_fusion.2.refs_0_, bf16[1024,128]{1,0:T(8,128)(2,1)S(1)} %constant_dynamic-update-slice_fusion.4.refs_1_, ...), custom_call_target="tpu_custom_call" | custom-call | flops 2147483648 | bytes 3145728 | tf_op jit(solution)/shard_map/multiply/pallas_call | solution.py:137
  197.2 6.0 %multiply.24 = (bf16[1024,128]{1,0:T(8,128)(2,1)S(1)}, f32[1024,128]{1,0:T(8,128)S(1)}) custom-call(s32[8]{0:T(128)S(1)} %stack.175.places, s32[4]{0:T(128)S(1)} %copy-done.5, s32[8]{0:T(128)S(1)} %copy-done.4, bf16[1024,128]{1,0:T(8,128)(2,1)S(1)} %pad_maximum_fusion.refs_0_, bf16[1024,128]{1,0:T(8,128)(2,1)S(1)} %constant_dynamic-update-slice_fusion.refs_1_, ...), custom_call_target="tpu_custom_call" | custom-call | flops 2147483648 | bytes 3145728 | tf_op jit(solution)/shard_map/multiply/pallas_call | solution.py:137
  205.3 6.3 %collective-permute-done.25 = bf16[1024,128]{1,0:T(8,128)(2,1)S(1)} collective-permute-done((bf16[1024,128]{1,0:T(8,128)(2,1)S(1)}, bf16[1024,128]{1,0:T(8,128)(2,1)S(1)}, u32[]{:S(2)}, u32[]{:S(2)}) %collective-permute-start.25) | collective-permute-done | bytes 262176 | tf_op jit(solution)/shard_map/ppermute | solution.py:17
  213.4 5.8 %fetch.19.refs_1_ = bf16[8192,1024]{1,0:T(8,128)(2,1)S(1)} custom-call(s32[1]{0:T(128)} %constant.43.clone.1.places.shown.refs_0_, bf16[8192,1024]{1,0:T(8,128)(2,1)} %refs_1_.3, bf16[1024,128]{1,0:T(8,128)(2,1)S(1)} %get-tuple-element.61.refs_2_), custom_call_target="tpu_custom_call" | custom-call | bytes 33554432 | tf_op jit(solution)/shard_map/fetch/pallas_call | solution.py:59
  219.6 7.8 %multiply.27 = (bf16[4096,128]{1,0:T(8,128)(2,1)S(1)}, f32[4096,128]{1,0:T(8,128)S(1)}) custom-call(s32[1]{0:T(128)} %constant.43.clone.1.places.shown.refs_0_, s32[16]{0:T(128)S(1)} %stack.193.visit, s32[1]{0:T(128)} %constant.43.clone.1.places.shown.refs_0_, bf16[1024,128]{1,0:T(8,128)(2,1)S(1)} %get-tuple-element.117.refs_0_, ...), custom_call_target="tpu_custom_call" | custom-call | flops 2147483648 | bytes 4718592 | tf_op jit(solution)/shard_map/multiply/pallas_call | solution.py:137
  227.5 7.8 %multiply.25 = (bf16[4096,128]{1,0:T(8,128)(2,1)S(1)}, f32[4096,128]{1,0:T(8,128)S(1)}) custom-call(s32[1]{0:T(128)} %constant.43.clone.1.places.shown.refs_0_, s32[16]{0:T(128)S(1)} %stack.193.visit, s32[1]{0:T(128)} %constant.43.clone.1.places.shown.refs_0_, bf16[1024,128]{1,0:T(8,128)(2,1)S(1)} %get-tuple-element.116.refs_0_, ...), custom_call_target="tpu_custom_call" | custom-call | flops 2147483648 | bytes 4718592 | tf_op jit(solution)/shard_map/multiply/pallas_call | solution.py:137
  290.9 5.9 %collective-permute-done.34 = bf16[128,512]{1,0:T(8,128)(2,1)S(1)} collective-permute-done((bf16[128,512]{1,0:T(8,128)(2,1)S(1)}, bf16[128,512]{1,0:T(8,128)(2,1)S(1)}, u32[]{:S(2)}, u32[]{:S(2)}) %collective-permute-start.34) | collective-permute-done | bytes 131104 | tf_op jit(solution)/shard_map/ppermute | solution.py:17
  296.9 5.8 %fetch.20.refs_8_ = bf16[8192,1024]{1,0:T(8,128)(2,1)S(1)} custom-call(s32[1]{0:T(128)} %constant.43.clone.1.places.shown.refs_0_, bf16[8192,1024]{1,0:T(8,128)(2,1)} %refs_1_.3, bf16[128,512]{1,0:T(8,128)(2,1)S(1)} %flip.8.refs_2_), custom_call_target="tpu_custom_call" | custom-call | bytes 33554432 | tf_op jit(solution)/shard_map/fetch/pallas_call | solution.py:59
  337.9 6.1 %collective-permute-done.70.refs_1_ = bf16[128,1024]{1,0:T(8,128)(2,1)S(1)} collective-permute-done((bf16[128,1024]{1,0:T(8,128)(2,1)S(1)}, bf16[128,1024]{1,0:T(8,128)(2,1)S(1)}, u32[]{:S(2)}, u32[]{:S(2)}) %collective-permute-start.70) | collective-permute-done | bytes 262176 | tf_op jit(solution)/shard_map/ppermute | solution.py:17
  371.6 6.3 %collective-permute-start.75 = (bf16[128,512]{1,0:T(8,128)(2,1)S(1)}, bf16[128,512]{1,0:T(8,128)(2,1)S(1)}, u32[]{:S(2)}, u32[]{:S(2)}) collective-permute-start(bf16[128,512]{1,0:T(8,128)(2,1)S(1)} %fusion.9), channel_id=1, source_target_pairs={{0,1},{1,0},{2,3},{3,2},{4,5},{5,4},{6,7},{7,6},{8,9},{9,8},{10,11... | collective-permute-start | bytes 393224 | tf_op jit(solution)/shard_map/ppermute | solution.py:17
  423.8 5.8 %fetch.24.refs_2_ = bf16[2048,4096]{1,0:T(8,128)(2,1)S(1)} custom-call(s32[1]{0:T(128)} %constant.43.clone.1.places.shown.refs_0_, bf16[2048,4096]{1,0:T(8,128)(2,1)} %bitcast.52, bf16[128,1024]{1,0:T(8,128)(2,1)S(1)} %multiply_back.16.refs_2_), custom_call_target="tpu_custom_call" | custom-call | bytes 33554432 | tf_op jit(solution)/shard_map/fetch/pallas_call | solution.py:59
  454.0 7.0 %collective-permute-done.102 = bf16[128,1024]{1,0:T(8,128)(2,1)S(1)} collective-permute-done((bf16[128,1024]{1,0:T(8,128)(2,1)S(1)}, bf16[128,1024]{1,0:T(8,128)(2,1)S(1)}, u32[]{:S(2)}, u32[]{:S(2)}) %collective-permute-start.102) | collective-permute-done | bytes 262176 | tf_op jit(solution)/shard_map/ppermute | solution.py:17
  464.8 7.5 %collective-permute-done.95 = bf16[128,1024]{1,0:T(8,128)(2,1)S(1)} collective-permute-done((bf16[128,1024]{1,0:T(8,128)(2,1)S(1)}, bf16[128,1024]{1,0:T(8,128)(2,1)S(1)}, u32[]{:S(2)}, u32[]{:S(2)}) %collective-permute-start.95) | collective-permute-done | bytes 262176 | tf_op jit(solution)/shard_map/ppermute | solution.py:17
  472.5 6.7 %collective-permute-start.97 = (bf16[128,1024]{1,0:T(8,128)(2,1)S(1)}, bf16[128,1024]{1,0:T(8,128)(2,1)S(1)}, u32[]{:S(2)}, u32[]{:S(2)}) collective-permute-start(bf16[128,1024]{1,0:T(8,128)(2,1)S(1)} %subtract_convert_fusion.1.refs_2_.refs_0_), channel_id=1, source_target_pairs={{0,3},{1,2},{2,1},{3,0},{4,7},{5,6},{6,5},{7,4},{8,11},{9,10},{10,... | collective-permute-start | bytes 786440 | tf_op jit(solution)/shard_map/ppermute | solution.py:17
  479.2 6.4 %collective-permute-start.105 = (bf16[128,1024]{1,0:T(8,128)(2,1)S(1)}, bf16[128,1024]{1,0:T(8,128)(2,1)S(1)}, u32[]{:S(2)}, u32[]{:S(2)}) collective-permute-start(bf16[128,1024]{1,0:T(8,128)(2,1)S(1)} %collective-permute-done.104.refs_3_), channel_id=1, source_target_pairs={{0,1},{1,0},{2,3},{3,2},{4,5},{5,4},{6,7},{7,6},{8,9},{9,8},{10,11... | collective-permute-start | bytes 786440 | tf_op jit(solution)/shard_map/ppermute | solution.py:17
  512.4 13.4 %collective-permute-done.106 = bf16[128,2048]{1,0:T(8,128)(2,1)S(1)} collective-permute-done((bf16[128,2048]{1,0:T(8,128)(2,1)S(1)}, bf16[128,2048]{1,0:T(8,128)(2,1)S(1)}, u32[]{:S(2)}, u32[]{:S(2)}) %collective-permute-start.106) | collective-permute-done | bytes 524320 | tf_op jit(solution)/shard_map/ppermute | solution.py:17
  (349 shorter events, 357.3 us)
Async XLA Ops:
  16.0 37.8 %collective-permute-start = (bf16[1024,128]{1,0:T(8,128)(2,1)S(1)}, bf16[1024,128]{1,0:T(8,128)(2,1)S(1)}, u32[]{:S(2)}, u32[]{:S(2)}) collective-permute-start(bf16[1024,128]{1,0:T(8,128)(2,1)S(1)} %get-tuple-element.47), channel_id=1, source_target_pairs={{0,1},{1,0},{2,3},{3,2},{4,5},{5,4},{6,7},{7,6},{8,9},{9,8},{10,11... | collective-permute-start | bytes 786440 | tf_op jit(solution)/shard_map/ppermute | solution.py:17
  16.1 17.8 %collective-permute-start.1 = (bf16[1024,128]{1,0:T(8,128)(2,1)S(1)}, bf16[1024,128]{1,0:T(8,128)(2,1)S(1)}, u32[]{:S(2)}, u32[]{:S(2)}) collective-permute-start(bf16[1024,128]{1,0:T(8,128)(2,1)S(1)} %get-tuple-element.49), channel_id=1, source_target_pairs={{0,1},{1,0},{2,3},{3,2},{4,5},{5,4},{6,7},{7,6},{8,9},{9,8},{10,11... | collective-permute-start | bytes 786440 | tf_op jit(solution)/shard_map/ppermute | solution.py:17
  18.1 18.0 %collective-permute-start.17 = (bf16[1024,128]{1,0:T(8,128)(2,1)S(1)}, bf16[1024,128]{1,0:T(8,128)(2,1)S(1)}, u32[]{:S(2)}, u32[]{:S(2)}) collective-permute-start(bf16[1024,128]{1,0:T(8,128)(2,1)S(1)} %get-tuple-element.55), channel_id=1, source_target_pairs={{0,1},{1,0},{2,3},{3,2},{4,5},{5,4},{6,7},{7,6},{8,9},{9,8},{10,11... | collective-permute-start | bytes 786440 | tf_op jit(solution)/shard_map/ppermute | solution.py:17
  26.5 17.9 %collective-permute-start.19 = (bf16[1024,128]{1,0:T(8,128)(2,1)}, bf16[1024,128]{1,0:T(8,128)(2,1)S(1)}, u32[]{:S(2)}, u32[]{:S(2)}) collective-permute-start(bf16[1024,128]{1,0:T(8,128)(2,1)} %add_convert_fusion.10), channel_id=1, source_target_pairs={{0,3},{1,2},{2,1},{3,0},{4,7},{5,6},{6,5},{7,4},{8,11},{9,10},{10,... | collective-permute-start | bytes 786440 | tf_op jit(solution)/shard_map/ppermute | solution.py:17
  34.0 19.8 %collective-permute-start.2 = (bf16[1024,128]{1,0:T(8,128)(2,1)S(1)}, bf16[1024,128]{1,0:T(8,128)(2,1)S(1)}, u32[]{:S(2)}, u32[]{:S(2)}) collective-permute-start(bf16[1024,128]{1,0:T(8,128)(2,1)S(1)} %add_convert_fusion.13), channel_id=1, source_target_pairs={{0,3},{1,2},{2,1},{3,0},{4,7},{5,6},{6,5},{7,4},{8,11},{9,10},{10,... | collective-permute-start | bytes 786440 | tf_op jit(solution)/shard_map/ppermute | solution.py:17
  53.8 27.1 %collective-permute-start.20 = (bf16[1024,128]{1,0:T(8,128)(2,1)S(1)}, bf16[1024,128]{1,0:T(8,128)(2,1)S(1)}, u32[]{:S(2)}, u32[]{:S(2)}) collective-permute-start(bf16[1024,128]{1,0:T(8,128)(2,1)S(1)} %add_convert_fusion.9.refs_0_), channel_id=1, source_target_pairs={{0,1},{1,0},{2,3},{3,2},{4,5},{5,4},{6,7},{7,6},{8,9},{9,8},{10,11... | collective-permute-start | bytes 786440 | tf_op jit(solution)/shard_map/ppermute | solution.py:17
  53.9 17.9 %collective-permute-start.4 = (bf16[1024,128]{1,0:T(8,128)(2,1)S(1)}, bf16[1024,128]{1,0:T(8,128)(2,1)S(1)}, u32[]{:S(2)}, u32[]{:S(2)}) collective-permute-start(bf16[1024,128]{1,0:T(8,128)(2,1)S(1)} %add_convert_fusion.12.refs_2_.refs_0_), channel_id=1, source_target_pairs={{0,3},{1,2},{2,1},{3,0},{4,7},{5,6},{6,5},{7,4},{8,11},{9,10},{10,... | collective-permute-start | bytes 786440 | tf_op jit(solution)/shard_map/ppermute | solution.py:17
  60.7 20.2 %collective-permute-start.22 = (bf16[1024,128]{1,0:T(8,128)(2,1)S(1)}, bf16[1024,128]{1,0:T(8,128)(2,1)S(1)}, u32[]{:S(2)}, u32[]{:S(2)}) collective-permute-start(bf16[1024,128]{1,0:T(8,128)(2,1)S(1)} %collective-permute-done.21.refs_3_), channel_id=1, source_target_pairs={{0,1},{1,0},{2,3},{3,2},{4,5},{5,4},{6,7},{7,6},{8,9},{9,8},{10,11... | collective-permute-start | bytes 786440 | tf_op jit(solution)/shard_map/ppermute | solution.py:17
  134.5 21.6 %collective-permute-start.9 = (bf16[512,128]{1,0:T(8,128)(2,1)S(1)}, bf16[512,128]{1,0:T(8,128)(2,1)S(1)}, u32[]{:S(2)}, u32[]{:S(2)}) collective-permute-start(bf16[512,128]{1,0:T(8,128)(2,1)S(1)} %get-tuple-element.118), channel_id=1, source_target_pairs={{0,1},{1,0},{2,3},{3,2},{4,5},{5,4},{6,7},{7,6},{8,9},{9,8},{10,11... | collective-permute-start | bytes 393224 | tf_op jit(solution)/shard_map/ppermute | solution.py:17
  156.1 21.5 %collective-permute-start.47 = (bf16[512,128]{1,0:T(8,128)(2,1)S(1)}, bf16[512,128]{1,0:T(8,128)(2,1)S(1)}, u32[]{:S(2)}, u32[]{:S(2)}) collective-permute-start(bf16[512,128]{1,0:T(8,128)(2,1)S(1)} %fusion.15.refs_0_), channel_id=1, source_target_pairs={{0,1},{1,0},{2,3},{3,2},{4,5},{5,4},{6,7},{7,6},{8,9},{9,8},{10,11... | collective-permute-start | bytes 393224 | tf_op jit(solution)/shard_map/ppermute | solution.py:17
  156.1 21.5 %collective-permute-start.13 = (bf16[512,128]{1,0:T(8,128)(2,1)S(1)}, bf16[512,128]{1,0:T(8,128)(2,1)S(1)}, u32[]{:S(2)}, u32[]{:S(2)}) collective-permute-start(bf16[512,128]{1,0:T(8,128)(2,1)S(1)} %fusion.21.refs_2_.refs_0_), channel_id=1, source_target_pairs={{0,3},{1,2},{2,1},{3,0},{4,7},{5,6},{6,5},{7,4},{8,11},{9,10},{10,... | collective-permute-start | bytes 393224 | tf_op jit(solution)/shard_map/ppermute | solution.py:17
  161.1 18.7 %collective-permute-start.49 = (bf16[512,128]{1,0:T(8,128)(2,1)S(1)}, bf16[512,128]{1,0:T(8,128)(2,1)S(1)}, u32[]{:S(2)}, u32[]{:S(2)}) collective-permute-start(bf16[512,128]{1,0:T(8,128)(2,1)S(1)} %collective-permute-done.48), channel_id=1, source_target_pairs={{0,1},{1,0},{2,3},{3,2},{4,5},{5,4},{6,7},{7,6},{8,9},{9,8},{10,11... | collective-permute-start | bytes 393224 | tf_op jit(solution)/shard_map/ppermute | solution.py:17
  238.7 18.0 %collective-permute-start.29 = (bf16[1024,128]{1,0:T(8,128)(2,1)S(1)}, bf16[1024,128]{1,0:T(8,128)(2,1)S(1)}, u32[]{:S(2)}, u32[]{:S(2)}) collective-permute-start(bf16[1024,128]{1,0:T(8,128)(2,1)S(1)} %get-tuple-element.106), channel_id=1, source_target_pairs={{0,16},{8,24},{16,0},{24,8},{1,17},{9,25},{17,1},{25,9},{2,18},{10... | collective-permute-start | bytes 786440 | tf_op jit(solution)/shard_map/ppermute | solution.py:17
  239.3 22.1 %collective-permute-start.28 = (bf16[1024,128]{1,0:T(8,128)(2,1)S(1)}, bf16[1024,128]{1,0:T(8,128)(2,1)S(1)}, u32[]{:S(2)}, u32[]{:S(2)}) collective-permute-start(bf16[1024,128]{1,0:T(8,128)(2,1)S(1)} %get-tuple-element.107), channel_id=1, source_target_pairs={{0,16},{8,24},{16,0},{24,8},{1,17},{9,25},{17,1},{25,9},{2,18},{10... | collective-permute-start | bytes 786440 | tf_op jit(solution)/shard_map/ppermute | solution.py:17
  283.7 19.6 %collective-permute-start.63 = (bf16[128,1024]{1,0:T(8,128)(2,1)S(1)}, bf16[128,1024]{1,0:T(8,128)(2,1)S(1)}, u32[]{:S(2)}, u32[]{:S(2)}) collective-permute-start(bf16[128,1024]{1,0:T(8,128)(2,1)S(1)} %pad_maximum_fusion.3.refs_0_), channel_id=1, source_target_pairs={{0,16},{8,24},{16,0},{24,8},{1,17},{9,25},{17,1},{25,9},{2,18},{10... | collective-permute-start | bytes 786440 | tf_op jit(solution)/shard_map/ppermute | solution.py:17
  351.9 19.3 %collective-permute-start.72 = (bf16[128,512]{1,0:T(8,128)(2,1)S(1)}, bf16[128,512]{1,0:T(8,128)(2,1)S(1)}, u32[]{:S(2)}, u32[]{:S(2)}) collective-permute-start(bf16[128,512]{1,0:T(8,128)(2,1)S(1)} %get-tuple-element.112), channel_id=1, source_target_pairs={{0,1},{1,0},{2,3},{3,2},{4,5},{5,4},{6,7},{7,6},{8,9},{9,8},{10,11... | collective-permute-start | bytes 393224 | tf_op jit(solution)/shard_map/ppermute | solution.py:17
  367.8 17.5 %collective-permute-start.87 = (bf16[128,512]{1,0:T(8,128)(2,1)S(1)}, bf16[128,512]{1,0:T(8,128)(2,1)S(1)}, u32[]{:S(2)}, u32[]{:S(2)}) collective-permute-start(bf16[128,512]{1,0:T(8,128)(2,1)S(1)} %fusion.5), channel_id=1, source_target_pairs={{0,3},{1,2},{2,1},{3,0},{4,7},{5,6},{6,5},{7,4},{8,11},{9,10},{10,... | collective-permute-start | bytes 393224 | tf_op jit(solution)/shard_map/ppermute | solution.py:17
  385.4 17.7 %collective-permute-start.89 = (bf16[128,1024]{1,0:T(8,128)(2,1)S(1)}, bf16[128,1024]{1,0:T(8,128)(2,1)S(1)}, u32[]{:S(2)}, u32[]{:S(2)}) collective-permute-start(bf16[128,1024]{1,0:T(8,128)(2,1)S(1)} %pad_maximum_fusion.5.refs_0_), channel_id=1, source_target_pairs={{0,8},{8,0},{16,24},{24,16},{1,9},{9,1},{17,25},{25,17},{2,10},{10... | collective-permute-start | bytes 786440 | tf_op jit(solution)/shard_map/ppermute | solution.py:17
  385.5 20.4 %collective-permute-start.78 = (bf16[128,1024]{1,0:T(8,128)(2,1)S(1)}, bf16[128,1024]{1,0:T(8,128)(2,1)S(1)}, u32[]{:S(2)}, u32[]{:S(2)}) collective-permute-start(bf16[128,1024]{1,0:T(8,128)(2,1)S(1)} %pad_maximum_fusion.4.refs_0_), channel_id=1, source_target_pairs={{0,8},{8,0},{16,24},{24,16},{1,9},{9,1},{17,25},{25,17},{2,10},{10... | collective-permute-start | bytes 786440 | tf_op jit(solution)/shard_map/ppermute | solution.py:17
  442.8 18.2 %collective-permute-start.102 = (bf16[128,1024]{1,0:T(8,128)(2,1)S(1)}, bf16[128,1024]{1,0:T(8,128)(2,1)S(1)}, u32[]{:S(2)}, u32[]{:S(2)}) collective-permute-start(bf16[128,1024]{1,0:T(8,128)(2,1)S(1)} %add_convert_fusion), channel_id=1, source_target_pairs={{0,3},{1,2},{2,1},{3,0},{4,7},{5,6},{6,5},{7,4},{8,11},{9,10},{10,... | collective-permute-start | bytes 786440 | tf_op jit(solution)/shard_map/ppermute | solution.py:17
  448.4 23.9 %collective-permute-start.95 = (bf16[128,1024]{1,0:T(8,128)(2,1)S(1)}, bf16[128,1024]{1,0:T(8,128)(2,1)S(1)}, u32[]{:S(2)}, u32[]{:S(2)}) collective-permute-start(bf16[128,1024]{1,0:T(8,128)(2,1)S(1)} %add_convert_fusion.1), channel_id=1, source_target_pairs={{0,3},{1,2},{2,1},{3,0},{4,7},{5,6},{6,5},{7,4},{8,11},{9,10},{10,... | collective-permute-start | bytes 786440 | tf_op jit(solution)/shard_map/ppermute | solution.py:17
  461.2 18.0 %collective-permute-start.104 = (bf16[128,1024]{1,0:T(8,128)(2,1)S(1)}, bf16[128,1024]{1,0:T(8,128)(2,1)S(1)}, u32[]{:S(2)}, u32[]{:S(2)}) collective-permute-start(bf16[128,1024]{1,0:T(8,128)(2,1)S(1)} %subtract_convert_fusion.refs_0_), channel_id=1, source_target_pairs={{0,3},{1,2},{2,1},{3,0},{4,7},{5,6},{6,5},{7,4},{8,11},{9,10},{10,... | collective-permute-start | bytes 786440 | tf_op jit(solution)/shard_map/ppermute | solution.py:17
  479.2 18.0 %collective-permute-start.105 = (bf16[128,1024]{1,0:T(8,128)(2,1)S(1)}, bf16[128,1024]{1,0:T(8,128)(2,1)S(1)}, u32[]{:S(2)}, u32[]{:S(2)}) collective-permute-start(bf16[128,1024]{1,0:T(8,128)(2,1)S(1)} %collective-permute-done.104.refs_3_), channel_id=1, source_target_pairs={{0,1},{1,0},{2,3},{3,2},{4,5},{5,4},{6,7},{7,6},{8,9},{9,8},{10,11... | collective-permute-start | bytes 786440 | tf_op jit(solution)/shard_map/ppermute | solution.py:17
  486.4 21.5 %collective-permute-start.98 = (bf16[128,1024]{1,0:T(8,128)(2,1)S(1)}, bf16[128,1024]{1,0:T(8,128)(2,1)S(1)}, u32[]{:S(2)}, u32[]{:S(2)}) collective-permute-start(bf16[128,1024]{1,0:T(8,128)(2,1)S(1)} %collective-permute-done.97.refs_3_), channel_id=1, source_target_pairs={{0,1},{1,0},{2,3},{3,2},{4,5},{5,4},{6,7},{7,6},{8,9},{9,8},{10,11... | collective-permute-start | bytes 786440 | tf_op jit(solution)/shard_map/ppermute | solution.py:17
  (91 other events, 925.1 us)
